TPU v7x, 32 devices: a whole 2x2x4 slice. The times are simulated.
32 devices in a mesh: dp: 4 (over x, core), context: 2 (over y), tensor: 4 (over z).
Axes of the slice: x: 2, y: 2, z: 4, core: 2. Of those that a mesh axis runs over, the one named last changes fastest.
Arguments:
- layer_input: bfloat16 [4, 4096, 2048], P('dp', 'context'), may hold values from -6 to 6
- cotangent: bfloat16 [4, 4096, 2048], P('dp', 'context'), may hold values from -6 to 6
- w_qkv: bfloat16 [2048, 1536], P(('dp', 'context'), 'tensor'), may hold values from -0.125 to 0.125
- w_out: bfloat16 [1024, 2048], P('tensor', ('dp', 'context')), may hold values from -1.5 to 1.5
- attn_gain: bfloat16 [2048], P(('dp', 'context')), may hold values from 0.5 to 1.5
- qk_gain: float32 [2, 64], replicated, may hold values from 0.1 to 1.9
- w_gate: bfloat16 [2048, 5120], P(('dp', 'context'), 'tensor'), may hold values from -0.125 to 0.125
- w_up: bfloat16 [2048, 5120], P(('dp', 'context'), 'tensor'), may hold values from -0.125 to 0.125
- w_down: bfloat16 [5120, 2048], P('tensor', ('dp', 'context')), may hold values from -0.078125 to 0.078125
- ffn_gain: bfloat16 [2048], P(('dp', 'context')), may hold values from 0.5 to 1.5
- seg_ids: int32 [4, 4096], P('dp'), may hold values from 0 to 8, as said below
- pos_ids: int32 [4, 4096], P('dp'), may hold values from 0 to 2431, as said below
Outputs:
- layer_output: bfloat16 [4, 4096, 2048], P('dp', 'context')
- grad_input: bfloat16 [4, 4096, 2048], P('dp', 'context')
- grad_qkv: float32 [2048, 1536], P(('dp', 'context'), 'tensor')
- grad_out_proj: float32 [1024, 2048], P('tensor', ('dp', 'context'))
- grad_attn_gain: float32 [2048], P(('dp', 'context'))
- grad_qk_gain: float32 [2, 64], replicated
- grad_gate: float32 [2048, 5120], P(('dp', 'context'), 'tensor')
- grad_up: float32 [2048, 5120], P(('dp', 'context'), 'tensor')
- grad_down: float32 [5120, 2048], P('tensor', ('dp', 'context'))
- grad_ffn_gain: float32 [2048], P(('dp', 'context'))
Inputs may be any that keep to these rules, and one draw needn't show every extreme that they name: `seg_ids`: within each group the first 2048 tokens have id 0; the rest form 8 runs of consecutive tokens with ids 1 to 8 rising along the tokens, each run 1 to 384 tokens long, one of exactly 384 in every group. `pos_ids`: prompt token t has position t; the tokens of a continuation have positions 2048, 2049, ... in order.
All inputs are finite; a program needn't handle non-finite values.
Results may differ from a plain program's by a relative error of at most 0.024.
Values may be sent and summed in bfloat16 or wider, within the bound.
A program may use at most 256 MiB of HBM per device.

v0:
```python
import math

import jax
import jax.numpy as jnp
from jax import lax
from jax.sharding import PartitionSpec as P

HEADS = 16
KV_HEADS = 4
HEAD_DIM = 64


epsilon = 1e-06
rope_base = 10000.0


def norm_rows(values, gains):
    return values * lax.rsqrt(jnp.mean(values * values, axis=-1, keepdims=True) + epsilon) * gains


def rope_tables(positions, head_width):
    half_width = head_width // 2
    inverse = jnp.exp(
        -math.log(rope_base) * jnp.arange(half_width, dtype=jnp.float32) * 2.0 / head_width
    )
    angles = positions.astype(jnp.float32)[..., None] * inverse
    cosine_tab = jnp.concatenate([jnp.cos(angles), jnp.cos(angles)], axis=-1)
    sine_table = jnp.concatenate([jnp.sin(angles), jnp.sin(angles)], axis=-1)
    return (cosine_tab, sine_table)


def rotate(values, cosine_tab, sine_table):
    half_width = values.shape[-1] // 2
    lower_half = values[..., :half_width]
    upper_half = values[..., half_width:]
    return values * cosine_tab + jnp.concatenate([-upper_half, lower_half], axis=-1) * sine_table


def visible(query_pos, query_seg, key_pos, key_seg):
    same_run = (key_seg[None, :] == 0) | (key_seg[None, :] == query_seg[:, None])
    return (key_pos[None, :] <= query_pos[:, None]) & same_run


def mixed_silu(gate_in, up_in):
    return jax.nn.silu(gate_in) * up_in


def tensor_total(partial_term):
    return lax.psum(partial_term.astype(jnp.bfloat16), "tensor").astype(jnp.float32)


def body(
    layer_input,
    cotangent,
    w_qkv,
    w_out,
    attn_gain,
    qk_gain,
    w_gate,
    w_up,
    w_down,
    ffn_gain,
    seg_ids,
    pos_ids,
):
    group_count, local_len, model_width = layer_input.shape
    group_len = seg_ids.shape[1]
    kv_local = KV_HEADS // lax.axis_size("tensor")
    head_ratio = HEADS // KV_HEADS
    row_count = group_count * local_len
    score_scale = HEAD_DIM ** (-0.5)
    block_rows = min(local_len, 128)
    block_count = local_len // block_rows
    first_row = lax.axis_index("context") * local_len
    my_seg = lax.dynamic_slice_in_dim(seg_ids, first_row, local_len, 1)
    my_pos = lax.dynamic_slice_in_dim(pos_ids, first_row, local_len, 1)
    qkv_all, out_all, attn_gain_all = (
        lax.all_gather(w_qkv, ("dp", "context"), axis=0, tiled=True),
        lax.all_gather(w_out, ("dp", "context"), axis=1, tiled=True),
        lax.all_gather(attn_gain, ("dp", "context"), axis=0, tiled=True),
    )
    inputs = layer_input.astype(jnp.float32).reshape(row_count, model_width)
    normed = norm_rows(inputs, attn_gain_all.astype(jnp.float32))
    normed_low = normed.astype(jnp.bfloat16)
    joint = jnp.dot(normed_low, qkv_all, preferred_element_type=jnp.float32)
    joint = joint.reshape(group_count, local_len, kv_local, head_ratio + 2, HEAD_DIM)
    cosine_tab, sine_table = rope_tables(my_pos, HEAD_DIM)

    def prepare(query_raw, key_raw, gains_qk):
        query_rot = rotate(
            norm_rows(query_raw, gains_qk[0]),
            cosine_tab[:, :, None, None, :],
            sine_table[:, :, None, None, :],
        )
        key_rot = rotate(
            norm_rows(key_raw, gains_qk[1]), cosine_tab[:, :, None, :], sine_table[:, :, None, :]
        )
        return (query_rot, key_rot)

    query_raw = joint[:, :, :, :head_ratio]
    key_raw = joint[:, :, :, head_ratio]
    query_rot, key_rot = prepare(query_raw, key_raw, qk_gain)
    queries = query_rot.astype(jnp.bfloat16)
    kv_mine = jnp.stack([key_rot, joint[:, :, :, head_ratio + 1]], axis=3).astype(jnp.bfloat16)
    kv_mine = kv_mine.reshape(group_count, local_len, kv_local * 2 * HEAD_DIM)
    kv_group = lax.all_gather(kv_mine, "context", axis=1, tiled=True).reshape(
        group_count, group_len, kv_local, 2, HEAD_DIM
    )

    def block_scores(query_block, keys, allowed):
        scores = jnp.einsum("qkrd,tkd->qkrt", query_block, keys, preferred_element_type=jnp.float32)
        return jnp.where(allowed[:, None, None, :], scores * score_scale, -1e30)

    member = 0
    keys = kv_group[member, :, :, 0]
    values = kv_group[member, :, :, 1]
    key_pos = pos_ids[member]
    key_seg = seg_ids[member]

    def forward_block(block_items):
        query_block, query_pos, query_seg = block_items
        scores = block_scores(query_block, keys, visible(query_pos, query_seg, key_pos, key_seg))
        row_max = jnp.max(scores, axis=-1, keepdims=True)
        exp_scores = jnp.exp(scores - row_max)
        totals = jnp.sum(exp_scores, axis=-1, keepdims=True)
        probs = (exp_scores / totals).astype(jnp.bfloat16)
        result = jnp.einsum("qkrt,tkd->qkrd", probs, values, preferred_element_type=jnp.float32)
        return (result, row_max[..., 0] + jnp.log(totals[..., 0]))

    result, log_total = lax.map(
        forward_block,
        (
            queries[member].reshape(block_count, block_rows, kv_local, head_ratio, HEAD_DIM),
            my_pos[member].reshape(block_count, block_rows),
            my_seg[member].reshape(block_count, block_rows),
        ),
    )
    attended_list = [result]
    log_total_list = [log_total]
    attended_low = (
        jnp.stack(attended_list)
        .astype(jnp.bfloat16)
        .reshape(row_count, kv_local * head_ratio * HEAD_DIM)
    )
    attn_part = jnp.dot(attended_low, out_all, preferred_element_type=jnp.float32)
    gate_all, up_all, down_all, ffn_gain_all = (
        lax.all_gather(w_gate, ("dp", "context"), axis=0, tiled=True),
        lax.all_gather(w_up, ("dp", "context"), axis=0, tiled=True),
        lax.all_gather(w_down, ("dp", "context"), axis=1, tiled=True),
        lax.all_gather(ffn_gain, ("dp", "context"), axis=0, tiled=True),
    )
    resid = inputs + tensor_total(attn_part)
    normed_ffn_low = norm_rows(resid, ffn_gain_all.astype(jnp.float32)).astype(jnp.bfloat16)
    gate = jnp.dot(normed_ffn_low, gate_all, preferred_element_type=jnp.float32)
    up = jnp.dot(normed_ffn_low, up_all, preferred_element_type=jnp.float32)
    act_low = mixed_silu(gate, up).astype(jnp.bfloat16)
    ffn_part = jnp.dot(act_low, down_all, preferred_element_type=jnp.float32)
    result_out = (resid + tensor_total(ffn_part)).astype(jnp.bfloat16)
    gate_all, up_all, down_all, ffn_gain_all = (
        lax.all_gather(w_gate, ("dp", "context"), axis=0, tiled=True),
        lax.all_gather(w_up, ("dp", "context"), axis=0, tiled=True),
        lax.all_gather(w_down, ("dp", "context"), axis=1, tiled=True),
        lax.all_gather(ffn_gain, ("dp", "context"), axis=0, tiled=True),
    )
    qkv_all, out_all, attn_gain_all = (
        lax.all_gather(w_qkv, ("dp", "context"), axis=0, tiled=True),
        lax.all_gather(w_out, ("dp", "context"), axis=1, tiled=True),
        lax.all_gather(attn_gain, ("dp", "context"), axis=0, tiled=True),
    )
    cot_low = cotangent.reshape(row_count, model_width)
    grad_down = jnp.dot(act_low.T, cot_low, preferred_element_type=jnp.float32)
    act_grad = jnp.dot(cot_low, down_all.T, preferred_element_type=jnp.float32)
    _, silu_pull = jax.vjp(mixed_silu, gate, up)
    gate_grad, up_grad = silu_pull(act_grad)
    gate_grad = gate_grad.astype(jnp.bfloat16)
    up_grad = up_grad.astype(jnp.bfloat16)
    grad_gate = jnp.dot(normed_ffn_low.T, gate_grad, preferred_element_type=jnp.float32)
    grad_up = jnp.dot(normed_ffn_low.T, up_grad, preferred_element_type=jnp.float32)
    ffn_in_part = jnp.dot(gate_grad, gate_all.T, preferred_element_type=jnp.float32) + jnp.dot(
        up_grad, up_all.T, preferred_element_type=jnp.float32
    )
    ffn_in_grad = tensor_total(ffn_in_part)
    _, norm_ffn_pull = jax.vjp(norm_rows, resid, ffn_gain_all.astype(jnp.float32))
    resid_norm_grad, grad_ffn_gain = norm_ffn_pull(ffn_in_grad)
    resid_grad = cot_low.astype(jnp.float32) + resid_norm_grad
    branch_grad = resid_grad.astype(jnp.bfloat16)
    grad_out_proj = jnp.dot(attended_low.T, branch_grad, preferred_element_type=jnp.float32)
    attended_grad = jnp.dot(branch_grad, out_all.T, preferred_element_type=jnp.float32).astype(
        jnp.bfloat16
    )
    attended_grad = attended_grad.reshape(group_count, local_len, kv_local, head_ratio, HEAD_DIM)
    member = 0
    keys = kv_group[member, :, :, 0]
    values = kv_group[member, :, :, 1]
    key_pos = pos_ids[member]
    key_seg = seg_ids[member]

    def backward_block(carried, block_items):
        query_block, query_pos, query_seg, log_total, grad_block = block_items
        scores = block_scores(query_block, keys, visible(query_pos, query_seg, key_pos, key_seg))
        probs = jnp.exp(scores - log_total[..., None])
        prob_grad = jnp.einsum(
            "qkrd,tkd->qkrt", grad_block, values, preferred_element_type=jnp.float32
        )
        inner = jnp.sum(probs * prob_grad, axis=-1, keepdims=True)
        score_grad = (probs * (prob_grad - inner) * score_scale).astype(jnp.bfloat16)
        query_grad = jnp.einsum(
            "qkrt,tkd->qkrd", score_grad, keys, preferred_element_type=jnp.float32
        )
        key_total = carried[0] + jnp.einsum(
            "qkrt,qkrd->tkd", score_grad, query_block, preferred_element_type=jnp.float32
        )
        value_total = carried[1] + jnp.einsum(
            "qkrt,qkrd->tkd",
            probs.astype(jnp.bfloat16),
            grad_block,
            preferred_element_type=jnp.float32,
        )
        return ((key_total, value_total), query_grad)

    empty = jnp.zeros((group_len, kv_local, HEAD_DIM), jnp.float32)
    (key_total, value_total), query_grad = lax.scan(
        backward_block,
        (empty, empty),
        (
            queries[member].reshape(block_count, block_rows, kv_local, head_ratio, HEAD_DIM),
            my_pos[member].reshape(block_count, block_rows),
            my_seg[member].reshape(block_count, block_rows),
            log_total_list[member],
            attended_grad[member].reshape(block_count, block_rows, kv_local, head_ratio, HEAD_DIM),
        ),
    )
    query_grads = [query_grad.reshape(local_len, kv_local, head_ratio, HEAD_DIM)]
    key_grads = [key_total]
    value_grads = [value_total]
    kv_grad_group = jnp.stack([jnp.stack(key_grads), jnp.stack(value_grads)], axis=3)
    kv_grad_group = kv_grad_group.reshape(group_count, group_len, kv_local * 2 * HEAD_DIM)
    kv_grad = lax.psum_scatter(
        kv_grad_group.astype(jnp.bfloat16), "context", scatter_dimension=1, tiled=True
    ).astype(jnp.float32)
    kv_grad = kv_grad.reshape(group_count, local_len, kv_local, 2, HEAD_DIM)
    _, prepare_pull = jax.vjp(prepare, query_raw, key_raw, qk_gain)
    query_raw_grad, key_raw_grad, qk_gain_part = prepare_pull(
        (jnp.stack(query_grads), kv_grad[:, :, :, 0])
    )
    joint_grad = jnp.concatenate(
        [query_raw_grad, key_raw_grad[:, :, :, None], kv_grad[:, :, :, 1][:, :, :, None]], axis=3
    )
    joint_grad = joint_grad.astype(jnp.bfloat16).reshape(
        row_count, kv_local * (head_ratio + 2) * HEAD_DIM
    )
    grad_qkv = jnp.dot(normed_low.T, joint_grad, preferred_element_type=jnp.float32)
    in_part = jnp.dot(joint_grad, qkv_all.T, preferred_element_type=jnp.float32)
    in_grad = tensor_total(in_part)
    _, norm_in_pull = jax.vjp(norm_rows, inputs, attn_gain_all.astype(jnp.float32))
    input_norm_grad, grad_attn_gain = norm_in_pull(in_grad)
    grad_input = (resid_grad + input_norm_grad).astype(jnp.bfloat16)
    grad_input = grad_input.reshape(group_count, local_len, model_width)
    grad_qk_gain = lax.psum(qk_gain_part, ("dp", "context", "tensor"))
    grads = (grad_qkv, grad_out_proj, grad_attn_gain, grad_gate, grad_up, grad_down, grad_ffn_gain)
    shard_qkv, shard_out, shard_attn_gain, shard_gate, shard_up, shard_down, shard_ffn_gain = (
        lax.psum_scatter(
            grads[0].astype(jnp.bfloat16), ("dp", "context"), scatter_dimension=0, tiled=True
        ).astype(jnp.float32),
        lax.psum_scatter(
            grads[1].astype(jnp.bfloat16), ("dp", "context"), scatter_dimension=1, tiled=True
        ).astype(jnp.float32),
        lax.psum_scatter(
            grads[2].astype(jnp.bfloat16), ("dp", "context"), scatter_dimension=0, tiled=True
        ).astype(jnp.float32),
        lax.psum_scatter(
            grads[3].astype(jnp.bfloat16), ("dp", "context"), scatter_dimension=0, tiled=True
        ).astype(jnp.float32),
        lax.psum_scatter(
            grads[4].astype(jnp.bfloat16), ("dp", "context"), scatter_dimension=0, tiled=True
        ).astype(jnp.float32),
        lax.psum_scatter(
            grads[5].astype(jnp.bfloat16), ("dp", "context"), scatter_dimension=1, tiled=True
        ).astype(jnp.float32),
        lax.psum_scatter(
            grads[6].astype(jnp.bfloat16), ("dp", "context"), scatter_dimension=0, tiled=True
        ).astype(jnp.float32),
    )
    return (
        result_out.reshape(group_count, local_len, model_width),
        grad_input,
        shard_qkv,
        shard_out,
        shard_attn_gain,
        grad_qk_gain,
        shard_gate,
        shard_up,
        shard_down,
        shard_ffn_gain,
    )


def solution(mesh):
    return jax.shard_map(
        body,
        mesh=mesh,
        in_specs=(
            P("dp", "context", None),
            P("dp", "context", None),
            P(("dp", "context"), "tensor"),
            P("tensor", ("dp", "context")),
            P(("dp", "context")),
            P(),
            P(("dp", "context"), "tensor"),
            P(("dp", "context"), "tensor"),
            P("tensor", ("dp", "context")),
            P(("dp", "context")),
            P("dp", None),
            P("dp", None),
        ),
        out_specs=(
            P("dp", "context", None),
            P("dp", "context", None),
            P(("dp", "context"), "tensor"),
            P("tensor", ("dp", "context")),
            P(("dp", "context")),
            P(),
            P(("dp", "context"), "tensor"),
            P(("dp", "context"), "tensor"),
            P("tensor", ("dp", "context")),
            P(("dp", "context")),
        ),
        check_vma=False,
    )
```

profile of v0, /device:TPU:0, one launch (start us, length us, event | category | flops | bytes accessed | tf_op | source)
XLA Modules:
  0.0 2420.3 jit_solution(337184587082190026)
XLA Ops:
  8.6 14.2 all-gather
  54.2 16.8 all-gather.11.cloned.1.call-done
  72.2 110.1 %while.27 = (s32[]{:T(128)}, bf16[16,128,1,4,64]{1,4,3,2,0:T(8,128)(2,1)}, f32[16,128,1,4]{1,3,2,0:T(4,128)}, s32[1,4096]{1,0:T(1,128)S(1)}, s32[16,128]{1,0:T(8...) while((s32[]{:T(128)}, ...), condition=%wide.region_6.7_spmd, body=%wide.region_3.6_spmd.sunk | while | flops 555748864 | bytes 27536516 | solution.py:130
  195.1 13.0 all-gather.1
  208.1 276.0 %all-reduce.14.cloned.1.call-done = bf16[2048,2048]{1,0:T(8,128)(2,1)} async-done(((bf16[2048,2048]{1,0:T(8,128)(2,1)}), bf16[2048,2048]{1,0:T(8,128)(2,1)}) %all-reduce.14.cloned.1.call-update) | async-done | bytes 8388624 | tf_op jit(solution)/shard_map/psum | solution.py:49
  492.6 11.6 multiply_convert_fusion
  504.2 21.8 all-gather.17.cloned.1.call-done
  526.0 16.5 fusion.132
  542.5 26.4 %all-gather.15.cloned.1.call-done = bf16[2048,1280]{1,0:T(8,128)(2,1)} async-done(((bf16[256,1280]{1,0:T(8,128)(2,1)}), bf16[2048,1280]{1,0:T(8,128)(2,1)}) %all-gather.15.cloned.1.call-update) | async-done | bytes 5242896 | tf_op jit(solution)/shard_map/all_gather | solution.py:147
  568.9 16.6 fusion.131
  585.5 27.3 %all-gather.19.cloned.1.call-done = bf16[1280,2048]{1,0:T(8,128)(2,1)} async-done(((bf16[1280,256]{1,0:T(8,128)(2,1)}), bf16[1280,2048]{1,0:T(8,128)(2,1)}) %all-gather.19.cloned.1.call-update) | async-done | bytes 5242896 | tf_op jit(solution)/shard_map/all_gather | solution.py:149
  612.8 23.4 multiply_convert_fusion.1
  636.2 18.0 fusion.133
  654.2 19.0 add_convert_fusion
  673.4 290.9 %all-reduce.16.cloned.1.call-done = bf16[2048,2048]{1,0:T(8,128)(2,1)} async-done(((bf16[2048,2048]{1,0:T(8,128)(2,1)}), bf16[2048,2048]{1,0:T(8,128)(2,1)}) %all-reduce.16.cloned.1.call-update) | async-done | bytes 8388624 | tf_op jit(solution)/shard_map/psum | solution.py:49
  964.3 12.6 fusion.59
  976.9 14.4 fusion.61
  1008.7 505.4 %while.28 = (s32[]{:T(128)}, f32[4096,1,64]{0,2,1:T(8,128)S(1)}, f32[4096,1,64]{0,2,1:T(8,128)}, f32[16,128,1,4,64]{1,0,4,3,2:T(8,128)}, bf16[16,128,1,4,64]{1,4...) while((s32[]{:T(128)}, f32[4096,1,64]{0,2,1:T(8,128)S(1)}, ...), condition=%wide.region_14.15_spmd.clone, body=%wide.region_12.14_spmd.clone.sunk | while | flops 1366298112 | bytes 104010976 | solution.py:222
  1516.6 16.8 fusion.78
  1533.5 16.8 convolution_convert_fusion.3
  1550.4 17.8 convolution_convert_fusion.4
  1575.9 9.3 fusion.94
  1593.0 9.8 fusion.88
  1603.1 17.1 convolution_convert_fusion.1
  1631.2 25.0 %reduce-scatter.15.cloned.1.call-done = bf16[256,1280]{1,0:T(8,128)(2,1)} async-done(((bf16[2048,1280]{1,0:T(8,128)(2,1)}), bf16[256,1280]{1,0:T(8,128)(2,1)}) %reduce-scatter.15.cloned.1.call-update) | async-done | bytes 655376 | tf_op jit(solution)/shard_map/reduce_scatter | solution.py:274
  1658.4 58.0 %reduce-scatter.13.cloned.1.call-done = bf16[256,1280]{1,0:T(8,128)(2,1)} async-done(((bf16[2048,1280]{1,0:T(8,128)(2,1)}), bf16[256,1280]{1,0:T(8,128)(2,1)}) %reduce-scatter.13.cloned.1.call-update) | async-done | bytes 655376 | tf_op jit(solution)/shard_map/reduce_scatter | solution.py:271
  1718.7 37.0 %reduce-scatter.11.cloned.1.call-done = bf16[256,256]{1,0:T(8,128)(2,1)} async-done(((bf16[256,2048]{1,0:T(8,128)(2,1)}), bf16[256,256]{1,0:T(8,128)(2,1)}) %reduce-scatter.11.cloned.1.call-update) | async-done | bytes 131088 | tf_op jit(solution)/shard_map/reduce_scatter | solution.py:265
  1757.3 39.3 %psum.39 = f32[2,64]{1,0:T(2,128)} all-reduce(f32[2,64]{1,0:T(2,128)S(1)} %pad_add_fusion.1), channel_id=1, replica_groups=mesh['dp'=4,'context'=2,'tensor'=4] {'dp','context','tensor'}, use_global_device_ids=true, to_apply=%region_26.27 | all-reduce | flops 128 | bytes 1024 | tf_op jit(solution)/shard_map/psum | solution.py:259
  1799.6 564.3 %all-reduce.18.cloned.1.call-done = (bf16[2048,2048]{1,0:T(8,128)(2,1)}, bf16[2048,2048]{1,0:T(8,128)(2,1)}) async-done(((bf16[2048,2048]{1,0:T(8,128)(2,1)}, bf16[2048,2048]{1,0:T(8,128)(2,1)}), (bf16[2048,2048]{1,0:T(8,128)(2,1)}, bf16[2048,2048]{1,0:T(8,128)(2,1)})) %all-reduce.18.cloned.1.call-update) | async-done | bytes 16777232 | tf_op jit(solution)/shard_map/psum | solution.py:49
  2363.9 10.1 fusion.60
  2374.0 14.3 all-reduce.8
  2389.6 24.0 fusion.69
  (519 shorter events, 725.7 us)
Async XLA Ops:
  7.2 21.5 copy-start.22
  7.2 31.1 %all-gather.9.cloned.1.call-start = ((), (), s32[]{:S(2)}) async-start(), calls=%async_computation.6 | async-start | bytes 1769472 | tf_op jit(solution)/shard_map/all_gather | solution.py:78
  7.9 63.1 %all-gather.11.cloned.1.call-start = ((), (), s32[]{:S(2)}) async-start(), calls=%async_computation.7 | async-start | bytes 1572864 | tf_op jit(solution)/shard_map/all_gather | solution.py:106
  22.8 24.7 %copy-start.31 = (f32[8,1,256]{2,1,0:T(1,128)}, f32[8,1,256]{2,1,0:T(1,128)S(1)}, u32[]{:S(2)}) copy-start(f32[8,1,256]{2,1,0:T(1,128)S(1)} %convert_element_type.227) | copy-start | bytes 24580
  23.6 24.8 %copy-start.44 = (f32[64]{0:T(128)}, f32[64]{0:T(128)S(1)}, u32[]{:S(2)}) copy-start(f32[64]{0:T(128)S(1)} %get-tuple-element.335) | copy-start | bytes 772
  23.6 29.3 %copy-start.42 = (f32[64]{0:T(128)}, f32[64]{0:T(128)S(1)}, u32[]{:S(2)}) copy-start(f32[64]{0:T(128)S(1)} %get-tuple-element.336) | copy-start | bytes 772
  28.7 18.8 copy-start.33
  31.0 19.8 copy-start.17
  40.9 11.1 copy-start.11
  49.5 136.2 %all-gather.13.cloned.1.call-start = ((), (), s32[]{:S(2)}) async-start(), calls=%async_computation.8 | async-start | bytes 1179648 | tf_op jit(solution)/shard_map/all_gather | solution.py:79
  50.2 433.9 %all-reduce.14.cloned.1.call-start = ((), (), s32[]{:S(2)}) async-start(), calls=%async_computation.9 | async-start | bytes 16777216 | tf_op jit(solution)/shard_map/psum | solution.py:49
  183.3 9.8 copy-start.39
  183.3 9.8 copy-start.40
  193.2 332.8 %all-gather.17.cloned.1.call-start = ((), (), s32[]{:S(2)}) async-start(), calls=%async_computation.11 | async-start | bytes 5898240 | tf_op jit(solution)/shard_map/all_gather | solution.py:148
  193.8 375.1 %all-gather.15.cloned.1.call-start = ((), (), s32[]{:S(2)}) async-start(), calls=%async_computation.10 | async-start | bytes 5898240 | tf_op jit(solution)/shard_map/all_gather | solution.py:147
  194.3 418.5 %all-gather.19.cloned.1.call-start = ((), (), s32[]{:S(2)}) async-start(), calls=%async_computation.12 | async-start | bytes 5898240 | tf_op jit(solution)/shard_map/all_gather | solution.py:149
  195.1 769.2 %all-reduce.16.cloned.1.call-start = ((), (), s32[]{:S(2)}) async-start(), calls=%async_computation.13 | async-start | bytes 16777216 | tf_op jit(solution)/shard_map/psum | solution.py:49
  673.3 915.6 %reduce-scatter.7.cloned.1.call-start = ((), (), s32[]{:S(2)}) async-start(), calls=%async_computation.14 | async-start | bytes 1572864 | tf_op jit(solution)/shard_map/reduce_scatter | solution.py:238
  976.9 20.1 copy-start.20
  997.0 11.7 copy-start.3
  997.0 11.7 copy-start.7
  997.0 11.7 copy-start.12
  997.0 11.7 copy-start.23
  1516.5 112.4 %reduce-scatter.17.cloned.1.call-start = ((), (), s32[]{:S(2)}) async-start(), calls=%async_computation.19 | async-start | bytes 5898240 | tf_op jit(solution)/shard_map/reduce_scatter | solution.py:277
  1533.4 122.8 %reduce-scatter.15.cloned.1.call-start = ((), (), s32[]{:S(2)}) async-start(), calls=%async_computation.18 | async-start | bytes 5898240 | tf_op jit(solution)/shard_map/reduce_scatter | solution.py:274
  1550.3 166.1 %reduce-scatter.13.cloned.1.call-start = ((), (), s32[]{:S(2)}) async-start(), calls=%async_computation.17 | async-start | bytes 5898240 | tf_op jit(solution)/shard_map/reduce_scatter | solution.py:271
  1568.2 187.5 %reduce-scatter.11.cloned.1.call-start = ((), (), s32[]{:S(2)}) async-start(), calls=%async_computation.16 | async-start | bytes 1179648 | tf_op jit(solution)/shard_map/reduce_scatter | solution.py:265
  1585.3 212.6 %reduce-scatter.9.cloned.1.call-start = ((), (), s32[]{:S(2)}) async-start(), calls=%async_computation.15 | async-start | bytes 1769472 | tf_op jit(solution)/shard_map/reduce_scatter | solution.py:262
  1602.8 17.4 copy-start.24
  1602.8 761.0 %all-reduce.18.cloned.1.call-start = ((), (), s32[]{:S(2)}) async-start(), calls=%async_computation.20 | async-start | bytes 33554432 | tf_op jit(solution)/shard_map/psum | solution.py:49
  2363.9 10.1 copy-start.36
  2363.9 10.1 copy-start.41
  (46 other events, 236.4 us)
Sparse Core Ops, SparseCore 0:
  9.9 28.3 all-gather.8
  49.6 21.3 all-gather.10
  72.9 23.5 all-gather.12
  193.2 290.8 all-reduce.13
  485.8 40.1 all-gather.16
  527.7 41.1 all-gather.14
  570.7 42.0 all-gather.18
  673.4 290.8 all-reduce.15
  1516.6 19.3 reduce-scatter.6
  1539.6 56.5 reduce-scatter.16
  1599.6 56.5 reduce-scatter.14
  1659.8 56.5 reduce-scatter.12
  1719.6 36.0 reduce-scatter.10
  1758.8 39.0 reduce-scatter.8
  1800.9 562.8 all-reduce.17
where the time goes:
time: 2430 us; the launch traced here: 2420 us
  waiting for transfers between devices  1360 us (56%)
  matrix products  547 us (23%)
  other arithmetic  295 us (12%)
  local copies, waits for them, and re-layouts  124 us (5%)
  blocking collectives  80.7 us (3%)
    psum x3, waiting for transfers between devices, tensor_total(): lax.psum(partial_term.astype(jnp.bfloat16), 'tensor').astype(jnp.float32)  1130 us
    another operation x19, other arithmetic  129 us
    dot_general x32, matrix products, block_scores(): jnp.einsum('qkrd,tkd->qkrt', query_block, keys, preferred_element_type=jn...  128 us
    dot_general x16, matrix products, backward_block(): jnp.einsum('qkrt,qkrd->tkd', probs.astype(jnp.bfloat16), grad_block, pref...  87.3 us
    dynamic_update_slice x16, local copies, waits for them, and re-layouts, body(): lax.map(forward_block, (queries[member].reshape(block_count, block_rows,...  72.3 us
    reduce_scatter x1, waiting for transfers between devices, body(): lax.psum_scatter(grads[3].astype(jnp.bfloat16), ('dp', 'context'), scatte...  58 us
  transfers between devices with their start and end apart: 15, of which 12 were waited for; matrix products, arithmetic and copies ran while one was open for 12% of the time, Pallas kernels for 0%

commit v1 on v0

v1 whole, which is shorter than its diff:
```python
import functools, math
import jax, jax.numpy as jnp
from jax import lax
from jax.experimental import pallas as pl
from jax.experimental.pallas import tpu as pltpu
from jax.sharding import PartitionSpec as P

HEAD_DIM = 64
LOG2E = math.log2(math.e)
LN2 = math.log(2.0)
f32 = jnp.float32
bf16 = jnp.bfloat16
epsilon = 1e-6


def dot_nt(a, b):
    return lax.dot_general(a, b, (((1,), (1,)), ((), ())), preferred_element_type=f32)

def dot_nn(a, b):
    return lax.dot_general(a, b, (((1,), (0,)), ((), ())), preferred_element_type=f32)

def dot_tn(a, b):
    return lax.dot_general(a, b, (((0,), (0,)), ((), ())), preferred_element_type=f32)


def head_norm(x):
    return x * lax.rsqrt(jnp.mean(x * x, axis=0, keepdims=True) + epsilon)


def prep_kernel(heads, joint_ref, cos_ref, sin_ref, gain_ref, q_ref, kv_ref):
    half = HEAD_DIM // 2
    cos, sin = cos_ref[...], sin_ref[...]

    def one(row, gain, scale):
        x = head_norm(joint_ref[row : row + HEAD_DIM, :]) * gain
        lo, hi = x[:half], x[half:]
        return jnp.concatenate([lo * cos - hi * sin, hi * cos + lo * sin], axis=0) * scale

    for h in range(heads):
        row = h * HEAD_DIM
        q_ref[row : row + HEAD_DIM, :] = one(row, gain_ref[:, 0:1], LOG2E * HEAD_DIM**-0.5).astype(bf16)
    row = heads * HEAD_DIM
    key = one(row, gain_ref[:, 1:2], 1.0)
    both = jnp.concatenate([key, joint_ref[row + HEAD_DIM : row + 2 * HEAD_DIM, :]], axis=0)
    kv_ref[...] = both.T.astype(bf16)


def prep(joint, cos, sin, gains, heads, block):
    rows, count = joint.shape
    block = min(block, count)
    return pl.pallas_call(
        functools.partial(prep_kernel, heads),
        out_shape=(
            jax.ShapeDtypeStruct((heads * HEAD_DIM, count), bf16),
            jax.ShapeDtypeStruct((count, 2 * HEAD_DIM), bf16),
        ),
        grid=(count // block,),
        in_specs=[
            pl.BlockSpec((rows, block), lambda i: (0, i)),
            pl.BlockSpec((HEAD_DIM // 2, block), lambda i: (0, i)),
            pl.BlockSpec((HEAD_DIM // 2, block), lambda i: (0, i)),
            pl.BlockSpec((HEAD_DIM, 2), lambda i: (0, 0)),
        ],
        out_specs=(
            pl.BlockSpec((heads * HEAD_DIM, block), lambda i: (0, i)),
            pl.BlockSpec((block, 2 * HEAD_DIM), lambda i: (i, 0)),
        ),
        cost_estimate=pl.CostEstimate(flops=rows * count * 20, bytes_accessed=rows * count * 6, transcendentals=0),
        name="prep",
    )(joint, cos, sin, gains)


def unprep_kernel(heads, joint_ref, cos_ref, sin_ref, gain_ref, dq_ref, dkv_ref, out_ref, dgain_ref):
    half = HEAD_DIM // 2
    cos, sin = cos_ref[...], sin_ref[...]

    @pl.when(pl.program_id(0) == 0)
    def _():
        dgain_ref[...] = jnp.zeros_like(dgain_ref)

    def one(row, grad, gain):
        x = joint_ref[row : row + HEAD_DIM, :]
        r = lax.rsqrt(jnp.mean(x * x, axis=0, keepdims=True) + epsilon)
        n = x * r
        lo, hi = grad[:half], grad[half:]
        back = jnp.concatenate([lo * cos + hi * sin, hi * cos - lo * sin], axis=0)
        scaled = back * gain
        result = r * (scaled - n * jnp.mean(scaled * n, axis=0, keepdims=True))
        out_ref[row : row + HEAD_DIM, :] = result.astype(bf16)
        return jnp.sum(back * n, axis=1, keepdims=True)

    total = None
    for h in range(heads):
        row = h * HEAD_DIM
        part = one(row, dq_ref[row : row + HEAD_DIM, :], gain_ref[:, 0:1])
        total = part if total is None else total + part
    row = heads * HEAD_DIM
    dkv = dkv_ref[...].astype(f32).T
    part = one(row, dkv[:HEAD_DIM], gain_ref[:, 1:2])
    out_ref[row + HEAD_DIM : row + 2 * HEAD_DIM, :] = dkv[HEAD_DIM:].astype(bf16)
    dgain_ref[...] += jnp.concatenate([total, part], axis=1)


def unprep(joint, cos, sin, gains, dq, dkv, heads, block):
    rows, count = joint.shape
    block = min(block, count)
    return pl.pallas_call(
        functools.partial(unprep_kernel, heads),
        out_shape=(
            jax.ShapeDtypeStruct((rows, count), bf16),
            jax.ShapeDtypeStruct((HEAD_DIM, 2), f32),
        ),
        grid=(count // block,),
        in_specs=[
            pl.BlockSpec((rows, block), lambda i: (0, i)),
            pl.BlockSpec((HEAD_DIM // 2, block), lambda i: (0, i)),
            pl.BlockSpec((HEAD_DIM // 2, block), lambda i: (0, i)),
            pl.BlockSpec((HEAD_DIM, 2), lambda i: (0, 0)),
            pl.BlockSpec((heads * HEAD_DIM, block), lambda i: (0, i)),
            pl.BlockSpec((block, 2 * HEAD_DIM), lambda i: (i, 0)),
        ],
        out_specs=(
            pl.BlockSpec((rows, block), lambda i: (0, i)),
            pl.BlockSpec((HEAD_DIM, 2), lambda i: (0, 0)),
        ),
        cost_estimate=pl.CostEstimate(flops=rows * count * 30, bytes_accessed=rows * count * 10, transcendentals=0),
        name="unprep",
    )(joint, cos, sin, gains, dq, dkv)


def block_state(seg_ref, start_ref, q_index, k_index, bq, bk):
    q_first = start_ref[0] + q_index * bq
    k_first = k_index * bk
    k_last_seg = seg_ref[k_first + bk - 1]
    needed = (k_first <= q_first + bq - 1) & ((k_last_seg == 0) | (k_last_seg >= seg_ref[q_first]) | (seg_ref[k_first] == 0))
    whole = (k_last_seg == 0) & (k_first + bk - 1 <= q_first)
    return needed, whole


def fwd_kernel(heads, bq, bk, start_ref, seg_ref, q_ref, kv_ref, qpos_ref, qseg_ref, kpos_ref, kseg_ref, o_ref, l_ref, vaug, qs, acc):
    qi = pl.program_id(0)
    nk = kv_ref.shape[0] // bk
    lane = lax.broadcasted_iota(jnp.int32, kv_ref.shape, 1)

    @pl.when(qi == 0)
    def _():
        vaug[...] = jnp.where(lane >= HEAD_DIM, kv_ref[...].astype(f32), jnp.where(lane == 0, 1.0, 0.0)).astype(bf16)

    zeros = jnp.zeros((HEAD_DIM, bq), f32)
    for h in range(heads):
        full = jnp.concatenate([q_ref[h * HEAD_DIM : (h + 1) * HEAD_DIM, :].astype(f32), zeros], axis=0)
        qs[h * bq : (h + 1) * bq, :] = full.T.astype(bf16)
    acc[...] = jnp.zeros_like(acc)

    def step(k_index, masked):
        rows = pl.ds(pl.multiple_of(k_index * bk, bk), bk)
        kb, vb = kv_ref[rows, :], vaug[rows, :]
        if masked:
            kseg = kseg_ref[k_index]
            mask = (kpos_ref[k_index] <= qpos_ref[...]) & ((kseg == 0) | (kseg == qseg_ref[...]))
        for h in range(heads):
            s = dot_nt(qs[h * bq : (h + 1) * bq, :], kb)
            p = jnp.exp2(s)
            if masked:
                p = jnp.where(mask, p, 0.0)
            acc[h * bq : (h + 1) * bq, :] += dot_nn(p.astype(bf16), vb)

    @pl.loop(0, nk)
    def _(k_index):
        needed, whole = block_state(seg_ref, start_ref, qi, k_index, bq, bk)

        @pl.when(needed & whole)
        def _():
            step(k_index, False)

        @pl.when(needed & jnp.logical_not(whole))
        def _():
            step(k_index, True)

    for h in range(heads):
        out = acc[h * bq : (h + 1) * bq, :].T
        total = out[0:1, :]
        o_ref[h * HEAD_DIM : (h + 1) * HEAD_DIM, :] = (out[HEAD_DIM:, :] / total).astype(bf16)
        l_ref[h : h + 1, :] = jnp.log2(total)


def attention(start, seg, q, kv, qpos, qseg, kpos, kseg, bq, bk):
    heads = q.shape[0] // HEAD_DIM
    count, total = q.shape[1], kv.shape[0]
    bq, bk = min(bq, count), min(bk, total)
    whole = lambda *shape: pl.BlockSpec(shape, lambda i, *_: (0,) * len(shape))
    return pl.pallas_call(
        functools.partial(fwd_kernel, heads, bq, bk),
        out_shape=(
            jax.ShapeDtypeStruct(q.shape, bf16),
            jax.ShapeDtypeStruct((heads, count), f32),
        ),
        grid_spec=pltpu.PrefetchScalarGridSpec(
            num_scalar_prefetch=2,
            grid=(count // bq,),
            in_specs=[
                pl.BlockSpec((q.shape[0], bq), lambda i, *_: (0, i)),
                whole(*kv.shape),
                pl.BlockSpec((bq, 1), lambda i, *_: (i, 0)),
                pl.BlockSpec((bq, 1), lambda i, *_: (i, 0)),
                whole(total // bk, 1, bk),
                whole(total // bk, 1, bk),
            ],
            out_specs=(
                pl.BlockSpec((q.shape[0], bq), lambda i, *_: (0, i)),
                pl.BlockSpec((heads, bq), lambda i, *_: (0, i)),
            ),
            scratch_shapes=[
                pltpu.VMEM(kv.shape, bf16),
                pltpu.VMEM((heads * bq, 2 * HEAD_DIM), bf16),
                pltpu.VMEM((heads * bq, 2 * HEAD_DIM), f32),
            ],
        ),
        cost_estimate=pl.CostEstimate(flops=heads * count * total * 256, bytes_accessed=4 << 20, transcendentals=heads * count * total // 2),
        name="attend",
    )(start, seg, q, kv, qpos.reshape(-1, 1), qseg.reshape(-1, 1), kpos.reshape(-1, 1, bk), kseg.reshape(-1, 1, bk))


def split3(x):
    a = x.astype(bf16).astype(f32)
    b = (x - a).astype(bf16).astype(f32)
    return a, b, x - a - b


def bwd_kernel(heads, bq, bk, start_ref, seg_ref, q_ref, kv_ref, o_ref, do_ref, l_ref, qpos_ref, qseg_ref, kpos_ref, kseg_ref,
               dq_ref, dkv_ref, kaug, vaug, qst, dst, qs, ds, dacc, dkv):
    qi = pl.program_id(0)
    nk = kv_ref.shape[0] // bk
    D = HEAD_DIM

    @pl.when(qi == 0)
    def _():
        lane = lax.broadcasted_iota(jnp.int32, kv_ref.shape, 1)
        kv = kv_ref[...].astype(f32)
        kaug[...] = jnp.where(lane < D, kv, jnp.where(lane < D + 3, -1.0, 0.0)).astype(bf16)
        vaug[...] = jnp.where(lane >= D, kv, jnp.where(lane < 3, -1.0, 0.0)).astype(bf16)
        dkv[...] = jnp.zeros_like(dkv)

    row = lax.broadcasted_iota(jnp.int32, (D, bq), 0)

    def extra(x):
        a, b, c = split3(x)
        return jnp.where(row == 0, a, jnp.where(row == 1, b, jnp.where(row == 2, c, 0.0)))

    zeros = jnp.zeros((D, bq), f32)
    for h in range(heads):
        part = slice(h * D, (h + 1) * D)
        wide = slice(h * 2 * D, (h + 1) * 2 * D)
        q, do, o = q_ref[part, :].astype(f32), do_ref[part, :].astype(f32), o_ref[part, :].astype(f32)
        delta = jnp.sum(do * o, axis=0, keepdims=True)
        qst[wide, :] = jnp.concatenate([q, extra(l_ref[h : h + 1, :])], axis=0).astype(bf16)
        dst[wide, :] = jnp.concatenate([extra(delta), do], axis=0).astype(bf16)
        qs[h * bq : (h + 1) * bq, :] = jnp.concatenate([q, zeros], axis=0).T.astype(bf16)
        ds[h * bq : (h + 1) * bq, :] = jnp.concatenate([zeros, do], axis=0).T.astype(bf16)
    dacc[...] = jnp.zeros_like(dacc)

    def step(k_index, masked):
        rows = pl.ds(pl.multiple_of(k_index * bk, bk), bk)
        kb, vb, kvb = kaug[rows, :], vaug[rows, :], kv_ref[rows, :]
        if masked:
            kseg = kseg_ref[rows, :]
            mask = (kpos_ref[rows, :] <= qpos_ref[...]) & ((kseg == 0) | (kseg == qseg_ref[...]))
        add = None
        for h in range(heads):
            wide = slice(h * 2 * D, (h + 1) * 2 * D)
            tall = slice(h * bq, (h + 1) * bq)
            p = jnp.exp2(dot_nn(kb, qst[wide, :]))
            if masked:
                p = jnp.where(mask, p, 0.0)
            sg = (p * dot_nn(vb, dst[wide, :])).astype(bf16)
            part = dot_nn(sg, qs[tall, :]) + dot_nn(p.astype(bf16), ds[tall, :])
            add = part if add is None else add + part
            dacc[tall, :] += dot_tn(sg, kvb)
        dkv[rows, :] += add

    @pl.loop(0, nk)
    def _(k_index):
        needed, whole = block_state(seg_ref, start_ref, qi, k_index, bq, bk)

        @pl.when(needed & whole)
        def _():
            step(k_index, False)

        @pl.when(needed & jnp.logical_not(whole))
        def _():
            step(k_index, True)

    for h in range(heads):
        dq_ref[h * D : (h + 1) * D, :] = dacc[h * bq : (h + 1) * bq, :].T[:D, :] * D**-0.5

    @pl.when(qi == pl.num_programs(0) - 1)
    def _():
        lane = lax.broadcasted_iota(jnp.int32, dkv.shape, 1)
        dkv_ref[...] = (dkv[...] * jnp.where(lane < D, LN2, 1.0)).astype(bf16)


def attention_grad(start, seg, q, kv, o, do, l, qpos, qseg, kpos, kseg, bq, bk):
    heads = q.shape[0] // HEAD_DIM
    count, total = q.shape[1], kv.shape[0]
    bq, bk = min(bq, count), min(bk, total)
    whole = lambda *shape: pl.BlockSpec(shape, lambda i, *_: (0,) * len(shape))
    wide = pl.BlockSpec((q.shape[0], bq), lambda i, *_: (0, i))
    return pl.pallas_call(
        functools.partial(bwd_kernel, heads, bq, bk),
        out_shape=(
            jax.ShapeDtypeStruct(q.shape, f32),
            jax.ShapeDtypeStruct(kv.shape, bf16),
        ),
        grid_spec=pltpu.PrefetchScalarGridSpec(
            num_scalar_prefetch=2,
            grid=(count // bq,),
            in_specs=[
                wide,
                whole(*kv.shape),
                wide,
                wide,
                pl.BlockSpec((heads, bq), lambda i, *_: (0, i)),
                pl.BlockSpec((1, bq), lambda i, *_: (0, i)),
                pl.BlockSpec((1, bq), lambda i, *_: (0, i)),
                whole(total, 1),
                whole(total, 1),
            ],
            out_specs=(wide, whole(*kv.shape)),
            scratch_shapes=[
                pltpu.VMEM(kv.shape, bf16),
                pltpu.VMEM(kv.shape, bf16),
                pltpu.VMEM((heads * 2 * HEAD_DIM, bq), bf16),
                pltpu.VMEM((heads * 2 * HEAD_DIM, bq), bf16),
                pltpu.VMEM((heads * bq, 2 * HEAD_DIM), bf16),
                pltpu.VMEM((heads * bq, 2 * HEAD_DIM), bf16),
                pltpu.VMEM((heads * bq, 2 * HEAD_DIM), f32),
                pltpu.VMEM(kv.shape, f32),
            ],
        ),
        cost_estimate=pl.CostEstimate(flops=heads * count * total * 640, bytes_accessed=8 << 20, transcendentals=heads * count * total // 2),
        name="attend_grad",
    )(start, seg, q, kv, o, do, l, qpos.reshape(1, -1), qseg.reshape(1, -1), kpos.reshape(-1, 1), kseg.reshape(-1, 1))


HEADS = 16
KV_HEADS = 4
rope_base = 10000.0
SHARE = ("dp", "context")
EVERY = ("dp", "context", "tensor")
QUERY_BLOCK = 512
KEY_BLOCK = 512


def unit_rows(values):
    r = lax.rsqrt(jnp.mean(values * values, axis=-1, keepdims=True) + epsilon)
    return values * r, r


def norm_back(grad, values, gains):
    n, r = unit_rows(values)
    scaled = grad * gains
    return r * (scaled - n * jnp.mean(scaled * n, axis=-1, keepdims=True)), jnp.sum(grad * n, axis=0)


def mixed_silu(gate_in, up_in):
    return jax.nn.silu(gate_in) * up_in


def gathered(part, axes, axis):
    return lax.all_gather(part, axes, axis=axis, tiled=True)


def scattered(part, axes, axis):
    return lax.psum_scatter(part.astype(bf16), axes, scatter_dimension=axis, tiled=True)


def rope_tables(positions):
    half = HEAD_DIM // 2
    inverse = jnp.exp(-math.log(rope_base) * jnp.arange(half, dtype=f32) * 2.0 / HEAD_DIM)
    angles = inverse[:, None] * positions.astype(f32)[None, :]
    return jnp.cos(angles), jnp.sin(angles)


def body(
    layer_input, cotangent, w_qkv, w_out, attn_gain, qk_gain, w_gate, w_up, w_down, ffn_gain, seg_ids, pos_ids
):
    _, rows, width = layer_input.shape
    ways = lax.axis_size("tensor")
    heads = HEADS // ways
    mine = lax.axis_index("tensor")
    group_seg, group_pos = seg_ids[0], pos_ids[0]
    first_row = lax.axis_index("context") * rows
    my_seg = lax.dynamic_slice_in_dim(group_seg, first_row, rows, 0)
    my_pos = lax.dynamic_slice_in_dim(group_pos, first_row, rows, 0)
    start = jnp.reshape(first_row, (1,)).astype(jnp.int32)
    part_rows = rows // ways

    def own_rows(values):
        return lax.dynamic_slice_in_dim(values, mine * part_rows, part_rows, 0)

    columns = w_qkv.shape[1]
    qkv_shard = w_qkv.T
    packed = jnp.concatenate(
        [qkv_shard, attn_gain[None], ffn_gain[None], jnp.zeros((14, w_qkv.shape[0]), bf16)], axis=0
    )
    packed_all = gathered(packed, SHARE, 1)
    qkv_mine = packed_all[:columns]
    attn_gain_all = packed_all[columns].astype(f32)
    ffn_gain_all = packed_all[columns + 1].astype(f32)
    out_all = gathered(gathered(w_out, "tensor", 0), SHARE, 1)
    out_mine = lax.dynamic_slice_in_dim(out_all, mine * w_out.shape[0], w_out.shape[0], 0)
    gate_all = gathered(w_gate, SHARE, 0)
    up_all = gathered(w_up, SHARE, 0)
    down_all = gathered(w_down, SHARE, 1)
    qkv_all = gathered(gathered(qkv_shard, "tensor", 0), SHARE, 1)

    inputs = layer_input.reshape(rows, width).astype(f32)
    normed_low = (unit_rows(inputs)[0] * attn_gain_all).astype(bf16)
    joint = dot_nt(qkv_mine, normed_low)
    cos, sin = rope_tables(my_pos)
    gains = qk_gain.T
    queries, kv_mine = prep(joint, cos, sin, gains, heads, 512)
    kv = gathered(kv_mine, "context", 0)
    places = (my_pos, my_seg, group_pos, group_seg)
    attended, log_total = attention(start, group_seg, queries, kv, *places, QUERY_BLOCK, KEY_BLOCK)
    attended_all = gathered(attended, "tensor", 0)
    resid = inputs + dot_tn(attended_all, out_all)

    normed_ffn = (unit_rows(resid)[0] * ffn_gain_all).astype(bf16)
    gate = dot_nn(normed_ffn, gate_all)
    up = dot_nn(normed_ffn, up_all)
    act = mixed_silu(gate, up).astype(bf16)
    resid_part = own_rows(resid)
    ffn_part = scattered(dot_nn(act, down_all), "tensor", 0).astype(f32)
    layer_output = gathered((resid_part + ffn_part).astype(bf16), "tensor", 0)

    cot = cotangent.reshape(rows, width)
    act_grad = dot_nt(cot, down_all)
    _, silu_pull = jax.vjp(mixed_silu, gate, up)
    gate_grad, up_grad = (g.astype(bf16) for g in silu_pull(act_grad))
    ffn_in_grad = scattered(dot_nt(gate_grad, gate_all) + dot_nt(up_grad, up_all), "tensor", 0).astype(f32)
    grad_gate = dot_tn(normed_ffn, gate_grad)
    grad_up = dot_tn(normed_ffn, up_grad)
    grad_down = dot_tn(act, cot)
    norm_grad, ffn_gain_part = norm_back(ffn_in_grad, resid_part, ffn_gain_all)
    branch_part = (own_rows(cot).astype(f32) + norm_grad).astype(bf16)
    branch = gathered(branch_part, "tensor", 0)

    attended_grad = dot_nt(out_mine, branch).astype(bf16)
    grad_out = dot_nn(attended, branch)
    query_grad, kv_grad_group = attention_grad(
        start, group_seg, queries, kv, attended, attended_grad, log_total, *places, QUERY_BLOCK, KEY_BLOCK
    )
    kv_grad = scattered(kv_grad_group, "context", 0)
    joint_grad, qk_part = unprep(joint, cos, sin, gains, query_grad, kv_grad, heads, 512)
    joint_grad_all = gathered(joint_grad, "tensor", 0)
    grad_qkv = lax.dot_general(normed_low, joint_grad, (((0,), (1,)), ((), ())), preferred_element_type=f32)
    attn_gain_part = jnp.sum(qkv_mine.astype(f32) * grad_qkv.T, axis=0) / attn_gain_all
    in_grad = dot_tn(joint_grad_all, qkv_all)
    grad_input = (branch.astype(f32) + norm_back(in_grad, inputs, attn_gain_all)[0]).astype(bf16)

    small = lax.psum(jnp.concatenate([attn_gain_part, ffn_gain_part, qk_part.T.reshape(-1)]), EVERY)
    share = attn_gain.shape[0]
    place = (lax.axis_index("dp") * lax.axis_size("context") + lax.axis_index("context")) * share
    grad_attn_gain = lax.dynamic_slice_in_dim(small, place, share, 0)
    grad_ffn_gain = lax.dynamic_slice_in_dim(small, width + place, share, 0)
    grad_qk_gain = small[2 * width :].reshape(2, HEAD_DIM)
    return (
        layer_output.reshape(layer_input.shape),
        grad_input.reshape(layer_input.shape),
        scattered(grad_qkv, SHARE, 0).astype(f32),
        scattered(grad_out, SHARE, 1).astype(f32),
        grad_attn_gain,
        grad_qk_gain,
        scattered(grad_gate, SHARE, 0).astype(f32),
        scattered(grad_up, SHARE, 0).astype(f32),
        scattered(grad_down, SHARE, 1).astype(f32),
        grad_ffn_gain,
    )


def solution(mesh):
    tokens, by_row, by_column = P("dp", "context", None), P(SHARE, "tensor"), P("tensor", SHARE)
    gain = P(SHARE)
    return jax.shard_map(
        body,
        mesh=mesh,
        in_specs=(
            tokens, tokens, by_row, by_column, gain, P(), by_row, by_row, by_column, gain, P("dp", None), P("dp", None)
        ),
        out_specs=(tokens, tokens, by_row, by_column, gain, P(), by_row, by_row, by_column, gain),
        check_vma=False,
    )
```

time: 2430 us -> 1580 us (0.65)
  matrix products: 547 us -> 231 us
  waiting for transfers between devices: 1360 us -> 1070 us
  other arithmetic: 295 us -> 48.6 us
  Pallas kernels: 0 us -> 70.7 us
  local copies, waits for them, and re-layouts: 124 us -> 62.9 us
    psum x3 -> x0, waiting for transfers between devices: 1130 us -> none  [tensor_total(): lax.psum(partial_term.astype(jnp.bfloat16), 'tensor').astype(jnp.float32)]
    all_gather x6 -> x11, waiting for transfers between devices: 99.7 us -> 636 us  [gathered(): return lax.all_gather(part, axes, axis=axis, tiled=True)]
    dot_general x127 -> x15, matrix products: 547 us -> 231 us  [the longest x5 87.9 us: dot_tn(): lax.dot_general(a, b, (((0,), (0,)), ((), ())), preferred_element_type=f32)]
    reduce_scatter x6 -> x8, waiting for transfers between devices: 121 us -> 430 us  [scattered(): lax.psum_scatter(part.astype(bf16), axes, scatter_dimension=axis, tiled=T...]
    another operation x23 -> x0, other arithmetic: 132 us -> none
    dynamic_update_slice x16 -> x0, local copies, waits for them, and re-layouts: 72.3 us -> none  [body(): lax.map(forward_block, (queries[member].reshape(block_count, block_rows,...]
    pallas_call x0 -> x4, Pallas kernels: none -> 70.7 us  [the longest x1 40.5 us: attention_grad(): pl.pallas_call(functools.partial(bwd_kernel, heads, bq, bk), out_shape=(j...]
    reduce_sum x24 -> x3, other arithmetic: 59.7 us -> 11.4 us  [the longest x2 7.66 us: unit_rows(): r = lax.rsqrt(jnp.mean(values * values, axis=-1, keepdims=True) + epsilon)]
  transfers between devices with their start and end apart: 15 -> 19, of which waited for: 12 -> 17; matrix products, arithmetic and copies ran while one was open for 12% -> 13% of each run, Pallas kernels for 0% -> 2%
where the time goes in v1:
time: 1580 us; the launch traced here: 1570 us
  waiting for transfers between devices  1070 us (68%)
  matrix products  231 us (15%)
  blocking collectives  74.5 us (5%)
  Pallas kernels  70.7 us (4%)
  local copies, waits for them, and re-layouts  62.9 us (4%)
  other arithmetic  48.6 us (3%)
    all_gather x11, waiting for transfers between devices, gathered(): return lax.all_gather(part, axes, axis=axis, tiled=True)  636 us
    reduce_scatter x8, waiting for transfers between devices, scattered(): lax.psum_scatter(part.astype(bf16), axes, scatter_dimension=axis, tiled=T...  430 us
    dot_general x5, matrix products, dot_tn(): lax.dot_general(a, b, (((0,), (0,)), ((), ())), preferred_element_type=f32)  87.9 us
    dot_general x5, matrix products, dot_nt(): lax.dot_general(a, b, (((1,), (1,)), ((), ())), preferred_element_type=f32)  75.2 us
    dot_general x4, matrix products, dot_nn(): lax.dot_general(a, b, (((1,), (0,)), ((), ())), preferred_element_type=f32)  59 us
    unnamed x43, local copies, waits for them, and re-layouts  49.6 us
    pallas_call x1, Pallas kernels, attention_grad(): pl.pallas_call(functools.partial(bwd_kernel, heads, bq, bk), out_shape=(j...  40.5 us
    psum x1, blocking collectives, body(): lax.psum(jnp.concatenate([attn_gain_part, ffn_gain_part, qk_part.T.reshap...  39.5 us
  transfers between devices with their start and end apart: 19, of which 17 were waited for; matrix products, arithmetic and copies ran while one was open for 13% of the time, Pallas kernels for 2%

profile of v1, /device:TPU:0, one launch (start us, length us, event | category | flops | bytes accessed | tf_op | source)
XLA Modules:
  0.0 1572.0 jit_solution(17499870750281244749)
XLA Ops:
  54.2 16.4 %all_gather.42 = bf16[1024,256]{1,0:T(8,128)(2,1)} all-gather(bf16[256,256]{1,0:T(8,128)(2,1)S(1)} %copy-done.4), channel_id=1, replica_groups=mesh['dp'=4,'context'=2,'tensor'=4] {'tensor'}, dimensions={0}, use_global_device_ids=true | all-gather | bytes 655360 | tf_op jit(solution)/shard_map/all_gather | solution.py:370
  75.6 20.0 %attend.1 = (bf16[256,2048]{1,0:T(8,128)(2,1)}, f32[4,2048]{1,0:T(4,128)}) custom-call(s32[1]{0:T(128)} %bitcast.1.start_ref, s32[4096]{0:T(1024)} %bitcast.82, bf16[256,2048]{1,0:T(8,128)(2,1)} %get-tuple-element.18.q_ref, bf16[4096,128]{1,0:T(8,128)(2,1)} %all-gather.14.cloned.1.call-done.kv_ref, s32[2048,1]{1,0:T(8,128)} %copy.36.qpos_ref, ...), custom_call_target="tpu_custom_call" | custom-call | flops 8589934592 | bytes 4194304 | tf_op jit(solution)/shard_map/attend/pallas_call | solution.py:192
  97.8 17.2 %all-gather.18.cloned.1.call-done = bf16[1024,2048]{1,0:T(8,128)(2,1)} async-done(((bf16[1024,256]{1,0:T(8,128)(2,1)}), bf16[1024,2048]{1,0:T(8,128)(2,1)}) %all-gather.18.cloned.1.call-update) | async-done | bytes 4194320 | tf_op jit(solution)/shard_map/all_gather | solution.py:370
  115.0 82.2 %all-gather.16.cloned.1.call-done = bf16[1024,2048]{1,0:T(8,128)(2,1)} async-done(((bf16[256,2048]{1,0:T(8,128)(2,1)}), bf16[1024,2048]{1,0:T(8,128)(2,1)}) %all-gather.16.cloned.1.call-update) | async-done | bytes 4194320 | tf_op jit(solution)/shard_map/all_gather | solution.py:370
  197.2 15.1 multiply_reduce_fusion
  222.5 16.2 %all-gather.20.cloned.1.call-done = bf16[2048,1280]{1,0:T(8,128)(2,1)} async-done(((bf16[256,1280]{1,0:T(8,128)(2,1)}), bf16[2048,1280]{1,0:T(8,128)(2,1)}) %all-gather.20.cloned.1.call-update) | async-done | bytes 5242896 | tf_op jit(solution)/shard_map/all_gather | solution.py:370
  238.6 17.6 %fusion.39 = f32[2048,1280]{1,0:T(8,128)} fusion(bf16[2048,2048]{0,1:T(8,128)(2,1)} %multiply_convert_fusion, bf16[2048,1280]{1,0:T(8,128)(2,1)} %all-gather.20.cloned.1.call-done), kind=kOutput, calls=%fused_computation.70 | convolution fusion | flops 10737418240 | bytes 24117248 | tf_op jit(solution)/shard_map/dot_general | solution.py:20
  256.2 25.3 %all-gather.22.cloned.1.call-done = bf16[2048,1280]{1,0:T(8,128)(2,1)} async-done(((bf16[256,1280]{1,0:T(8,128)(2,1)}), bf16[2048,1280]{1,0:T(8,128)(2,1)}) %all-gather.22.cloned.1.call-update) | async-done | bytes 5242896 | tf_op jit(solution)/shard_map/all_gather | solution.py:370
  281.5 18.0 %fusion.40 = f32[2048,1280]{1,0:T(8,128)} fusion(bf16[2048,2048]{0,1:T(8,128)(2,1)} %multiply_convert_fusion, bf16[2048,1280]{1,0:T(8,128)(2,1)} %all-gather.22.cloned.1.call-done), kind=kOutput, calls=%fused_computation.71 | convolution fusion | flops 10737418240 | bytes 24117248 | tf_op jit(solution)/shard_map/dot_general | solution.py:20
  299.5 25.9 %all-gather.24.cloned.1.call-done = bf16[1280,2048]{1,0:T(8,128)(2,1)} async-done(((bf16[1280,256]{1,0:T(8,128)(2,1)}), bf16[1280,2048]{1,0:T(8,128)(2,1)}) %all-gather.24.cloned.1.call-update) | async-done | bytes 5242896 | tf_op jit(solution)/shard_map/all_gather | solution.py:370
  325.5 23.5 %multiply_convert_fusion.1 = (bf16[2048,1280]{1,0:T(8,128)(2,1)}, bf16[2048,1280]{1,0:T(8,128)(2,1)}, bf16[2048,1280]{1,0:T(8,128)(2,1)}) fusion(f32[2048,1280]{1,0:T(8,128)} %fusion.39, f32[2048,1280]{1,0:T(8,128)} %fusion.40, bf16[1280,2048]{1,0:T(8,128)(2,1)} %all-gather.24.cloned.1.call-done, bf16[1,2048,2048]{2,1,0:T(8,128)(2,1)} %param.13), kind=kOutput, calls=%fused_computation.20 | convolution fusion | flops 10779361280 | bytes 50331648 | tf_op jit(solution)/shard_map/dot_general | solution.py:17
  348.9 18.1 %fusion.41 = f32[2048,2048]{0,1:T(8,128)} fusion(bf16[2048,1280]{1,0:T(8,128)(2,1)} %get-tuple-element.51, bf16[2048,1280]{1,0:T(8,128)(2,1)} %all-gather.20.cloned.1.call-done), kind=kOutput, calls=%fused_computation.72 | convolution fusion | flops 10737418240 | bytes 27262976 | tf_op jit(solution)/shard_map/dot_general | solution.py:17
  367.0 17.4 %add_convert_fusion = bf16[2048,2048]{0,1:T(8,128)(2,1)} fusion(f32[2048,2048]{0,1:T(8,128)} %fusion.41, bf16[2048,1280]{1,0:T(8,128)(2,1)} %get-tuple-element.50, bf16[2048,1280]{1,0:T(8,128)(2,1)S(1)} %copy-done.17), kind=kOutput, calls=%fused_computation.13 | convolution fusion | flops 10745806848 | bytes 35651584 | tf_op jit(solution)/shard_map/dot_general | solution.py:17
  384.4 16.6 %convolution_convert_fusion = bf16[2048,2048]{0,1:T(8,128)(2,1)} fusion(bf16[2048,1280]{1,0:T(8,128)(2,1)} %get-tuple-element.52, bf16[1280,2048]{1,0:T(8,128)(2,1)} %all-gather.24.cloned.1.call-done), kind=kOutput, calls=%fused_computation.30 | convolution fusion | flops 10741612544 | bytes 18874368 | tf_op jit(solution)/shard_map/dot_general | solution.py:20
  409.7 119.3 %reduce-scatter.11.cloned.1.call-done = bf16[512,2048]{0,1:T(8,128)(2,1)} async-done(((bf16[2048,2048]{0,1:T(8,128)(2,1)}), bf16[512,2048]{0,1:T(8,128)(2,1)}) %reduce-scatter.11.cloned.1.call-update) | async-done | bytes 2097168 | tf_op jit(solution)/shard_map/reduce_scatter | solution.py:374
  532.8 143.9 %reduce-scatter.9.cloned.1.call-done = bf16[512,2048]{0,1:T(8,128)(2,1)} async-done(((bf16[2048,2048]{0,1:T(8,128)(2,1)}), bf16[512,2048]{0,1:T(8,128)(2,1)}) %reduce-scatter.9.cloned.1.call-update) | async-done | bytes 2097168 | tf_op jit(solution)/shard_map/reduce_scatter | solution.py:374
  686.9 145.8 %all-gather.28.cloned.1.call-done = bf16[2048,2048]{0,1:T(8,128)(2,1)} async-done(((bf16[512,2048]{0,1:T(8,128)(2,1)}), bf16[2048,2048]{0,1:T(8,128)(2,1)}) %all-gather.28.cloned.1.call-update) | async-done | bytes 8388624 | tf_op jit(solution)/shard_map/all_gather | solution.py:370
  839.7 40.5 %attend_grad.1 = (f32[256,2048]{1,0:T(8,128)}, bf16[4096,128]{1,0:T(8,128)(2,1)}) custom-call(s32[1]{0:T(128)} %bitcast.1.start_ref, s32[4096]{0:T(1024)} %bitcast.84, bf16[256,2048]{1,0:T(8,128)(2,1)} %get-tuple-element.18.q_ref, bf16[4096,128]{1,0:T(8,128)(2,1)} %all-gather.14.cloned.1.call-done.kv_ref, bf16[256,2048]{1,0:T(8,128)(2,1)} %get-tuple-element.20.o_ref, ...), custom_call_target="tpu_custom_call" | custom-call | flops 21474836480 | bytes 8388608 | tf_op jit(solution)/shard_map/attend_grad/pallas_call | solution.py:308
  880.3 16.5 %convolution_convert_fusion.2 = bf16[2048,1280]{1,0:T(8,128)(2,1)} fusion(bf16[2048,2048]{0,1:T(8,128)(2,1)} %multiply_convert_fusion, bf16[2048,1280]{1,0:T(8,128)(2,1)} %get-tuple-element.51), kind=kOutput, calls=%fused_computation.32 | convolution fusion | flops 10740039680 | bytes 18874368 | tf_op jit(solution)/shard_map/dot_general | solution.py:23
  896.9 16.6 %convolution_convert_fusion.1 = bf16[2048,1280]{1,0:T(8,128)(2,1)} fusion(bf16[2048,2048]{0,1:T(8,128)(2,1)} %multiply_convert_fusion, bf16[2048,1280]{1,0:T(8,128)(2,1)} %get-tuple-element.50), kind=kOutput, calls=%fused_computation.31 | convolution fusion | flops 10740039680 | bytes 18874368 | tf_op jit(solution)/shard_map/dot_general | solution.py:23
  913.5 16.6 %fusion.19 = bf16[1280,2048]{1,0:T(8,128)(2,1)} fusion(bf16[2048,1280]{1,0:T(8,128)(2,1)} %get-tuple-element.52, bf16[1,2048,2048]{2,1,0:T(8,128)(2,1)} %param.13), kind=kOutput, calls=%fused_computation.29 | convolution fusion | flops 10740039680 | bytes 18874368 | tf_op jit(solution)/shard_map/dot_general | solution.py:23
  953.3 18.7 %all_gather.50 = bf16[1536,256]{1,0:T(8,128)(2,1)} all-gather(bf16[384,256]{1,0:T(8,128)(2,1)S(1)} %bitcast.71), channel_id=1, replica_groups=mesh['dp'=4,'context'=2,'tensor'=4] {'tensor'}, dimensions={0}, use_global_device_ids=true | all-gather | bytes 983040 | tf_op jit(solution)/shard_map/all_gather | solution.py:370
  972.8 25.1 %reduce-scatter.19.cloned.1.call-done = bf16[256,1280]{1,0:T(8,128)(2,1)} async-done(((bf16[2048,1280]{1,0:T(8,128)(2,1)}), bf16[256,1280]{1,0:T(8,128)(2,1)}) %reduce-scatter.19.cloned.1.call-update) | async-done | bytes 655376 | tf_op jit(solution)/shard_map/reduce_scatter | solution.py:374
  1000.1 57.7 %reduce-scatter.21.cloned.1.call-done = bf16[256,1280]{1,0:T(8,128)(2,1)} async-done(((bf16[2048,1280]{1,0:T(8,128)(2,1)}), bf16[256,1280]{1,0:T(8,128)(2,1)}) %reduce-scatter.21.cloned.1.call-update) | async-done | bytes 655376 | tf_op jit(solution)/shard_map/reduce_scatter | solution.py:374
  1060.1 58.6 %reduce-scatter.23.cloned.1.call-done = bf16[1280,256]{1,0:T(8,128)(2,1)} async-done(((bf16[1280,2048]{1,0:T(8,128)(2,1)}), bf16[1280,256]{1,0:T(8,128)(2,1)}) %reduce-scatter.23.cloned.1.call-update) | async-done | bytes 655376 | tf_op jit(solution)/shard_map/reduce_scatter | solution.py:374
  1120.9 148.8 %all-gather.26.cloned.1.call-done = bf16[2048,2048]{0,1:T(8,128)(2,1)} async-done(((bf16[512,2048]{0,1:T(8,128)(2,1)}), bf16[2048,2048]{0,1:T(8,128)(2,1)}) %all-gather.26.cloned.1.call-update) | async-done | bytes 8388624 | tf_op jit(solution)/shard_map/all_gather | solution.py:370
  1282.0 25.0 %reduce-scatter.17.cloned.1.call-done = bf16[256,256]{1,0:T(8,128)(2,1)} async-done(((bf16[256,2048]{1,0:T(8,128)(2,1)}), bf16[256,256]{1,0:T(8,128)(2,1)}) %reduce-scatter.17.cloned.1.call-update) | async-done | bytes 131088 | tf_op jit(solution)/shard_map/reduce_scatter | solution.py:374
  1308.8 39.5 %psum.7 = f32[4224]{0:T(1024)S(1)} all-reduce(f32[4224]{0:T(1024)S(1)} %pad_maximum_fusion), channel_id=1, replica_groups=mesh['dp'=4,'context'=2,'tensor'=4] {'dp','context','tensor'}, use_global_device_ids=true, to_apply=%region_12.13 | all-reduce | flops 4224 | bytes 33792 | tf_op jit(solution)/shard_map/psum | solution.py:462
  1351.4 46.0 %all-gather.32.cloned.1.call-done = bf16[1536,2048]{1,0:T(8,128)(2,1)} async-done(((bf16[1536,256]{1,0:T(8,128)(2,1)}), bf16[1536,2048]{1,0:T(8,128)(2,1)}) %all-gather.32.cloned.1.call-update) | async-done | bytes 6291472 | tf_op jit(solution)/shard_map/all_gather | solution.py:370
  1397.3 117.0 %all-gather.30.cloned.1.call-done = bf16[1536,2048]{1,0:T(8,128)(2,1)} async-done(((bf16[384,2048]{1,0:T(8,128)(2,1)}), bf16[1536,2048]{1,0:T(8,128)(2,1)}) %all-gather.30.cloned.1.call-update) | async-done | bytes 6291472 | tf_op jit(solution)/shard_map/all_gather | solution.py:370
  1514.3 23.2 %fusion.4 = (f32[2048]{0:T(1024)S(1)}, f32[2048,2048]{0,1:T(8,128)}) fusion(bf16[1,2048,2048]{1,2,0:T(8,128)(2,1)} %copy.33, f32[2048]{0:T(1024)S(1)} %bitcast.80, f32[2048]{0:T(1024)S(1)} %copy-done.14, bf16[1536,2048]{1,0:T(8,128)(2,1)} %all-gather.30.cloned.1.call-done, bf16[1536,2048]{1,0:T(8,128)(2,1)} %all-gather.32.cloned.1.call-done), kind=kOutput, calls=%fused_computation.7 | convolution fusion | flops 12905871360 | bytes 37773312 | tf_op jit(solution)/shard_map/dot_general | solution.py:23
  1537.5 15.4 fusion.14
  (128 shorter events, 153.9 us)
Async XLA Ops:
  7.2 32.4 %all-gather.12.cloned.1.call-start = ((), (), s32[]{:S(2)}) async-start(), calls=%async_computation.8 | async-start | bytes 1843200 | tf_op jit(solution)/shard_map/all_gather | solution.py:370
  8.3 14.6 copy-start.1
  10.6 65.1 %all-gather.14.cloned.1.call-start = ((), (), s32[]{:S(2)}) async-start(), calls=%async_computation.9 | async-start | bytes 1572864 | tf_op jit(solution)/shard_map/all_gather | solution.py:370
  10.6 12.3 copy-start.15
  28.7 11.7 copy-start.13
  28.8 41.9 %copy-start.11 = (s32[1,2048]{1,0:T(1,128)}, s32[1,2048]{1,0:T(1,128)S(1)}, u32[]{:S(2)}) copy-start(s32[1,2048]{1,0:T(1,128)S(1)} %get-tuple-element.49.qpos_ref) | copy-start | bytes 24580
  40.5 9.3 copy-start.5
  40.5 13.8 copy-start.4
  49.8 22.3 %copy-start.7 = (s32[1,4096]{1,0:T(1,128)S(1)}, s32[1,4096]{1,0:T(1,128)}, u32[]{:S(2)}) copy-start(s32[1,4096]{1,0:T(1,128)} %param.22) | copy-start | bytes 49156
  54.2 60.8 %all-gather.18.cloned.1.call-start = ((), (), s32[]{:S(2)}) async-start(), calls=%async_computation.11 | async-start | bytes 4718592 | tf_op jit(solution)/shard_map/all_gather | solution.py:370
  70.6 126.6 %all-gather.16.cloned.1.call-start = ((), (), s32[]{:S(2)}) async-start(), calls=%async_computation.10 | async-start | bytes 5242880 | tf_op jit(solution)/shard_map/all_gather | solution.py:370
  95.7 143.0 %all-gather.20.cloned.1.call-start = ((), (), s32[]{:S(2)}) async-start(), calls=%async_computation.12 | async-start | bytes 5898240 | tf_op jit(solution)/shard_map/all_gather | solution.py:370
  96.2 185.3 %all-gather.22.cloned.1.call-start = ((), (), s32[]{:S(2)}) async-start(), calls=%async_computation.13 | async-start | bytes 5898240 | tf_op jit(solution)/shard_map/all_gather | solution.py:370
  96.8 228.6 %all-gather.24.cloned.1.call-start = ((), (), s32[]{:S(2)}) async-start(), calls=%async_computation.14 | async-start | bytes 5898240 | tf_op jit(solution)/shard_map/all_gather | solution.py:370
  97.6 431.4 %reduce-scatter.11.cloned.1.call-start = ((), (), s32[]{:S(2)}) async-start(), calls=%async_computation.17 | async-start | bytes 10485760 | tf_op jit(solution)/shard_map/reduce_scatter | solution.py:374
  348.9 18.1 %copy-start.17 = (bf16[2048,1280]{1,0:T(8,128)(2,1)S(1)}, bf16[2048,1280]{1,0:T(8,128)(2,1)}, u32[]{:S(2)}) copy-start(bf16[2048,1280]{1,0:T(8,128)(2,1)} %all-gather.22.cloned.1.call-done) | copy-start | bytes 15728644
  384.4 292.3 %reduce-scatter.9.cloned.1.call-start = ((), (), s32[]{:S(2)}) async-start(), calls=%async_computation.15 | async-start | bytes 10485760 | tf_op jit(solution)/shard_map/reduce_scatter | solution.py:374
  401.1 431.6 %all-gather.28.cloned.1.call-start = ((), (), s32[]{:S(2)}) async-start(), calls=%async_computation.18 | async-start | bytes 10485760 | tf_op jit(solution)/shard_map/all_gather | solution.py:370
  532.7 149.5 %copy-start.10 = (s32[1,4096]{1,0:T(1,128)S(1)}, s32[1,4096]{1,0:T(1,128)}, u32[]{:S(2)}) copy-start(s32[1,4096]{1,0:T(1,128)} %param.23) | copy-start | bytes 49156
  532.7 151.6 %copy-start.8 = (s32[1,4096]{1,0:T(1,128)S(1)}, s32[1,4096]{1,0:T(1,128)}, u32[]{:S(2)}) copy-start(s32[1,4096]{1,0:T(1,128)} %param.22) | copy-start | bytes 49156
  682.2 256.0 %reduce-scatter.13.cloned.1.call-start = ((), (), s32[]{:S(2)}) async-start(), calls=%async_computation.19 | async-start | bytes 1572864 | tf_op jit(solution)/shard_map/reduce_scatter | solution.py:374
  880.3 117.6 %reduce-scatter.19.cloned.1.call-start = ((), (), s32[]{:S(2)}) async-start(), calls=%async_computation.24 | async-start | bytes 5898240 | tf_op jit(solution)/shard_map/reduce_scatter | solution.py:374
  896.9 161.0 %reduce-scatter.21.cloned.1.call-start = ((), (), s32[]{:S(2)}) async-start(), calls=%async_computation.25 | async-start | bytes 5898240 | tf_op jit(solution)/shard_map/reduce_scatter | solution.py:374
  913.5 205.2 %reduce-scatter.23.cloned.1.call-start = ((), (), s32[]{:S(2)}) async-start(), calls=%async_computation.26 | async-start | bytes 5898240 | tf_op jit(solution)/shard_map/reduce_scatter | solution.py:374
  930.1 339.6 %all-gather.26.cloned.1.call-start = ((), (), s32[]{:S(2)}) async-start(), calls=%async_computation.16 | async-start | bytes 10485760 | tf_op jit(solution)/shard_map/all_gather | solution.py:370
  930.7 376.3 %reduce-scatter.17.cloned.1.call-start = ((), (), s32[]{:S(2)}) async-start(), calls=%async_computation.23 | async-start | bytes 1179648 | tf_op jit(solution)/shard_map/reduce_scatter | solution.py:374
  938.1 6.0 copy-start.16
  938.2 411.4 %reduce-scatter.15.cloned.1.call-start = ((), (), s32[]{:S(2)}) async-start(), calls=%async_computation.22 | async-start | bytes 1769472 | tf_op jit(solution)/shard_map/reduce_scatter | solution.py:374
  944.1 9.1 copy-start.2
  953.2 444.1 %all-gather.32.cloned.1.call-start = ((), (), s32[]{:S(2)}) async-start(), calls=%async_computation.21 | async-start | bytes 7077888 | tf_op jit(solution)/shard_map/all_gather | solution.py:370
  972.0 542.3 %all-gather.30.cloned.1.call-start = ((), (), s32[]{:S(2)}) async-start(), calls=%async_computation.20 | async-start | bytes 7864320 | tf_op jit(solution)/shard_map/all_gather | solution.py:370
  1269.7 38.9 %copy-start.12 = (f32[64,2]{1,0:T(8,128)S(1)}, f32[64,2]{1,0:T(8,128)}, u32[]{:S(2)}) copy-start(f32[64,2]{1,0:T(8,128)} %get-tuple-element.25) | copy-start | bytes 1540
  (5 other events, 24.7 us)
Sparse Core Ops, SparseCore 0:
  10.7 28.8 all-gather.11
  54.3 21.2 all-gather.13
  77.5 37.4 all-gather.17
  116.4 80.7 all-gather.15
  198.9 39.6 all-gather.19
  240.4 41.1 all-gather.21
  283.4 42.0 all-gather.23
  384.5 144.4 reduce-scatter.10
  531.4 145.2 reduce-scatter.8
  682.3 150.3 all-gather.27
  880.4 57.1 reduce-scatter.12
  941.2 56.6 reduce-scatter.18
  1001.3 56.5 reduce-scatter.20
  1062.1 56.5 reduce-scatter.22
  1120.1 149.6 all-gather.25
  1272.8 34.1 reduce-scatter.16
  1310.1 39.0 reduce-scatter.14
  1350.9 46.3 all-gather.31
  1398.9 115.3 all-gather.29

commit v2 on v1

--- a/solution.py
+++ b/solution.py
@@ -3,6 +3,7 @@
 from jax import lax
 from jax.experimental import pallas as pl
 from jax.experimental.pallas import tpu as pltpu
+from jax.experimental.layout import Layout, with_layout_constraint
 from jax.sharding import PartitionSpec as P
 
 HEAD_DIM = 64
@@ -374,6 +375,68 @@
     return lax.psum_scatter(part.astype(bf16), axes, scatter_dimension=axis, tiled=True)
 
 
+def natural(values):
+    return with_layout_constraint(values, Layout(major_to_minor=tuple(range(values.ndim))))
+
+
+def after(value, *others):
+    return lax.optimization_barrier((value,) + others)[0]
+
+
+def both_halves(part):
+    if lax.axis_size("context") != 2:
+        return gathered(part, "context", 0)
+    other = lax.ppermute(part, "context", [(0, 1), (1, 0)])
+    low = lax.axis_index("context") == 0
+    return jnp.concatenate([jnp.where(low, part, other), jnp.where(low, other, part)], axis=0)
+
+
+def halving_scatter(terms, axes):
+    sizes = [lax.axis_size(axis) for axis in axes]
+    blocks = terms.reshape(tuple(sizes) + (-1,) + terms.shape[1:])
+    for place, axis in enumerate(axes):
+        size, me = sizes[place], lax.axis_index(axis)
+        stride = 1
+        while stride < size:
+            shape = blocks.shape
+            split = blocks.reshape(shape[:place] + (shape[place] // 2, 2) + shape[place + 1 :])
+            bit = (me // stride) % 2
+            kept, sent = (
+                lax.dynamic_index_in_dim(split, index, place + 1, keepdims=False) for index in (bit, 1 - bit)
+            )
+            got = lax.ppermute(sent, axis, [(i, i ^ stride) for i in range(size)])
+            blocks = (kept.astype(f32) + got.astype(f32)).astype(bf16)
+            stride *= 2
+    return blocks.reshape((-1,) + terms.shape[1:])
+
+
+def spread(part):
+    ways, me = lax.axis_size("tensor"), lax.axis_index("tensor")
+    out = lax.dynamic_update_index_in_dim(jnp.zeros((ways,) + part.shape, part.dtype), part, me, 0)
+    for step in range(1, ways):
+        got = lax.ppermute(part, "tensor", [(i, (i + step) % ways) for i in range(ways)])
+        out = lax.dynamic_update_index_in_dim(out, got, (me - step) % ways, 0)
+    return out
+
+
+def line_total(part):
+    total = part
+    ways = lax.axis_size("tensor")
+    for step in range(1, ways):
+        total = total + lax.ppermute(part, "tensor", [(i, (i + step) % ways) for i in range(ways)])
+    return total
+
+
+def swap(blocks):
+    ways, me = lax.axis_size("tensor"), lax.axis_index("tensor")
+    out = blocks
+    for step in range(1, ways):
+        sent = lax.dynamic_index_in_dim(blocks, (me + step) % ways, 0, keepdims=False)
+        got = lax.ppermute(sent, "tensor", [(i, (i + step) % ways) for i in range(ways)])
+        out = lax.dynamic_update_index_in_dim(out, got, (me - step) % ways, 0)
+    return out
+
+
 def rope_tables(positions):
     half = HEAD_DIM // 2
     inverse = jnp.exp(-math.log(rope_base) * jnp.arange(half, dtype=f32) * 2.0 / HEAD_DIM)
@@ -407,75 +470,83 @@
     qkv_mine = packed_all[:columns]
     attn_gain_all = packed_all[columns].astype(f32)
     ffn_gain_all = packed_all[columns + 1].astype(f32)
-    out_all = gathered(gathered(w_out, "tensor", 0), SHARE, 1)
-    out_mine = lax.dynamic_slice_in_dim(out_all, mine * w_out.shape[0], w_out.shape[0], 0)
+    out_all = gathered(spread(w_out).reshape(ways * w_out.shape[0], -1), SHARE, 1)
     gate_all = gathered(w_gate, SHARE, 0)
     up_all = gathered(w_up, SHARE, 0)
     down_all = gathered(w_down, SHARE, 1)
-    qkv_all = gathered(gathered(qkv_shard, "tensor", 0), SHARE, 1)
+    qkv_all = gathered(spread(qkv_shard).reshape(ways * columns, -1), SHARE, 1)
 
     inputs = layer_input.reshape(rows, width).astype(f32)
+    cot = cotangent.reshape(rows, width)
     normed_low = (unit_rows(inputs)[0] * attn_gain_all).astype(bf16)
     joint = dot_nt(qkv_mine, normed_low)
     cos, sin = rope_tables(my_pos)
     gains = qk_gain.T
     queries, kv_mine = prep(joint, cos, sin, gains, heads, 512)
-    kv = gathered(kv_mine, "context", 0)
+    kv = both_halves(kv_mine)
     places = (my_pos, my_seg, group_pos, group_seg)
     attended, log_total = attention(start, group_seg, queries, kv, *places, QUERY_BLOCK, KEY_BLOCK)
     attended_all = gathered(attended, "tensor", 0)
-    resid = inputs + dot_tn(attended_all, out_all)
+    act_grad = dot_nt(after(cot, attended), down_all)
+    resid = inputs + natural(dot_tn(attended_all, out_all))
 
     normed_ffn = (unit_rows(resid)[0] * ffn_gain_all).astype(bf16)
-    gate = dot_nn(normed_ffn, gate_all)
+    gate = dot_nn(after(normed_ffn, act_grad), gate_all)
     up = dot_nn(normed_ffn, up_all)
-    act = mixed_silu(gate, up).astype(bf16)
+    act, silu_pull = jax.vjp(mixed_silu, gate, up)
+    act = act.astype(bf16)
+    gate_grad, up_grad = (g.astype(bf16) for g in silu_pull(act_grad))
+    ffn_in_part = (dot_nt(gate_grad, gate_all) + dot_nt(up_grad, up_all)).astype(bf16)
+    ffn_in_grad = scattered(ffn_in_part, "tensor", 0).astype(f32)
+    act, gate_grad, up_grad, _ = lax.optimization_barrier((act, gate_grad, up_grad, ffn_in_part))
+    ffn_part = dot_nn(act, down_all).astype(bf16)
+    grad_down = dot_tn(cot, act).astype(bf16)
+    grad_gate = dot_tn(normed_ffn, gate_grad).astype(bf16)
+    grad_up = dot_tn(normed_ffn, up_grad).astype(bf16)
     resid_part = own_rows(resid)
-    ffn_part = scattered(dot_nn(act, down_all), "tensor", 0).astype(f32)
-    layer_output = gathered((resid_part + ffn_part).astype(bf16), "tensor", 0)
-
-    cot = cotangent.reshape(rows, width)
-    act_grad = dot_nt(cot, down_all)
-    _, silu_pull = jax.vjp(mixed_silu, gate, up)
-    gate_grad, up_grad = (g.astype(bf16) for g in silu_pull(act_grad))
-    ffn_in_grad = scattered(dot_nt(gate_grad, gate_all) + dot_nt(up_grad, up_all), "tensor", 0).astype(f32)
-    grad_gate = dot_tn(normed_ffn, gate_grad)
-    grad_up = dot_tn(normed_ffn, up_grad)
-    grad_down = dot_tn(act, cot)
     norm_grad, ffn_gain_part = norm_back(ffn_in_grad, resid_part, ffn_gain_all)
-    branch_part = (own_rows(cot).astype(f32) + norm_grad).astype(bf16)
-    branch = gathered(branch_part, "tensor", 0)
-
-    attended_grad = dot_nt(out_mine, branch).astype(bf16)
-    grad_out = dot_nn(attended, branch)
+    resid_grad = own_rows(cot).astype(f32) + norm_grad
+    branch = after(resid_grad.astype(bf16), ffn_part, grad_down, grad_gate, grad_up)
+
+    attended_grad = dot_nt(out_all, branch).astype(bf16)
+    attended_grad = swap(attended_grad.reshape(ways, heads * HEAD_DIM, part_rows))
+    attended_grad = jnp.concatenate([attended_grad[i] for i in range(ways)], axis=1)
+    ffn_sum = scattered(ffn_part, "tensor", 0).astype(f32)
+    layer_output = gathered((resid_part + ffn_sum).astype(bf16), "tensor", 0)
+    attended_part = lax.dynamic_slice_in_dim(attended_all, mine * part_rows, part_rows, 1)
+    grad_out = lax.dot_general(branch, attended_part, (((0,), (1,)), ((), ())), preferred_element_type=f32)
+    grad_out = halving_scatter(grad_out.astype(bf16), SHARE)
+    grad_out = swap(jnp.stack([part.T for part in jnp.split(grad_out, ways, axis=1)]))
     query_grad, kv_grad_group = attention_grad(
         start, group_seg, queries, kv, attended, attended_grad, log_total, *places, QUERY_BLOCK, KEY_BLOCK
     )
-    kv_grad = scattered(kv_grad_group, "context", 0)
+    kv_grad = halving_scatter(kv_grad_group, ("context",))
     joint_grad, qk_part = unprep(joint, cos, sin, gains, query_grad, kv_grad, heads, 512)
-    joint_grad_all = gathered(joint_grad, "tensor", 0)
-    grad_qkv = lax.dot_general(normed_low, joint_grad, (((0,), (1,)), ((), ())), preferred_element_type=f32)
-    attn_gain_part = jnp.sum(qkv_mine.astype(f32) * grad_qkv.T, axis=0) / attn_gain_all
-    in_grad = dot_tn(joint_grad_all, qkv_all)
-    grad_input = (branch.astype(f32) + norm_back(in_grad, inputs, attn_gain_all)[0]).astype(bf16)
-
-    small = lax.psum(jnp.concatenate([attn_gain_part, ffn_gain_part, qk_part.T.reshape(-1)]), EVERY)
+    joint_grad_part = swap(jnp.stack([joint_grad[:, i * part_rows : (i + 1) * part_rows] for i in range(ways)]))
+    in_grad = natural(dot_tn(joint_grad_part.reshape(ways * columns, part_rows), qkv_all))
+    grad_qkv = dot_nn(joint_grad, normed_low)
+    attn_gain_part = jnp.sum(qkv_mine.astype(f32) * grad_qkv, axis=0) / attn_gain_all
+    norm_grad = norm_back(in_grad, own_rows(inputs), attn_gain_all)[0]
+    grad_input = gathered((resid_grad + norm_grad).astype(bf16), "tensor", 0)
+
     share = attn_gain.shape[0]
-    place = (lax.axis_index("dp") * lax.axis_size("context") + lax.axis_index("context")) * share
-    grad_attn_gain = lax.dynamic_slice_in_dim(small, place, share, 0)
-    grad_ffn_gain = lax.dynamic_slice_in_dim(small, width + place, share, 0)
-    grad_qk_gain = small[2 * width :].reshape(2, HEAD_DIM)
+    qk_rows = jnp.tile(qk_part.T, (1, width // HEAD_DIM))
+    grad_qkv = jnp.concatenate(
+        [grad_qkv, attn_gain_part[None], ffn_gain_part[None], qk_rows, jnp.zeros((12, width), f32)], axis=0
+    )
+    grad_qkv = halving_scatter(grad_qkv.astype(bf16).T, SHARE).astype(f32)
+    small = line_total(grad_qkv[:, columns:].T)
     return (
         layer_output.reshape(layer_input.shape),
         grad_input.reshape(layer_input.shape),
-        scattered(grad_qkv, SHARE, 0).astype(f32),
-        scattered(grad_out, SHARE, 1).astype(f32),
-        grad_attn_gain,
-        grad_qk_gain,
-        scattered(grad_gate, SHARE, 0).astype(f32),
-        scattered(grad_up, SHARE, 0).astype(f32),
-        scattered(grad_down, SHARE, 1).astype(f32),
-        grad_ffn_gain,
+        grad_qkv[:, :columns],
+        jnp.sum(grad_out.astype(f32), axis=0),
+        small[0],
+        small[2:4, :HEAD_DIM],
+        halving_scatter(grad_gate, SHARE).astype(f32),
+        halving_scatter(grad_up, SHARE).astype(f32),
+        halving_scatter(grad_down, SHARE).astype(f32).T,
+        small[1],
     )
 
 

time: 1580 us -> 1100 us (0.70)
  waiting for transfers between devices: 1070 us -> 525 us
  starting transfers between devices: 0.99 us -> 119 us
  blocking collectives: 74.5 us -> 0 us
  matrix products: 231 us -> 204 us
  other arithmetic: 48.6 us -> 74.7 us
  local copies, waits for them, and re-layouts: 62.9 us -> 85.3 us
    all_gather x11 -> x9, waiting for transfers between devices: 636 us -> 230 us  [gathered(): return lax.all_gather(part, axes, axis=axis, tiled=True)]
    reduce_scatter x8 -> x2, waiting for transfers between devices: 430 us -> 57.4 us  [scattered(): lax.psum_scatter(part.astype(bf16), axes, scatter_dimension=axis, tiled=T...]
    ppermute x0 -> x35, waiting for transfers between devices: none -> 235 us  [the longest x16 115 us: halving_scatter(): got = lax.ppermute(sent, axis, [(i, i ^ stride) for i in range(size)])]
    ppermute x0 -> x35, starting transfers between devices: none -> 118 us  [the longest x16 49.5 us: halving_scatter(): got = lax.ppermute(sent, axis, [(i, i ^ stride) for i in range(size)])]
    psum x1 -> x0, blocking collectives: 39.5 us -> none  [body(): lax.psum(jnp.concatenate([attn_gain_part, ffn_gain_part, qk_part.T.reshap...]
    all_gather x2 -> x0, blocking collectives: 35.1 us -> none  [gathered(): return lax.all_gather(part, axes, axis=axis, tiled=True)]
    convert_element_type x5 -> x16, other arithmetic: 13.9 us -> 42 us  [the longest x10 13 us: halving_scatter(): blocks = (kept.astype(f32) + got.astype(f32)).astype(bf16)]
    unnamed x43 -> x94, local copies, waits for them, and re-layouts: 49.6 us -> 33 us
  transfers between devices with their start and end apart: 19 -> 46, of which waited for: 17 -> 26; matrix products, arithmetic and copies ran while one was open for 13% -> 24% of each run, Pallas kernels for 2% -> 6%
where the time goes in v2:
time: 1100 us; the launch traced here: 1090 us
  waiting for transfers between devices  525 us (48%)
  matrix products  204 us (19%)
  starting transfers between devices  119 us (11%)
  local copies, waits for them, and re-layouts  85.3 us (8%)
  other arithmetic  74.7 us (7%)
  Pallas kernels  70.2 us (6%)
  between operations  15 us (1%)
    all_gather x9, waiting for transfers between devices, gathered(): return lax.all_gather(part, axes, axis=axis, tiled=True)  230 us
    ppermute x16, waiting for transfers between devices, halving_scatter(): got = lax.ppermute(sent, axis, [(i, i ^ stride) for i in range(size)])  115 us
    ppermute x9, waiting for transfers between devices, swap(): lax.ppermute(sent, 'tensor', [(i, (i + step) % ways) for i in range(ways)])  78 us
    dot_general x5, matrix products, dot_tn(): lax.dot_general(a, b, (((0,), (0,)), ((), ())), preferred_element_type=f32)  73.4 us
    dot_general x5, matrix products, dot_nt(): lax.dot_general(a, b, (((1,), (1,)), ((), ())), preferred_element_type=f32)  63.8 us
    dot_general x4, matrix products, dot_nn(): lax.dot_general(a, b, (((1,), (0,)), ((), ())), preferred_element_type=f32)  63.3 us
    reduce_scatter x2, waiting for transfers between devices, scattered(): lax.psum_scatter(part.astype(bf16), axes, scatter_dimension=axis, tiled=T...  57.4 us
    ppermute x16, starting transfers between devices, halving_scatter(): got = lax.ppermute(sent, axis, [(i, i ^ stride) for i in range(size)])  49.5 us
  transfers between devices with their start and end apart: 46, of which 26 were waited for; matrix products, arithmetic and copies ran while one was open for 24% of the time, Pallas kernels for 6%

profile of v2, /device:TPU:0, one launch (start us, length us, event | category | flops | bytes accessed | tf_op | source)
XLA Modules:
  0.0 1093.0 jit_solution(15112102832054737979)
XLA Ops:
  57.9 14.1 %collective-permute-done = bf16[2048,128]{1,0:T(8,128)(2,1)S(1)} collective-permute-done((bf16[2048,128]{1,0:T(8,128)(2,1)}, bf16[2048,128]{1,0:T(8,128)(2,1)S(1)}, u32[]{:S(2)}, u32[]{:S(2)}) %collective-permute-start) | collective-permute-done | bytes 524320 | tf_op jit(solution)/shard_map/ppermute | solution.py:389
  74.1 20.0 %attend.1 = (bf16[256,2048]{1,0:T(8,128)(2,1)}, f32[4,2048]{1,0:T(4,128)}) custom-call(s32[1]{0:T(128)} %bitcast.1.start_ref, s32[4096]{0:T(1024)} %bitcast.292, bf16[256,2048]{1,0:T(8,128)(2,1)} %get-tuple-element.24.q_ref, bf16[4096,128]{1,0:T(8,128)(2,1)} %pad_maximum_fusion.1.kv_ref, s32[2048,1]{1,0:T(8,128)} %copy.48.qpos_ref, ...), custom_call_target="tpu_custom_call" | custom-call | flops 8589934592 | bytes 4194304 | tf_op jit(solution)/shard_map/attend/pallas_call | solution.py:193
  95.5 17.0 %fusion.41 = f32[2048,1280]{1,0:T(8,128)} fusion(bf16[2048,2048]{1,0:T(8,128)(2,1)} %bitcast.274, bf16[1280,2048]{1,0:T(8,128)(2,1)} %all-gather.16.cloned.1.call-done), kind=kOutput, calls=%fused_computation.166 | convolution fusion | flops 10737418240 | bytes 24117248 | tf_op jit(solution)/shard_map/dot_general | solution.py:18
  112.6 14.6 %all-gather.14.cloned.1.call-done = bf16[1024,2048]{1,0:T(8,128)(2,1)} async-done(((bf16[1024,256]{1,0:T(8,128)(2,1)}), bf16[1024,2048]{1,0:T(8,128)(2,1)}) %all-gather.14.cloned.1.call-update) | async-done | bytes 4194320 | tf_op jit(solution)/shard_map/all_gather | solution.py:371
  127.1 82.2 %all-gather.12.cloned.1.call-done = bf16[1024,2048]{1,0:T(8,128)(2,1)} async-done(((bf16[256,2048]{1,0:T(8,128)(2,1)}), bf16[1024,2048]{1,0:T(8,128)(2,1)}) %all-gather.12.cloned.1.call-update) | async-done | bytes 4194320 | tf_op jit(solution)/shard_map/all_gather | solution.py:371
  209.4 14.8 %multiply_reduce_fusion = (f32[2048]{0:T(1024)S(1)}, f32[2048,2048]{1,0:T(8,128)S(1)}) fusion(bf16[1024,2048]{1,0:T(8,128)(2,1)} %all-gather.12.cloned.1.call-done, bf16[1024,2048]{1,0:T(8,128)(2,1)} %all-gather.14.cloned.1.call-done, bf16[1,2048,2048]{2,1,0:T(8,128)(2,1)} %param.12), kind=kOutput, calls=%fused_computation.8 | convolution fusion | flops 8606709760 | bytes 33562624 | tf_op jit(solution)/shard_map/dot_general | solution.py:24
  234.5 16.3 %all-gather.20.cloned.1.call-done = bf16[2048,1280]{1,0:T(8,128)(2,1)} async-done(((bf16[256,1280]{1,0:T(8,128)(2,1)}), bf16[2048,1280]{1,0:T(8,128)(2,1)}) %all-gather.20.cloned.1.call-update) | async-done | bytes 5242896 | tf_op jit(solution)/shard_map/all_gather | solution.py:371
  250.8 16.5 %fusion.42 = f32[2048,1280]{1,0:T(8,128)} fusion(bf16[2048,2048]{1,0:T(8,128)(2,1)} %multiply_convert_fusion, bf16[2048,1280]{1,0:T(8,128)(2,1)} %all-gather.20.cloned.1.call-done), kind=kOutput, calls=%fused_computation.167 | convolution fusion | flops 10737418240 | bytes 24117248 | tf_op jit(solution)/shard_map/dot_general | solution.py:21
  267.3 26.4 %all-gather.18.cloned.1.call-done = bf16[2048,1280]{1,0:T(8,128)(2,1)} async-done(((bf16[256,1280]{1,0:T(8,128)(2,1)}), bf16[2048,1280]{1,0:T(8,128)(2,1)}) %all-gather.18.cloned.1.call-update) | async-done | bytes 5242896 | tf_op jit(solution)/shard_map/all_gather | solution.py:371
  293.7 26.3 %multiply_convert_fusion.1 = (bf16[2048,1280]{1,0:T(8,128)(2,1)}, bf16[2048,1280]{1,0:T(8,128)(2,1)}, bf16[2048,1280]{1,0:T(8,128)(2,1)}) fusion(f32[2048,1280]{1,0:T(8,128)} %fusion.41, f32[2048,1280]{1,0:T(8,128)} %fusion.42, bf16[2048,2048]{1,0:T(8,128)(2,1)} %multiply_convert_fusion, bf16[2048,1280]{1,0:T(8,128)(2,1)} %all-gather.18.cloned.1.call-done), kind=kOutput, calls=%fused_computation.13 | convolution fusion | flops 10779361280 | bytes 50331648 | tf_op jit(solution)/shard_map/dot_general | solution.py:21
  320.0 18.1 %fusion.43 = f32[2048,2048]{1,0:T(8,128)} fusion(bf16[2048,1280]{1,0:T(8,128)(2,1)} %get-tuple-element.30, bf16[2048,1280]{1,0:T(8,128)(2,1)} %all-gather.18.cloned.1.call-done), kind=kOutput, calls=%fused_computation.168 | convolution fusion | flops 10737418240 | bytes 27262976 | tf_op jit(solution)/shard_map/dot_general | solution.py:18
  338.1 17.3 %add_convert_fusion = bf16[2048,2048]{1,0:T(8,128)(2,1)} fusion(f32[2048,2048]{1,0:T(8,128)} %fusion.43, bf16[2048,1280]{1,0:T(8,128)(2,1)} %get-tuple-element.31, bf16[2048,1280]{1,0:T(8,128)(2,1)S(1)} %copy-done.30), kind=kOutput, calls=%fused_computation.6 | convolution fusion | flops 10745806848 | bytes 35651584 | tf_op jit(solution)/shard_map/dot_general | solution.py:18
  366.4 17.2 %collective-permute-done.12 = bf16[384,256]{1,0:T(8,128)(2,1)S(1)} collective-permute-done((bf16[384,256]{1,0:T(8,128)(2,1)S(1)}, bf16[384,256]{1,0:T(8,128)(2,1)S(1)}, u32[]{:S(2)}, u32[]{:S(2)}) %collective-permute-start.12) | collective-permute-done | bytes 196640 | tf_op jit(solution)/shard_map/ppermute | solution.py:417
  384.6 16.7 %convolution_convert_fusion = bf16[2048,2048]{1,0:T(8,128)(2,1)} fusion(bf16[2048,1280]{1,0:T(8,128)(2,1)} %get-tuple-element.29, bf16[1280,2048]{1,0:T(8,128)(2,1)} %all-gather.16.cloned.1.call-done), kind=kOutput, calls=%fused_computation.17 | convolution fusion | flops 10741612544 | bytes 18874368 | tf_op jit(solution)/shard_map/dot_general | solution.py:21
  401.3 16.9 %fusion.7 = bf16[2048,1280]{0,1:T(8,128)(2,1)} fusion(bf16[2048,1280]{1,0:T(8,128)(2,1)} %get-tuple-element.29, bf16[1,2048,2048]{2,1,0:T(8,128)(2,1)} %param.13), kind=kOutput, calls=%fused_computation.21 | convolution fusion | flops 10740039680 | bytes 18874368 | tf_op jit(solution)/shard_map/dot_general | solution.py:24
  421.0 17.5 %convolution_convert_fusion.1 = bf16[2048,1280]{1,0:T(8,128)(2,1)} fusion(bf16[2048,2048]{1,0:T(8,128)(2,1)} %multiply_convert_fusion, bf16[2048,1280]{1,0:T(8,128)(2,1)} %get-tuple-element.31), kind=kOutput, calls=%fused_computation.18 | convolution fusion | flops 10740039680 | bytes 18874368 | tf_op jit(solution)/shard_map/dot_general | solution.py:24
  438.5 13.9 %convolution_convert_fusion.2 = bf16[2048,1280]{1,0:T(8,128)(2,1)} fusion(bf16[2048,2048]{1,0:T(8,128)(2,1)S(1)} %bitcast.256, bf16[2048,1280]{1,0:T(8,128)(2,1)S(1)} %bitcast.304), kind=kOutput, calls=%fused_computation.19 | convolution fusion | flops 10740039680 | bytes 18874368 | tf_op jit(solution)/shard_map/dot_general | solution.py:24
  452.4 57.4 %reduce-scatter.5.cloned.1.call-done = bf16[512,2048]{1,0:T(8,128)(2,1)} async-done(((bf16[2048,2048]{1,0:T(8,128)(2,1)}), bf16[512,2048]{1,0:T(8,128)(2,1)}) %reduce-scatter.5.cloned.1.call-update) | async-done | bytes 2097168 | tf_op jit(solution)/shard_map/reduce_scatter | solution.py:375
  551.7 40.4 %attend_grad.1 = (f32[256,2048]{1,0:T(8,128)}, bf16[4096,128]{1,0:T(8,128)(2,1)}) custom-call(s32[1]{0:T(128)} %bitcast.1.start_ref, s32[4096]{0:T(1024)} %bitcast.294, bf16[256,2048]{1,0:T(8,128)(2,1)} %get-tuple-element.24.q_ref, bf16[4096,128]{1,0:T(8,128)(2,1)} %pad_maximum_fusion.1.kv_ref, bf16[256,2048]{1,0:T(8,128)(2,1)} %get-tuple-element.26.o_ref, ...), custom_call_target="tpu_custom_call" | custom-call | flops 21474836480 | bytes 8388608 | tf_op jit(solution)/shard_map/attend_grad/pallas_call | solution.py:309
  593.1 36.6 %collective-permute-start.7 = (bf16[1,2048,128]{2,1,0:T(8,128)(2,1)S(1)}, bf16[1,2048,128]{2,1,0:T(8,128)(2,1)S(1)}, u32[]{:S(2)}, u32[]{:S(2)}) collective-permute-start(bf16[1,2048,128]{2,1,0:T(8,128)(2,1)S(1)} %dynamic-slice_bitcast_fusion.3), channel_id=1, source_target_pairs={{0,4},{4,0},{1,5},{5,1},{2,6},{6,2},{3,7},{7,3},{8,12},{12,8},{9,1... | collective-permute-start | bytes 1572872 | tf_op jit(solution)/shard_map/ppermute | solution.py:407
  655.8 20.7 %collective-permute-done.8 = bf16[384,512]{1,0:T(8,128)(2,1)S(1)} collective-permute-done((bf16[384,512]{1,0:T(8,128)(2,1)S(1)}, bf16[384,512]{1,0:T(8,128)(2,1)S(1)}, u32[]{:S(2)}, u32[]{:S(2)}) %collective-permute-start.8) | collective-permute-done | bytes 393248 | tf_op jit(solution)/shard_map/ppermute | solution.py:435
  678.5 10.5 collective-permute-start.9
  689.0 11.2 %convert_element_type.296 = f32[1,2048,2048]{2,1,0:T(8,128)} convert(bf16[1,2048,2048]{2,1,0:T(8,128)(2,1)} %param.12) | non-fusion elementwise | flops 4194304 | bytes 25165824 | tf_op jit(solution)/shard_map/convert_element_type | solution.py:479
  705.1 19.6 %collective-permute-done.9 = bf16[384,512]{1,0:T(8,128)(2,1)S(1)} collective-permute-done((bf16[384,512]{1,0:T(8,128)(2,1)S(1)}, bf16[384,512]{1,0:T(8,128)(2,1)S(1)}, u32[]{:S(2)}, u32[]{:S(2)}) %collective-permute-start.9) | collective-permute-done | bytes 393248 | tf_op jit(solution)/shard_map/ppermute | solution.py:435
  731.1 10.3 multiply_reduce_fusion.1
  788.1 22.2 %collective-permute-done.33 = bf16[1,2,256,1280]{2,3,1,0:T(8,128)(2,1)S(1)} collective-permute-done((bf16[1,2,256,1280]{2,3,1,0:T(8,128)(2,1)S(1)}, bf16[1,2,256,1280]{2,3,1,0:T(8,128)(2,1)S(1)}, u32[]{:S(2)}, u32[]{:S(2)}) %collective-permute-start.33) | collective-permute-done | bytes 1310752 | tf_op jit(solution)/shard_map/ppermute | solution.py:407
  813.1 25.3 %collective-permute-done.30 = bf16[1,2,256,1280]{3,2,1,0:T(8,128)(2,1)S(1)} collective-permute-done((bf16[1,2,256,1280]{3,2,1,0:T(8,128)(2,1)S(1)}, bf16[1,2,256,1280]{3,2,1,0:T(8,128)(2,1)S(1)}, u32[]{:S(2)}, u32[]{:S(2)}) %collective-permute-start.30) | collective-permute-done | bytes 1310752 | tf_op jit(solution)/shard_map/ppermute | solution.py:407
  841.1 24.6 %collective-permute-done.27 = bf16[1,2,256,1280]{3,2,1,0:T(8,128)(2,1)S(1)} collective-permute-done((bf16[1,2,256,1280]{3,2,1,0:T(8,128)(2,1)S(1)}, bf16[1,2,256,1280]{3,2,1,0:T(8,128)(2,1)S(1)}, u32[]{:S(2)}, u32[]{:S(2)}) %collective-permute-start.27) | collective-permute-done | bytes 1310752 | tf_op jit(solution)/shard_map/ppermute | solution.py:407
  895.4 29.5 %collective-permute-done.15 = bf16[1,2,256,400]{2,3,1,0:T(8,128)(2,1)S(1)} collective-permute-done((bf16[1,2,256,400]{2,3,1,0:T(8,128)(2,1)S(1)}, bf16[1,2,256,400]{2,3,1,0:T(8,128)(2,1)S(1)}, u32[]{:S(2)}, u32[]{:S(2)}) %collective-permute-start.15) | collective-permute-done | bytes 409632 | tf_op jit(solution)/shard_map/ppermute | solution.py:407
  933.1 10.6 collective-permute-start.23
  967.9 14.1 %collective-permute-done.21 = bf16[256,256]{0,1:T(8,128)(2,1)S(1)} collective-permute-done((bf16[256,256]{0,1:T(8,128)(2,1)S(1)}, bf16[256,256]{0,1:T(8,128)(2,1)S(1)}, u32[]{:S(2)}, u32[]{:S(2)}) %collective-permute-start.21) | collective-permute-done | bytes 131104 | tf_op jit(solution)/shard_map/ppermute | solution.py:435
  982.9 86.5 %all-gather.26.cloned.1.call-done = bf16[2048,2048]{1,0:T(8,128)(2,1)} async-done(((bf16[512,2048]{1,0:T(8,128)(2,1)}), bf16[2048,2048]{1,0:T(8,128)(2,1)}) %all-gather.26.cloned.1.call-update) | async-done | bytes 8388624 | tf_op jit(solution)/shard_map/all_gather | solution.py:371
  (299 shorter events, 292.7 us)
Async XLA Ops:
  7.2 32.4 %all-gather.10.cloned.1.call-start = ((), (), s32[]{:S(2)}) async-start(), calls=%async_computation.2 | async-start | bytes 1843200 | tf_op jit(solution)/shard_map/all_gather | solution.py:371
  10.6 85.0 %all-gather.16.cloned.1.call-start = ((), (), s32[]{:S(2)}) async-start(), calls=%async_computation.5 | async-start | bytes 5898240 | tf_op jit(solution)/shard_map/all_gather | solution.py:371
  11.3 115.8 %all-gather.14.cloned.1.call-start = ((), (), s32[]{:S(2)}) async-start(), calls=%async_computation.4 | async-start | bytes 4718592 | tf_op jit(solution)/shard_map/all_gather | solution.py:371
  26.7 182.6 %all-gather.12.cloned.1.call-start = ((), (), s32[]{:S(2)}) async-start(), calls=%async_computation.3 | async-start | bytes 5242880 | tf_op jit(solution)/shard_map/all_gather | solution.py:371
  53.9 18.0 %collective-permute-start = (bf16[2048,128]{1,0:T(8,128)(2,1)}, bf16[2048,128]{1,0:T(8,128)(2,1)S(1)}, u32[]{:S(2)}, u32[]{:S(2)}) collective-permute-start(bf16[2048,128]{1,0:T(8,128)(2,1)} %get-tuple-element.25), channel_id=1, source_target_pairs={{0,4},{4,0},{1,5},{5,1},{2,6},{6,2},{3,7},{7,3},{8,12},{12,8},{9,1... | collective-permute-start | bytes 1572872 | tf_op jit(solution)/shard_map/ppermute | solution.py:389
  94.1 156.6 %all-gather.20.cloned.1.call-start = ((), (), s32[]{:S(2)}) async-start(), calls=%async_computation.7 | async-start | bytes 5898240 | tf_op jit(solution)/shard_map/all_gather | solution.py:371
  94.7 198.9 %all-gather.18.cloned.1.call-start = ((), (), s32[]{:S(2)}) async-start(), calls=%async_computation.6 | async-start | bytes 5898240 | tf_op jit(solution)/shard_map/all_gather | solution.py:371
  95.3 414.5 %reduce-scatter.5.cloned.1.call-start = ((), (), s32[]{:S(2)}) async-start(), calls=%async_computation.10 | async-start | bytes 10485760 | tf_op jit(solution)/shard_map/reduce_scatter | solution.py:375
  355.4 375.7 %all-gather.24.cloned.1.call-start = ((), (), s32[]{:S(2)}) async-start(), calls=%async_computation.11 | async-start | bytes 7077888 | tf_op jit(solution)/shard_map/all_gather | solution.py:371
  357.8 25.8 %collective-permute-start.12 = (bf16[384,256]{1,0:T(8,128)(2,1)S(1)}, bf16[384,256]{1,0:T(8,128)(2,1)S(1)}, u32[]{:S(2)}, u32[]{:S(2)}) collective-permute-start(bf16[384,256]{1,0:T(8,128)(2,1)S(1)} %bitcast.277), channel_id=1, source_target_pairs={{0,2},{1,3},{2,0},{3,1},{4,6},{5,7},{6,4},{7,5},{8,10},{9,11},{10,... | collective-permute-start | bytes 589832 | tf_op jit(solution)/shard_map/ppermute | solution.py:417
  360.2 23.4 %collective-permute-start.13 = (bf16[384,256]{1,0:T(8,128)(2,1)S(1)}, bf16[384,256]{1,0:T(8,128)(2,1)S(1)}, u32[]{:S(2)}, u32[]{:S(2)}) collective-permute-start(bf16[384,256]{1,0:T(8,128)(2,1)S(1)} %bitcast.278), channel_id=1, source_target_pairs={{0,3},{1,0},{2,1},{3,2},{4,7},{5,4},{6,5},{7,6},{8,11},{9,8},{10,9... | collective-permute-start | bytes 589832 | tf_op jit(solution)/shard_map/ppermute | solution.py:417
  384.5 356.8 %reduce-scatter.3.cloned.1.call-start = ((), (), s32[]{:S(2)}) async-start(), calls=%async_computation.8 | async-start | bytes 10485760 | tf_op jit(solution)/shard_map/reduce_scatter | solution.py:375
  401.2 581.6 %all-gather.22.cloned.1.call-start = ((), (), s32[]{:S(2)}) async-start(), calls=%async_computation.9 | async-start | bytes 10485760 | tf_op jit(solution)/shard_map/all_gather | solution.py:371
  533.4 16.1 %collective-permute-start.5 = (bf16[256,512]{1,0:T(8,128)(2,1)}, bf16[256,512]{1,0:T(8,128)(2,1)}, u32[]{:S(2)}, u32[]{:S(2)}) collective-permute-start(bf16[256,512]{1,0:T(8,128)(2,1)} %get-tuple-element.97), channel_id=1, source_target_pairs={{0,2},{1,3},{2,0},{3,1},{4,6},{5,7},{6,4},{7,5},{8,10},{9,11},{10,... | collective-permute-start | bytes 786440 | tf_op jit(solution)/shard_map/ppermute | solution.py:435
  535.7 14.8 %collective-permute-start.6 = (bf16[256,512]{1,0:T(8,128)(2,1)}, bf16[256,512]{1,0:T(8,128)(2,1)S(1)}, u32[]{:S(2)}, u32[]{:S(2)}) collective-permute-start(bf16[256,512]{1,0:T(8,128)(2,1)} %get-tuple-element.96), channel_id=1, source_target_pairs={{0,3},{1,0},{2,1},{3,2},{4,7},{5,4},{6,5},{7,6},{8,11},{9,8},{10,9... | collective-permute-start | bytes 786440 | tf_op jit(solution)/shard_map/ppermute | solution.py:435
  593.1 45.3 %collective-permute-start.7 = (bf16[1,2048,128]{2,1,0:T(8,128)(2,1)S(1)}, bf16[1,2048,128]{2,1,0:T(8,128)(2,1)S(1)}, u32[]{:S(2)}, u32[]{:S(2)}) collective-permute-start(bf16[1,2048,128]{2,1,0:T(8,128)(2,1)S(1)} %dynamic-slice_bitcast_fusion.3), channel_id=1, source_target_pairs={{0,4},{4,0},{1,5},{5,1},{2,6},{6,2},{3,7},{7,3},{8,12},{12,8},{9,1... | collective-permute-start | bytes 1572872 | tf_op jit(solution)/shard_map/ppermute | solution.py:407
  649.8 26.8 %collective-permute-start.8 = (bf16[384,512]{1,0:T(8,128)(2,1)S(1)}, bf16[384,512]{1,0:T(8,128)(2,1)S(1)}, u32[]{:S(2)}, u32[]{:S(2)}) collective-permute-start(bf16[384,512]{1,0:T(8,128)(2,1)S(1)} %dynamic-slice_bitcast_fusion.6), channel_id=1, source_target_pairs={{0,1},{1,2},{2,3},{3,0},{4,5},{5,6},{6,7},{7,4},{8,9},{9,10},{10,1... | collective-permute-start | bytes 1179656 | tf_op jit(solution)/shard_map/ppermute | solution.py:435
  678.5 46.2 %collective-permute-start.9 = (bf16[384,512]{1,0:T(8,128)(2,1)S(1)}, bf16[384,512]{1,0:T(8,128)(2,1)S(1)}, u32[]{:S(2)}, u32[]{:S(2)}) collective-permute-start(bf16[384,512]{1,0:T(8,128)(2,1)S(1)} %get-tuple-element.86), channel_id=1, source_target_pairs={{0,2},{1,3},{2,0},{3,1},{4,6},{5,7},{6,4},{7,5},{8,10},{9,11},{10,... | collective-permute-start | bytes 1179656 | tf_op jit(solution)/shard_map/ppermute | solution.py:435
  702.8 27.5 %collective-permute-start.10 = (bf16[384,512]{1,0:T(8,128)(2,1)S(1)}, bf16[384,512]{1,0:T(8,128)(2,1)S(1)}, u32[]{:S(2)}, u32[]{:S(2)}) collective-permute-start(bf16[384,512]{1,0:T(8,128)(2,1)S(1)} %get-tuple-element.85), channel_id=1, source_target_pairs={{0,3},{1,0},{2,1},{3,2},{4,7},{5,4},{6,5},{7,6},{8,11},{9,8},{10,9... | collective-permute-start | bytes 1179656 | tf_op jit(solution)/shard_map/ppermute | solution.py:435
  750.1 319.3 %all-gather.26.cloned.1.call-start = ((), (), s32[]{:S(2)}) async-start(), calls=%async_computation.12 | async-start | bytes 10485760 | tf_op jit(solution)/shard_map/all_gather | solution.py:371
  778.6 31.7 %collective-permute-start.33 = (bf16[1,2,256,1280]{2,3,1,0:T(8,128)(2,1)S(1)}, bf16[1,2,256,1280]{2,3,1,0:T(8,128)(2,1)S(1)}, u32[]{:S(2)}, u32[]{:S(2)}) collective-permute-start(bf16[1,2,256,1280]{2,3,1,0:T(8,128)(2,1)S(1)} %constant_dynamic-slice_fusion.1), channel_id=1, source_target_pairs={{0,16},{8,24},{16,0},{24,8},{1,17},{9,25},{17,1},{25,9},{2,18},{10... | collective-permute-start | bytes 3932168 | tf_op jit(solution)/shard_map/ppermute | solution.py:407
  783.3 55.1 %collective-permute-start.30 = (bf16[1,2,256,1280]{3,2,1,0:T(8,128)(2,1)S(1)}, bf16[1,2,256,1280]{3,2,1,0:T(8,128)(2,1)S(1)}, u32[]{:S(2)}, u32[]{:S(2)}) collective-permute-start(bf16[1,2,256,1280]{3,2,1,0:T(8,128)(2,1)S(1)} %constant_dynamic-slice_fusion.5), channel_id=1, source_target_pairs={{0,16},{8,24},{16,0},{24,8},{1,17},{9,25},{17,1},{25,9},{2,18},{10... | collective-permute-start | bytes 3932168 | tf_op jit(solution)/shard_map/ppermute | solution.py:407
  787.1 78.6 %collective-permute-start.27 = (bf16[1,2,256,1280]{3,2,1,0:T(8,128)(2,1)S(1)}, bf16[1,2,256,1280]{3,2,1,0:T(8,128)(2,1)S(1)}, u32[]{:S(2)}, u32[]{:S(2)}) collective-permute-start(bf16[1,2,256,1280]{3,2,1,0:T(8,128)(2,1)S(1)} %constant_dynamic-slice_fusion.7), channel_id=1, source_target_pairs={{0,16},{8,24},{16,0},{24,8},{1,17},{9,25},{17,1},{25,9},{2,18},{10... | collective-permute-start | bytes 3932168 | tf_op jit(solution)/shard_map/ppermute | solution.py:407
  811.7 74.0 %collective-permute-start.34 = (bf16[1,1,256,1280]{2,3,1,0:T(8,128)(2,1)}, bf16[1,1,256,1280]{2,3,1,0:T(8,128)(2,1)}, u32[]{:S(2)}, u32[]{:S(2)}) collective-permute-start(bf16[1,1,256,1280]{2,3,1,0:T(8,128)(2,1)} %constant_dynamic-slice_fusion), channel_id=1, source_target_pairs={{0,4},{4,0},{1,5},{5,1},{2,6},{6,2},{3,7},{7,3},{8,12},{12,8},{9,1... | collective-permute-start | bytes 1966088 | tf_op jit(solution)/shard_map/ppermute | solution.py:407
  839.7 53.3 %collective-permute-start.31 = (bf16[1,1,256,1280]{3,2,1,0:T(8,128)(2,1)}, bf16[1,1,256,1280]{3,2,1,0:T(8,128)(2,1)}, u32[]{:S(2)}, u32[]{:S(2)}) collective-permute-start(bf16[1,1,256,1280]{3,2,1,0:T(8,128)(2,1)} %constant_dynamic-slice_fusion.4), channel_id=1, source_target_pairs={{0,4},{4,0},{1,5},{5,1},{2,6},{6,2},{3,7},{7,3},{8,12},{12,8},{9,1... | collective-permute-start | bytes 1966088 | tf_op jit(solution)/shard_map/ppermute | solution.py:407
  868.1 59.5 %collective-permute-start.28 = (bf16[1,1,256,1280]{3,2,1,0:T(8,128)(2,1)}, bf16[1,1,256,1280]{3,2,1,0:T(8,128)(2,1)}, u32[]{:S(2)}, u32[]{:S(2)}) collective-permute-start(bf16[1,1,256,1280]{3,2,1,0:T(8,128)(2,1)} %constant_dynamic-slice_fusion.6), channel_id=1, source_target_pairs={{0,4},{4,0},{1,5},{5,1},{2,6},{6,2},{3,7},{7,3},{8,12},{12,8},{9,1... | collective-permute-start | bytes 1966088 | tf_op jit(solution)/shard_map/ppermute | solution.py:407
  890.7 35.0 %collective-permute-start.18 = (bf16[1,2,256,1024]{3,2,1,0:T(8,128)(2,1)S(1)}, bf16[1,2,256,1024]{3,2,1,0:T(8,128)(2,1)S(1)}, u32[]{:S(2)}, u32[]{:S(2)}) collective-permute-start(bf16[1,2,256,1024]{3,2,1,0:T(8,128)(2,1)S(1)} %constant_dynamic-slice_fusion.9), channel_id=1, source_target_pairs={{0,16},{8,24},{16,0},{24,8},{1,17},{9,25},{17,1},{25,9},{2,18},{10... | collective-permute-start | bytes 3145736 | tf_op jit(solution)/shard_map/ppermute | solution.py:407
  892.4 32.5 %collective-permute-start.15 = (bf16[1,2,256,400]{2,3,1,0:T(8,128)(2,1)S(1)}, bf16[1,2,256,400]{2,3,1,0:T(8,128)(2,1)S(1)}, u32[]{:S(2)}, u32[]{:S(2)}) collective-permute-start(bf16[1,2,256,400]{2,3,1,0:T(8,128)(2,1)S(1)} %constant_dynamic-slice_fusion.11), channel_id=1, source_target_pairs={{0,16},{8,24},{16,0},{24,8},{1,17},{9,25},{17,1},{25,9},{2,18},{10... | collective-permute-start | bytes 1228808 | tf_op jit(solution)/shard_map/ppermute | solution.py:407
  926.1 21.0 %collective-permute-start.19 = (bf16[1,1,256,1024]{3,2,1,0:T(8,128)(2,1)S(1)}, bf16[1,1,256,1024]{3,2,1,0:T(8,128)(2,1)S(1)}, u32[]{:S(2)}, u32[]{:S(2)}) collective-permute-start(bf16[1,1,256,1024]{3,2,1,0:T(8,128)(2,1)S(1)} %constant_dynamic-slice_fusion.8), channel_id=1, source_target_pairs={{0,4},{4,0},{1,5},{5,1},{2,6},{6,2},{3,7},{7,3},{8,12},{12,8},{9,1... | collective-permute-start | bytes 1572872 | tf_op jit(solution)/shard_map/ppermute | solution.py:407
  933.1 20.7 %collective-permute-start.23 = (f32[16,256]{1,0:T(8,128)S(1)}, f32[16,256]{1,0:T(8,128)S(1)}, u32[]{:S(2)}, u32[]{:S(2)}) collective-permute-start(f32[16,256]{1,0:T(8,128)S(1)} %slice_bitcast_fusion.12), channel_id=1, source_target_pairs={{0,1},{1,2},{2,3},{3,0},{4,5},{5,6},{6,7},{7,4},{8,9},{9,10},{10,1... | collective-permute-start | bytes 49160 | tf_op jit(solution)/shard_map/ppermute | solution.py:426
  960.2 21.7 %collective-permute-start.21 = (bf16[256,256]{0,1:T(8,128)(2,1)S(1)}, bf16[256,256]{0,1:T(8,128)(2,1)S(1)}, u32[]{:S(2)}, u32[]{:S(2)}) collective-permute-start(bf16[256,256]{0,1:T(8,128)(2,1)S(1)} %get-tuple-element.102), channel_id=1, source_target_pairs={{0,2},{1,3},{2,0},{3,1},{4,6},{5,7},{6,4},{7,5},{8,10},{9,11},{10,... | collective-permute-start | bytes 393224 | tf_op jit(solution)/shard_map/ppermute | solution.py:435
  967.4 14.5 %collective-permute-start.22 = (bf16[256,256]{0,1:T(8,128)(2,1)S(1)}, bf16[256,256]{0,1:T(8,128)(2,1)S(1)}, u32[]{:S(2)}, u32[]{:S(2)}) collective-permute-start(bf16[256,256]{0,1:T(8,128)(2,1)S(1)} %get-tuple-element.101), channel_id=1, source_target_pairs={{0,3},{1,0},{2,1},{3,2},{4,7},{5,4},{6,5},{7,6},{8,11},{9,8},{10,9... | collective-permute-start | bytes 393224 | tf_op jit(solution)/shard_map/ppermute | solution.py:435
  (58 other events, 886.1 us)
Sparse Core Ops, SparseCore 0:
  10.7 28.8 all-gather.9
  41.4 45.7 all-gather.15
  89.7 37.4 all-gather.13
  128.6 80.7 all-gather.11
  211.1 39.6 all-gather.19
  252.5 41.1 all-gather.17
  355.5 154.2 reduce-scatter.4
  511.6 48.1 all-gather.23
  562.2 169.4 reduce-scatter.2
  750.2 157.1 all-gather.21
  909.0 160.4 all-gather.25

commit v3 on v2

--- a/solution.py
+++ b/solution.py
@@ -22,6 +22,10 @@
 
 def dot_tn(a, b):
     return lax.dot_general(a, b, (((0,), (0,)), ((), ())), preferred_element_type=f32)
+
+
+def dot_tt(a, b):
+    return lax.dot_general(a, b, (((0,), (1,)), ((), ())), preferred_element_type=f32)
 
 
 def head_norm(x):
@@ -185,25 +189,26 @@
         l_ref[h : h + 1, :] = jnp.log2(total)
 
 
-def attention(start, seg, q, kv, qpos, qseg, kpos, kseg, bq, bk):
+def attention(start, seg, q, kv, qpos, qseg, kpos, kseg, bq, bk, part, parts):
     heads = q.shape[0] // HEAD_DIM
-    count, total = q.shape[1], kv.shape[0]
+    count, total = q.shape[1] // parts, kv.shape[0]
     bq, bk = min(bq, count), min(bk, total)
+    first = part * (count // bq)
     whole = lambda *shape: pl.BlockSpec(shape, lambda i, *_: (0,) * len(shape))
     return pl.pallas_call(
         functools.partial(fwd_kernel, heads, bq, bk),
         out_shape=(
-            jax.ShapeDtypeStruct(q.shape, bf16),
+            jax.ShapeDtypeStruct((q.shape[0], count), bf16),
             jax.ShapeDtypeStruct((heads, count), f32),
         ),
         grid_spec=pltpu.PrefetchScalarGridSpec(
             num_scalar_prefetch=2,
             grid=(count // bq,),
             in_specs=[
-                pl.BlockSpec((q.shape[0], bq), lambda i, *_: (0, i)),
+                pl.BlockSpec((q.shape[0], bq), lambda i, *_: (0, i + first)),
                 whole(*kv.shape),
-                pl.BlockSpec((bq, 1), lambda i, *_: (i, 0)),
-                pl.BlockSpec((bq, 1), lambda i, *_: (i, 0)),
+                pl.BlockSpec((bq, 1), lambda i, *_: (i + first, 0)),
+                pl.BlockSpec((bq, 1), lambda i, *_: (i + first, 0)),
                 whole(total // bk, 1, bk),
                 whole(total // bk, 1, bk),
             ],
@@ -249,10 +254,11 @@
         return jnp.where(row == 0, a, jnp.where(row == 1, b, jnp.where(row == 2, c, 0.0)))
 
     zeros = jnp.zeros((D, bq), f32)
+    do_all = do_ref[...].astype(f32).T
     for h in range(heads):
         part = slice(h * D, (h + 1) * D)
         wide = slice(h * 2 * D, (h + 1) * 2 * D)
-        q, do, o = q_ref[part, :].astype(f32), do_ref[part, :].astype(f32), o_ref[part, :].astype(f32)
+        q, do, o = q_ref[part, :].astype(f32), do_all[part, :], o_ref[part, :].astype(f32)
         delta = jnp.sum(do * o, axis=0, keepdims=True)
         qst[wide, :] = jnp.concatenate([q, extra(l_ref[h : h + 1, :])], axis=0).astype(bf16)
         dst[wide, :] = jnp.concatenate([extra(delta), do], axis=0).astype(bf16)
@@ -319,7 +325,7 @@
                 wide,
                 whole(*kv.shape),
                 wide,
-                wide,
+                pl.BlockSpec((bq, q.shape[0]), lambda i, *_: (i, 0)),
                 pl.BlockSpec((heads, bq), lambda i, *_: (0, i)),
                 pl.BlockSpec((1, bq), lambda i, *_: (0, i)),
                 pl.BlockSpec((1, bq), lambda i, *_: (0, i)),
@@ -350,6 +356,7 @@
 EVERY = ("dp", "context", "tensor")
 QUERY_BLOCK = 512
 KEY_BLOCK = 512
+CHUNKS = 2
 
 
 def unit_rows(values):
@@ -437,6 +444,91 @@
     return out
 
 
+def gather_kernel(count, *refs):
+    sources, targets = refs[:count], refs[count : 2 * count]
+    own_sem, send_sem, recv_sem = refs[2 * count :]
+    dp, context = lax.axis_index("dp"), lax.axis_index("context")
+    outer, inner = dp // 2, dp % 2
+    across, along, beside = (
+        {"dp": dp + 2 - 4 * outer},
+        {"context": 1 - context},
+        {"dp": dp + 1 - 2 * inner},
+    )
+    barrier = pltpu.get_barrier_semaphore()
+    for device in (across, along, beside):
+        pl.semaphore_signal(barrier, inc=1, device_id=device, device_id_type=pl.DeviceIdType.MESH)
+    pl.semaphore_wait(barrier, 3)
+
+    def place(array, o, k, first=0, parts=1):
+        rows = sources[array].shape[0]
+        start = ((2 * o + inner) * 2 + k) * rows + first * (rows // parts)
+        return targets[array].at[pl.ds(pl.multiple_of(start, rows // parts), rows // parts), :]
+
+    def send(array, kind, source, target, device):
+        copy = pltpu.make_async_remote_copy(
+            src_ref=source,
+            dst_ref=target,
+            send_sem=send_sem.at[array, kind],
+            recv_sem=recv_sem.at[array, kind],
+            device_id=device,
+            device_id_type=pl.DeviceIdType.MESH,
+        )
+        copy.start()
+        return copy
+
+    copies, kept = {}, []
+    for a in range(count):
+        mine = place(a, outer, context)
+        copies[a, 0] = send(a, 0, sources[a], mine, across)
+        copies[a, 1] = send(a, 1, sources[a], mine, along)
+        copies[a, 2] = send(a, 2, sources[a], mine, beside)
+        keep = pltpu.make_async_copy(sources[a], mine, own_sem.at[a])
+        keep.start()
+        kept.append(keep)
+    for a in range(count):
+        copies[a, 0].wait_recv()
+        got = place(a, 1 - outer, context)
+        half = place(a, 1 - outer, context, 0, 2)
+        copies[a, 3] = send(a, 3, half, half, along)
+        copies[a, 4] = send(a, 4, got, got, beside)
+        copies[a, 1].wait_recv()
+        got = place(a, outer, 1 - context)
+        half = place(a, outer, 1 - context, 1, 2)
+        copies[a, 5] = send(a, 5, half, half, across)
+        copies[a, 6] = send(a, 6, got, got, beside)
+    for a in range(count):
+        for kind, first in ((3, 0), (5, 1)):
+            copies[a, kind].wait_recv()
+            half = place(a, 1 - outer, 1 - context, first, 2)
+            copies[a, 7 + first] = send(a, 7 + first, half, half, beside)
+    for a in range(count):
+        kept[a].wait()
+        for kind in (2, 4, 6, 7, 8):
+            copies[a, kind].wait_recv()
+    for copy in copies.values():
+        copy.wait_send()
+
+
+def plane_gather(parts, collective):
+    share = lax.axis_size("dp") * lax.axis_size("context")
+    if (lax.axis_size("dp"), lax.axis_size("context")) != (4, 2):
+        return [gathered(part, SHARE, 0) for part in parts]
+    count = len(parts)
+    return pl.pallas_call(
+        functools.partial(gather_kernel, count),
+        out_shape=tuple(jax.ShapeDtypeStruct((share * part.shape[0],) + part.shape[1:], part.dtype) for part in parts),
+        in_specs=[pl.BlockSpec(memory_space=pltpu.VMEM)] * count,
+        out_specs=(pl.BlockSpec(memory_space=pl.ANY),) * count,
+        scratch_shapes=[
+            pltpu.SemaphoreType.DMA((count,)),
+            pltpu.SemaphoreType.DMA((count, 9)),
+            pltpu.SemaphoreType.DMA((count, 9)),
+        ],
+        compiler_params=pltpu.CompilerParams(collective_id=collective, has_side_effects=True),
+        name="plane_gather",
+    )(*parts)
+
+
 def rope_tables(positions):
     half = HEAD_DIM // 2
     inverse = jnp.exp(-math.log(rope_base) * jnp.arange(half, dtype=f32) * 2.0 / HEAD_DIM)
@@ -456,80 +548,117 @@
     my_seg = lax.dynamic_slice_in_dim(group_seg, first_row, rows, 0)
     my_pos = lax.dynamic_slice_in_dim(group_pos, first_row, rows, 0)
     start = jnp.reshape(first_row, (1,)).astype(jnp.int32)
-    part_rows = rows // ways
-
-    def own_rows(values):
-        return lax.dynamic_slice_in_dim(values, mine * part_rows, part_rows, 0)
-
     columns = w_qkv.shape[1]
     qkv_shard = w_qkv.T
     packed = jnp.concatenate(
         [qkv_shard, attn_gain[None], ffn_gain[None], jnp.zeros((14, w_qkv.shape[0]), bf16)], axis=0
     )
-    packed_all = gathered(packed, SHARE, 1)
+    packed_all, gate_all, up_all = plane_gather([packed.T, w_gate, w_up], 0)
+    packed_all = packed_all.T
     qkv_mine = packed_all[:columns]
     attn_gain_all = packed_all[columns].astype(f32)
     ffn_gain_all = packed_all[columns + 1].astype(f32)
-    out_all = gathered(spread(w_out).reshape(ways * w_out.shape[0], -1), SHARE, 1)
-    gate_all = gathered(w_gate, SHARE, 0)
-    up_all = gathered(w_up, SHARE, 0)
-    down_all = gathered(w_down, SHARE, 1)
-    qkv_all = gathered(spread(qkv_shard).reshape(ways * columns, -1), SHARE, 1)
-
-    inputs = layer_input.reshape(rows, width).astype(f32)
+    out_t = jnp.concatenate(list(spread(w_out.T)), axis=1)
+    qkv_t = jnp.concatenate(list(spread(after(w_qkv, gate_all))), axis=1)
+    down_all = gathered(after(w_down.T, gate_all), SHARE, 0)
+    out_all = gathered(after(out_t, gate_all), SHARE, 0)
+
+    tokens_in = layer_input.reshape(rows, width)
     cot = cotangent.reshape(rows, width)
-    normed_low = (unit_rows(inputs)[0] * attn_gain_all).astype(bf16)
+    normed_low = (unit_rows(tokens_in.astype(f32))[0] * attn_gain_all).astype(bf16)
     joint = dot_nt(qkv_mine, normed_low)
     cos, sin = rope_tables(my_pos)
     gains = qk_gain.T
     queries, kv_mine = prep(joint, cos, sin, gains, heads, 512)
     kv = both_halves(kv_mine)
-    places = (my_pos, my_seg, group_pos, group_seg)
-    attended, log_total = attention(start, group_seg, queries, kv, *places, QUERY_BLOCK, KEY_BLOCK)
-    attended_all = gathered(attended, "tensor", 0)
-    act_grad = dot_nt(after(cot, attended), down_all)
-    resid = inputs + natural(dot_tn(attended_all, out_all))
-
-    normed_ffn = (unit_rows(resid)[0] * ffn_gain_all).astype(bf16)
-    gate = dot_nn(after(normed_ffn, act_grad), gate_all)
-    up = dot_nn(normed_ffn, up_all)
-    act, silu_pull = jax.vjp(mixed_silu, gate, up)
-    act = act.astype(bf16)
-    gate_grad, up_grad = (g.astype(bf16) for g in silu_pull(act_grad))
-    ffn_in_part = (dot_nt(gate_grad, gate_all) + dot_nt(up_grad, up_all)).astype(bf16)
-    ffn_in_grad = scattered(ffn_in_part, "tensor", 0).astype(f32)
-    act, gate_grad, up_grad, _ = lax.optimization_barrier((act, gate_grad, up_grad, ffn_in_part))
-    ffn_part = dot_nn(act, down_all).astype(bf16)
+    chunk_rows = rows // CHUNKS
+    part_rows = chunk_rows // ways
+    chunks = [slice(c * chunk_rows, (c + 1) * chunk_rows) for c in range(CHUNKS)]
+
+    def own_rows(values, c):
+        return lax.dynamic_slice_in_dim(values, c * chunk_rows + mine * part_rows, part_rows, 0)
+
+    keys = (group_pos, group_seg)
+    attended, log_total, attended_all = [], [], []
+    for c in range(CHUNKS):
+        arrived = (down_all,) if c == 0 else (out_all,)
+        result, total = attention(
+            start + c * chunk_rows, group_seg, after(queries, *arrived), kv, my_pos, my_seg, *keys, QUERY_BLOCK, KEY_BLOCK, c, CHUNKS
+        )
+        attended.append(result)
+        log_total.append(total)
+        attended_all.append(gathered(result, "tensor", 0))
+
+    resid_parts, normed_ffns, acts, gate_grads, up_grads, ffn_in_grads = [], [], [], [], [], []
+    previous = attended[-1]
+    for c, chunk in enumerate(chunks):
+        act_grad = dot_nn(after(cot[chunk], previous), down_all)
+        resid = tokens_in[chunk].astype(f32) + natural(dot_tt(after(attended_all[c], act_grad), out_all))
+        normed_ffn = (unit_rows(resid)[0] * ffn_gain_all).astype(bf16)
+        gate, up = dot_nn(normed_ffn, gate_all), dot_nn(normed_ffn, up_all)
+        act, silu_pull = jax.vjp(mixed_silu, gate, up)
+        gate_grad, up_grad = (g.astype(bf16) for g in silu_pull(act_grad))
+        previous = (dot_nt(gate_grad, gate_all) + dot_nt(up_grad, up_all)).astype(bf16)
+        ffn_in_grads.append(scattered(previous, "tensor", 0).astype(f32))
+        resid_parts.append(own_rows(resid, 0))
+        normed_ffns.append(normed_ffn)
+        acts.append(act.astype(bf16))
+        gate_grads.append(gate_grad)
+        up_grads.append(up_grad)
+    normed_ffn, act, gate_grad, up_grad = (
+        jnp.concatenate(pieces, axis=0) for pieces in (normed_ffns, acts, gate_grads, up_grads)
+    )
+    act, gate_grad, up_grad, _ = lax.optimization_barrier((act, gate_grad, up_grad, previous))
+    ffn_part = dot_nt(act, down_all).astype(bf16)
     grad_down = dot_tn(cot, act).astype(bf16)
     grad_gate = dot_tn(normed_ffn, gate_grad).astype(bf16)
     grad_up = dot_tn(normed_ffn, up_grad).astype(bf16)
-    resid_part = own_rows(resid)
-    norm_grad, ffn_gain_part = norm_back(ffn_in_grad, resid_part, ffn_gain_all)
-    resid_grad = own_rows(cot).astype(f32) + norm_grad
-    branch = after(resid_grad.astype(bf16), ffn_part, grad_down, grad_gate, grad_up)
-
-    attended_grad = dot_nt(out_all, branch).astype(bf16)
-    attended_grad = swap(attended_grad.reshape(ways, heads * HEAD_DIM, part_rows))
-    attended_grad = jnp.concatenate([attended_grad[i] for i in range(ways)], axis=1)
-    ffn_sum = scattered(ffn_part, "tensor", 0).astype(f32)
-    layer_output = gathered((resid_part + ffn_sum).astype(bf16), "tensor", 0)
-    attended_part = lax.dynamic_slice_in_dim(attended_all, mine * part_rows, part_rows, 1)
+    (qkv_all,) = plane_gather([after(qkv_t, ffn_part, grad_down, grad_gate, grad_up)], 1)
+    ffn_gain_part, resid_grads, attended_grads, attended_parts, branches = 0.0, [], [], [], []
+    for c in range(CHUNKS):
+        norm_grad, gain_part = norm_back(ffn_in_grads[c], resid_parts[c], ffn_gain_all)
+        ffn_gain_part += gain_part
+        resid_grad = own_rows(cot, c).astype(f32) + norm_grad
+        branch = resid_grad.astype(bf16)
+        resid_grads.append(resid_grad)
+        branches.append(branch)
+        attended_grad = dot_nn(branch, out_all).astype(bf16)
+        attended_grad = swap(jnp.stack(jnp.split(attended_grad, ways, axis=1)))
+        attended_grads.append(attended_grad.reshape(chunk_rows, -1))
+        attended_parts.append(lax.dynamic_slice_in_dim(attended_all[c], mine * part_rows, part_rows, 1))
+
+    attended_grad = jnp.concatenate(attended_grads, axis=0)
+    attended_grad = after(attended_grad, qkv_all)
+    branch, attended_part = jnp.concatenate(branches, axis=0), jnp.concatenate(attended_parts, axis=1)
     grad_out = lax.dot_general(branch, attended_part, (((0,), (1,)), ((), ())), preferred_element_type=f32)
     grad_out = halving_scatter(grad_out.astype(bf16), SHARE)
     grad_out = swap(jnp.stack([part.T for part in jnp.split(grad_out, ways, axis=1)]))
     query_grad, kv_grad_group = attention_grad(
-        start, group_seg, queries, kv, attended, attended_grad, log_total, *places, QUERY_BLOCK, KEY_BLOCK
+        start, group_seg, queries, kv, jnp.concatenate(attended, axis=1), attended_grad, jnp.concatenate(log_total, axis=1),
+        my_pos, my_seg, *keys, QUERY_BLOCK, KEY_BLOCK
     )
     kv_grad = halving_scatter(kv_grad_group, ("context",))
+    ffn_part = after(ffn_part, attended_grad)
+    ffn_sums = [scattered(ffn_part[chunk], "tensor", 0).astype(f32) for chunk in chunks]
     joint_grad, qk_part = unprep(joint, cos, sin, gains, query_grad, kv_grad, heads, 512)
-    joint_grad_part = swap(jnp.stack([joint_grad[:, i * part_rows : (i + 1) * part_rows] for i in range(ways)]))
-    in_grad = natural(dot_tn(joint_grad_part.reshape(ways * columns, part_rows), qkv_all))
+    tokens = joint_grad.reshape(columns, CHUNKS, ways, part_rows)
+    joint_grad_part = swap(jnp.stack([tokens[:, :, i].reshape(columns, -1) for i in range(ways)]))
+    in_grad = natural(dot_tt(joint_grad_part.reshape(ways * columns, -1), qkv_all))
     grad_qkv = dot_nn(joint_grad, normed_low)
     attn_gain_part = jnp.sum(qkv_mine.astype(f32) * grad_qkv, axis=0) / attn_gain_all
-    norm_grad = norm_back(in_grad, own_rows(inputs), attn_gain_all)[0]
-    grad_input = gathered((resid_grad + norm_grad).astype(bf16), "tensor", 0)
-
-    share = attn_gain.shape[0]
+    own_inputs = jnp.concatenate([own_rows(tokens_in, c) for c in range(CHUNKS)], axis=0).astype(f32)
+    norm_grad = norm_back(in_grad, own_inputs, attn_gain_all)[0]
+    grad_input = (jnp.concatenate(resid_grads, axis=0) + norm_grad).astype(bf16)
+    layer_output = [
+        (after(part, query_grad) + ffn_sum).astype(bf16) for part, ffn_sum in zip(resid_parts, ffn_sums, strict=True)
+    ]
+
+    def all_rows(parts):
+        return gathered(jnp.stack(parts), "tensor", 1).reshape(layer_input.shape)
+
+    layer_output = all_rows([after(part, grad_input) for part in layer_output])
+    grad_input = all_rows(jnp.split(grad_input, CHUNKS, axis=0))
+
     qk_rows = jnp.tile(qk_part.T, (1, width // HEAD_DIM))
     grad_qkv = jnp.concatenate(
         [grad_qkv, attn_gain_part[None], ffn_gain_part[None], qk_rows, jnp.zeros((12, width), f32)], axis=0
@@ -537,8 +666,8 @@
     grad_qkv = halving_scatter(grad_qkv.astype(bf16).T, SHARE).astype(f32)
     small = line_total(grad_qkv[:, columns:].T)
     return (
-        layer_output.reshape(layer_input.shape),
-        grad_input.reshape(layer_input.shape),
+        layer_output,
+        grad_input,
         grad_qkv[:, :columns],
         jnp.sum(grad_out.astype(f32), axis=0),
         small[0],

time: 1100 us -> 1030 us (0.936)
  waiting for transfers between devices: 525 us -> 317 us
  Pallas kernels: 70.2 us -> 167 us
  local copies, waits for them, and re-layouts: 85.3 us -> 121 us
  starting transfers between devices: 119 us -> 96.1 us
  matrix products: 204 us -> 216 us
    all_gather x9 -> x6, waiting for transfers between devices: 230 us -> 104 us  [gathered(): return lax.all_gather(part, axes, axis=axis, tiled=True)]
    pallas_call x0 -> x2, Pallas kernels: none -> 93.3 us  [plane_gather(): pl.pallas_call(functools.partial(gather_kernel, count), out_shape=tuple((...]
    reduce_scatter x2 -> x4, waiting for transfers between devices: 57.4 us -> 0.06 us  [scattered(): lax.psum_scatter(part.astype(bf16), axes, scatter_dimension=axis, tiled=T...]
    dot_general x5 -> x3, matrix products: 73.4 us -> 44 us  [dot_tn(): lax.dot_general(a, b, (((0,), (0,)), ((), ())), preferred_element_type=f32)]
    dot_general x0 -> x3, matrix products: none -> 26.9 us  [dot_tt(): lax.dot_general(a, b, (((0,), (1,)), ((), ())), preferred_element_type=f32)]
    slice x0 -> x3, local copies, waits for them, and re-layouts: none -> 17 us  [the longest x1 6.94 us: body(): tokens[:, :, i].reshape(columns, -1)]
    ppermute x6, waiting for transfers between devices: 28.3 us -> 11.7 us  [spread(): lax.ppermute(part, 'tensor', [(i, (i + step) % ways) for i in range(ways)])]
    ppermute x9 -> x12, starting transfers between devices: 41.8 us -> 26.4 us  [swap(): lax.ppermute(sent, 'tensor', [(i, (i + step) % ways) for i in range(ways)])]
  transfers between devices with their start and end apart: 46 -> 48, of which waited for: 26 -> 25; matrix products, arithmetic and copies ran while one was open for 24% -> 37% of each run, Pallas kernels for 6% -> 11%
where the time goes in v3:
time: 1030 us; the launch traced here: 1010 us
  waiting for transfers between devices  317 us (31%)
  matrix products  216 us (21%)
  Pallas kernels  167 us (16%)
  local copies, waits for them, and re-layouts  121 us (12%)
  starting transfers between devices  96.1 us (9%)
  other arithmetic  80.5 us (8%)
  between operations  16 us (2%)
    ppermute x16, waiting for transfers between devices, halving_scatter(): got = lax.ppermute(sent, axis, [(i, i ^ stride) for i in range(size)])  114 us
    all_gather x6, waiting for transfers between devices, gathered(): return lax.all_gather(part, axes, axis=axis, tiled=True)  104 us
    pallas_call x2, Pallas kernels, plane_gather(): pl.pallas_call(functools.partial(gather_kernel, count), out_shape=tuple((...  93.3 us
    dot_general x9, matrix products, dot_nn(): lax.dot_general(a, b, (((1,), (0,)), ((), ())), preferred_element_type=f32)  77.8 us
    ppermute x12, waiting for transfers between devices, swap(): lax.ppermute(sent, 'tensor', [(i, (i + step) % ways) for i in range(ways)])  75.3 us
    dot_general x6, matrix products, dot_nt(): lax.dot_general(a, b, (((1,), (1,)), ((), ())), preferred_element_type=f32)  65 us
    ppermute x16, starting transfers between devices, halving_scatter(): got = lax.ppermute(sent, axis, [(i, i ^ stride) for i in range(size)])  50.9 us
    dot_general x3, matrix products, dot_tn(): lax.dot_general(a, b, (((0,), (0,)), ((), ())), preferred_element_type=f32)  44 us
  transfers between devices with their start and end apart: 48, of which 25 were waited for; matrix products, arithmetic and copies ran while one was open for 37% of the time, Pallas kernels for 11%

profile of v3, /device:TPU:0, one launch (start us, length us, event | category | flops | bytes accessed | tf_op | source)
XLA Modules:
  0.0 1014.4 jit_solution(10055363606815229685)
XLA Ops:
  10.6 59.5 %plane_gather.2 = (bf16[2048,400]{1,0:T(8,128)(2,1)}, bf16[2048,1280]{1,0:T(8,128)(2,1)}, bf16[2048,1280]{1,0:T(8,128)(2,1)}) custom-call(bf16[256,400]{1,0:T(8,128)(2,1)} %maximum_bitcast_fusion.refs_0_, bf16[256,1280]{1,0:T(8,128)(2,1)} %refs_1_.1, bf16[256,1280]{1,0:T(8,128)(2,1)} %refs_2_.1), custom_call_target="tpu_custom_call" | custom-call | tf_op jit(solution)/shard_map/plane_gather/pallas_call | solution.py:517
  93.1 9.5 fusion.37.joint_ref
  110.2 10.9 %collective-permute-done = bf16[2048,128]{1,0:T(8,128)(2,1)S(1)} collective-permute-done((bf16[2048,128]{1,0:T(8,128)(2,1)}, bf16[2048,128]{1,0:T(8,128)(2,1)S(1)}, u32[]{:S(2)}, u32[]{:S(2)}) %collective-permute-start) | collective-permute-done | bytes 524320 | tf_op jit(solution)/shard_map/ppermute | solution.py:396
  152.0 14.2 %attend.3 = (bf16[256,1024]{1,0:T(8,128)(2,1)}, f32[4,1024]{1,0:T(4,128)}) custom-call(s32[1]{0:T(128)S(6)} %add.391.start_ref, s32[4096]{0:T(1024)} %bitcast.352, bf16[256,2048]{1,0:T(8,128)(2,1)} %get-tuple-element.50.q_ref, bf16[4096,128]{1,0:T(8,128)(2,1)} %pad_maximum_fusion.10.kv_ref, s32[2048,1]{1,0:T(8,128)} %copy.112.qpos_ref, ...), custom_call_target="tpu_custom_call" | custom-call | flops 4294967296 | bytes 4194304 | tf_op jit(solution)/shard_map/attend/pallas_call | solution.py:198
  166.2 10.5 %fusion.78 = f32[1024,1280]{1,0:T(8,128)} fusion(bf16[1024,2048]{1,0:T(8,128)(2,1)} %get-tuple-element.52, bf16[2048,1280]{0,1:T(8,128)(2,1)} %all-gather.7.cloned.1.call-done), kind=kOutput, calls=%fused_computation.248 | convolution fusion | flops 5368709120 | bytes 14680064 | tf_op jit(solution)/shard_map/dot_general | solution.py:21
  176.7 22.8 %all-gather.9.cloned.1.call-done = bf16[1024,1024]{1,0:T(8,128)(2,1)} async-done(((bf16[256,1024]{1,0:T(8,128)(2,1)}), bf16[1024,1024]{1,0:T(8,128)(2,1)}) %all-gather.9.cloned.1.call-update) | async-done | bytes 2097168 | tf_op jit(solution)/shard_map/all_gather | solution.py:378
  199.5 9.5 multiply_reduce_fusion.1
  212.3 11.3 %fusion.79 = f32[1024,1280]{1,0:T(8,128)} fusion(bf16[1024,2048]{1,0:T(8,128)(2,1)S(1)} %multiply_convert_fusion.1, bf16[2048,1280]{1,0:T(8,128)(2,1)} %get-tuple-element.44), kind=kOutput, calls=%fused_computation.249 | convolution fusion | flops 5368709120 | bytes 14680064 | tf_op jit(solution)/shard_map/dot_general | solution.py:21
  223.6 11.9 %multiply_convert_fusion.3 = (bf16[1024,1280]{1,0:T(8,128)(2,1)S(1)}, bf16[1024,1280]{1,0:T(8,128)(2,1)S(1)}, bf16[1024,1280]{1,0:T(8,128)(2,1)S(1)}) fusion(f32[1024,1280]{1,0:T(8,128)} %fusion.79, f32[1024,1280]{1,0:T(8,128)} %fusion.78, bf16[1024,2048]{1,0:T(8,128)(2,1)S(1)} %multiply_convert_fusion.1, bf16[2048,1280]{1,0:T(8,128)(2,1)} %get-tuple-element.54), kind=kOutput, calls=%fused_computation.41 | convolution fusion | flops 5389680640 | bytes 27787264 | tf_op jit(solution)/shard_map/dot_general | solution.py:21
  245.0 9.7 add_convert_fusion.1
  254.8 10.7 %fusion.81 = f32[1024,1280]{1,0:T(8,128)} fusion(bf16[1024,2048]{1,0:T(8,128)(2,1)} %get-tuple-element.55, bf16[2048,1280]{0,1:T(8,128)(2,1)} %all-gather.7.cloned.1.call-done), kind=kOutput, calls=%fused_computation.251 | convolution fusion | flops 5368709120 | bytes 14680064 | tf_op jit(solution)/shard_map/dot_general | solution.py:21
  265.5 9.6 multiply_reduce_fusion
  278.5 11.3 %fusion.82 = f32[1024,1280]{1,0:T(8,128)} fusion(bf16[1024,2048]{1,0:T(8,128)(2,1)S(1)} %multiply_convert_fusion, bf16[2048,1280]{1,0:T(8,128)(2,1)} %get-tuple-element.44), kind=kOutput, calls=%fused_computation.252 | convolution fusion | flops 5368709120 | bytes 14680064 | tf_op jit(solution)/shard_map/dot_general | solution.py:21
  289.8 13.5 %multiply_convert_fusion.2 = (bf16[1024,1280]{1,0:T(8,128)(2,1)}, bf16[1024,1280]{1,0:T(8,128)(2,1)}, bf16[1024,1280]{1,0:T(8,128)(2,1)S(1)}) fusion(f32[1024,1280]{1,0:T(8,128)} %fusion.82, f32[1024,1280]{1,0:T(8,128)} %fusion.81, bf16[1024,2048]{1,0:T(8,128)(2,1)S(1)} %multiply_convert_fusion, bf16[2048,1280]{1,0:T(8,128)(2,1)} %get-tuple-element.54), kind=kOutput, calls=%fused_computation.40 | convolution fusion | flops 5389680640 | bytes 27787264 | tf_op jit(solution)/shard_map/dot_general | solution.py:21
  310.9 11.2 %fusion.83 = f32[1024,2048]{1,0:T(8,128)} fusion(bf16[1024,1280]{1,0:T(8,128)(2,1)S(1)} %copy-done.30, bf16[2048,1280]{1,0:T(8,128)(2,1)} %get-tuple-element.44), kind=kOutput, calls=%fused_computation.253 | convolution fusion | flops 5368709120 | bytes 16252928 | tf_op jit(solution)/shard_map/dot_general | solution.py:18
  333.7 15.4 %fusion.8 = bf16[2048,1280]{0,1:T(8,128)(2,1)} fusion(bf16[2048,1280]{1,0:T(8,128)(2,1)S(1)} %pad_maximum_fusion.3, bf16[1,2048,2048]{2,1,0:T(8,128)(2,1)} %param.13), kind=kOutput, calls=%fused_computation.22 | convolution fusion | flops 10740039680 | bytes 18874368 | tf_op jit(solution)/shard_map/dot_general | solution.py:24
  349.1 15.6 %convolution_convert_fusion = bf16[2048,2048]{1,0:T(8,128)(2,1)} fusion(bf16[2048,1280]{1,0:T(8,128)(2,1)S(1)} %pad_maximum_fusion.3, bf16[2048,1280]{0,1:T(8,128)(2,1)} %all-gather.7.cloned.1.call-done), kind=kOutput, calls=%fused_computation.19 | convolution fusion | flops 10741612544 | bytes 18874368 | tf_op jit(solution)/shard_map/dot_general | solution.py:18
  364.7 15.1 %convolution_convert_fusion.2 = bf16[2048,1280]{1,0:T(8,128)(2,1)} fusion(bf16[2048,1280]{1,0:T(8,128)(2,1)S(1)} %bitcast.321, bf16[1024,2048]{1,0:T(8,128)(2,1)} %copy-done.20, bf16[1024,2048]{1,0:T(8,128)(2,1)S(1)} %copy-done.19), kind=kOutput, calls=%fused_computation.21 | convolution fusion | flops 10756816896 | bytes 18874368 | tf_op jit(solution)/shard_map/dot_general | solution.py:24
  379.9 13.6 %convolution_convert_fusion.1 = bf16[2048,1280]{1,0:T(8,128)(2,1)} fusion(bf16[2048,1280]{1,0:T(8,128)(2,1)S(1)} %bitcast.319, bf16[1024,2048]{1,0:T(8,128)(2,1)S(1)} %copy-done.21, bf16[1024,2048]{1,0:T(8,128)(2,1)S(1)} %copy-done.19), kind=kOutput, calls=%fused_computation.20 | convolution fusion | flops 10756816896 | bytes 18874368 | tf_op jit(solution)/shard_map/dot_general | solution.py:24
  393.4 33.8 %plane_gather.3 = bf16[2048,1536]{1,0:T(8,128)(2,1)} custom-call(bf16[256,1536]{1,0:T(8,128)(2,1)} %pad_maximum_fusion.13.refs_0_), custom_call_target="tpu_custom_call" | custom-call | tf_op jit(solution)/shard_map/plane_gather/pallas_call | solution.py:517
  478.5 40.7 %attend_grad.1 = (f32[256,2048]{1,0:T(8,128)}, bf16[4096,128]{1,0:T(8,128)(2,1)}) custom-call(s32[1]{0:T(128)} %bitcast.1.start_ref, s32[4096]{0:T(1024)} %bitcast.354, bf16[256,2048]{1,0:T(8,128)(2,1)} %get-tuple-element.50.q_ref, bf16[4096,128]{1,0:T(8,128)(2,1)} %pad_maximum_fusion.10.kv_ref, bf16[256,2048]{1,0:T(8,128)(2,1)} %pad_maximum_fusion.11.o_ref, ...), custom_call_target="tpu_custom_call" | custom-call | flops 21474836480 | bytes 8388608 | tf_op jit(solution)/shard_map/attend_grad/pallas_call | solution.py:315
  520.3 39.6 %collective-permute-start.13 = (bf16[1,2048,128]{2,1,0:T(8,128)(2,1)S(1)}, bf16[1,2048,128]{2,1,0:T(8,128)(2,1)S(1)}, u32[]{:S(2)}, u32[]{:S(2)}) collective-permute-start(bf16[1,2048,128]{2,1,0:T(8,128)(2,1)S(1)} %dynamic-slice_bitcast_fusion.5), channel_id=1, source_target_pairs={{0,4},{4,0},{1,5},{5,1},{2,6},{6,2},{3,7},{7,3},{8,12},{12,8},{9,1... | collective-permute-start | bytes 1572872 | tf_op jit(solution)/shard_map/ppermute | solution.py:414
  559.9 12.0 %collective-permute-done.13 = bf16[1,2048,128]{2,1,0:T(8,128)(2,1)S(1)} collective-permute-done((bf16[1,2048,128]{2,1,0:T(8,128)(2,1)S(1)}, bf16[1,2048,128]{2,1,0:T(8,128)(2,1)S(1)}, u32[]{:S(2)}, u32[]{:S(2)}) %collective-permute-start.13) | collective-permute-done | bytes 524320 | tf_op jit(solution)/shard_map/ppermute | solution.py:414
  607.1 18.5 %collective-permute-done.14 = bf16[384,512]{0,1:T(8,128)(2,1)S(1)} collective-permute-done((bf16[384,512]{0,1:T(8,128)(2,1)S(1)}, bf16[384,512]{0,1:T(8,128)(2,1)S(1)}, u32[]{:S(2)}, u32[]{:S(2)}) %collective-permute-start.14) | collective-permute-done | bytes 393248 | tf_op jit(solution)/shard_map/ppermute | solution.py:442
  640.0 14.6 %collective-permute-done.15 = bf16[384,512]{0,1:T(8,128)(2,1)S(1)} collective-permute-done((bf16[384,512]{0,1:T(8,128)(2,1)S(1)}, bf16[384,512]{0,1:T(8,128)(2,1)S(1)}, u32[]{:S(2)}, u32[]{:S(2)}) %collective-permute-start.15) | collective-permute-done | bytes 393248 | tf_op jit(solution)/shard_map/ppermute | solution.py:442
  679.9 9.6 reshape_reshape.23
  721.7 18.6 %collective-permute-done.30 = bf16[1,2,256,1280]{3,2,1,0:T(8,128)(2,1)} collective-permute-done((bf16[1,2,256,1280]{3,2,1,0:T(8,128)(2,1)}, bf16[1,2,256,1280]{3,2,1,0:T(8,128)(2,1)}, u32[]{:S(2)}, u32[]{:S(2)}) %collective-permute-start.30) | collective-permute-done | bytes 1310752 | tf_op jit(solution)/shard_map/ppermute | solution.py:414
  744.2 24.1 %collective-permute-done.33 = bf16[1,2,256,1280]{3,2,1,0:T(8,128)(2,1)S(1)} collective-permute-done((bf16[1,2,256,1280]{3,2,1,0:T(8,128)(2,1)S(1)}, bf16[1,2,256,1280]{3,2,1,0:T(8,128)(2,1)S(1)}, u32[]{:S(2)}, u32[]{:S(2)}) %collective-permute-start.33) | collective-permute-done | bytes 1310752 | tf_op jit(solution)/shard_map/ppermute | solution.py:414
  770.8 24.6 %collective-permute-done.36 = bf16[1,2,256,1280]{2,3,1,0:T(8,128)(2,1)S(1)} collective-permute-done((bf16[1,2,256,1280]{2,3,1,0:T(8,128)(2,1)S(1)}, bf16[1,2,256,1280]{2,3,1,0:T(8,128)(2,1)S(1)}, u32[]{:S(2)}, u32[]{:S(2)}) %collective-permute-start.36) | collective-permute-done | bytes 1310752 | tf_op jit(solution)/shard_map/ppermute | solution.py:414
  829.8 29.5 %collective-permute-done.18 = bf16[1,2,256,400]{2,3,1,0:T(8,128)(2,1)S(1)} collective-permute-done((bf16[1,2,256,400]{2,3,1,0:T(8,128)(2,1)S(1)}, bf16[1,2,256,400]{2,3,1,0:T(8,128)(2,1)S(1)}, u32[]{:S(2)}, u32[]{:S(2)}) %collective-permute-start.18) | collective-permute-done | bytes 409632 | tf_op jit(solution)/shard_map/ppermute | solution.py:414
  895.6 9.5 collective-permute-done.24
  910.7 79.6 %all-gather.15.cloned.1.call-done = bf16[2,1024,2048]{2,1,0:T(8,128)(2,1)} async-done(((bf16[2,256,2048]{2,1,0:T(8,128)(2,1)}), bf16[2,1024,2048]{2,1,0:T(8,128)(2,1)}) %all-gather.15.cloned.1.call-update) | async-done | bytes 8388624 | tf_op jit(solution)/shard_map/all_gather | solution.py:378
  (400 shorter events, 357.9 us)
Async XLA Ops:
  7.2 116.1 %all-gather.7.cloned.1.call-start = ((), (), s32[]{:S(2)}) async-start(), calls=%async_computation.4 | async-start | bytes 5898240 | tf_op jit(solution)/shard_map/all_gather | solution.py:378
  70.1 81.9 %all-gather.11.cloned.1.call-start = ((), (), s32[]{:S(2)}) async-start(), calls=%async_computation.6 | async-start | bytes 4718592 | tf_op jit(solution)/shard_map/all_gather | solution.py:378
  84.7 114.8 %all-gather.9.cloned.1.call-start = ((), (), s32[]{:S(2)}) async-start(), calls=%async_computation.5 | async-start | bytes 2621440 | tf_op jit(solution)/shard_map/all_gather | solution.py:378
  106.9 14.2 %collective-permute-start = (bf16[2048,128]{1,0:T(8,128)(2,1)}, bf16[2048,128]{1,0:T(8,128)(2,1)S(1)}, u32[]{:S(2)}, u32[]{:S(2)}) collective-permute-start(bf16[2048,128]{1,0:T(8,128)(2,1)} %get-tuple-element.47), channel_id=1, source_target_pairs={{0,4},{4,0},{1,5},{5,1},{2,6},{6,2},{3,7},{7,3},{8,12},{12,8},{9,1... | collective-permute-start | bytes 1572872 | tf_op jit(solution)/shard_map/ppermute | solution.py:396
  132.7 132.8 %all-gather.13.cloned.1.call-start = ((), (), s32[]{:S(2)}) async-start(), calls=%async_computation.8 | async-start | bytes 2621440 | tf_op jit(solution)/shard_map/all_gather | solution.py:378
  135.6 13.6 %collective-permute-start.11 = (bf16[256,384]{1,0:T(8,128)(2,1)S(1)}, bf16[256,384]{1,0:T(8,128)(2,1)S(1)}, u32[]{:S(2)}, u32[]{:S(2)}) collective-permute-start(bf16[256,384]{1,0:T(8,128)(2,1)S(1)} %copy-done.39), channel_id=1, source_target_pairs={{0,2},{1,3},{2,0},{3,1},{4,6},{5,7},{6,4},{7,5},{8,10},{9,11},{10,... | collective-permute-start | bytes 589832 | tf_op jit(solution)/shard_map/ppermute | solution.py:424
  166.2 266.2 %reduce-scatter.5.cloned.1.call-start = ((), (), s32[]{:S(2)}) async-start(), calls=%async_computation.7 | async-start | bytes 5242880 | tf_op jit(solution)/shard_map/reduce_scatter | solution.py:382
  254.8 177.6 %reduce-scatter.7.cloned.1.call-start = ((), (), s32[]{:S(2)}) async-start(), calls=%async_computation.9 | async-start | bytes 5242880 | tf_op jit(solution)/shard_map/reduce_scatter | solution.py:382
  331.5 376.8 %reduce-scatter.11.cloned.1.call-start = ((), (), s32[]{:S(2)}) async-start(), calls=%async_computation.11 | async-start | bytes 5242880 | tf_op jit(solution)/shard_map/reduce_scatter | solution.py:382
  472.2 238.4 %reduce-scatter.9.cloned.1.call-start = ((), (), s32[]{:S(2)}) async-start(), calls=%async_computation.10 | async-start | bytes 5242880 | tf_op jit(solution)/shard_map/reduce_scatter | solution.py:382
  478.5 432.2 %all-gather.17.cloned.1.call-start = ((), (), s32[]{:S(2)}) async-start(), calls=%async_computation.13 | async-start | bytes 10485760 | tf_op jit(solution)/shard_map/all_gather | solution.py:378
  520.3 51.5 %collective-permute-start.13 = (bf16[1,2048,128]{2,1,0:T(8,128)(2,1)S(1)}, bf16[1,2048,128]{2,1,0:T(8,128)(2,1)S(1)}, u32[]{:S(2)}, u32[]{:S(2)}) collective-permute-start(bf16[1,2048,128]{2,1,0:T(8,128)(2,1)S(1)} %dynamic-slice_bitcast_fusion.5), channel_id=1, source_target_pairs={{0,4},{4,0},{1,5},{5,1},{2,6},{6,2},{3,7},{7,3},{8,12},{12,8},{9,1... | collective-permute-start | bytes 1572872 | tf_op jit(solution)/shard_map/ppermute | solution.py:414
  603.5 22.1 %collective-permute-start.14 = (bf16[384,512]{0,1:T(8,128)(2,1)S(1)}, bf16[384,512]{0,1:T(8,128)(2,1)S(1)}, u32[]{:S(2)}, u32[]{:S(2)}) collective-permute-start(bf16[384,512]{0,1:T(8,128)(2,1)S(1)} %dynamic-slice_bitcast_fusion.8), channel_id=1, source_target_pairs={{0,1},{1,2},{2,3},{3,0},{4,5},{5,6},{6,7},{7,4},{8,9},{9,10},{10,1... | collective-permute-start | bytes 1179656 | tf_op jit(solution)/shard_map/ppermute | solution.py:442
  627.6 27.0 %collective-permute-start.15 = (bf16[384,512]{0,1:T(8,128)(2,1)S(1)}, bf16[384,512]{0,1:T(8,128)(2,1)S(1)}, u32[]{:S(2)}, u32[]{:S(2)}) collective-permute-start(bf16[384,512]{0,1:T(8,128)(2,1)S(1)} %get-tuple-element.161), channel_id=1, source_target_pairs={{0,2},{1,3},{2,0},{3,1},{4,6},{5,7},{6,4},{7,5},{8,10},{9,11},{10,... | collective-permute-start | bytes 1179656 | tf_op jit(solution)/shard_map/ppermute | solution.py:442
  639.6 18.5 %collective-permute-start.16 = (bf16[384,512]{0,1:T(8,128)(2,1)S(1)}, bf16[384,512]{0,1:T(8,128)(2,1)S(1)}, u32[]{:S(2)}, u32[]{:S(2)}) collective-permute-start(bf16[384,512]{0,1:T(8,128)(2,1)S(1)} %get-tuple-element.160), channel_id=1, source_target_pairs={{0,3},{1,0},{2,1},{3,2},{4,7},{5,4},{6,5},{7,6},{8,11},{9,8},{10,9... | collective-permute-start | bytes 1179656 | tf_op jit(solution)/shard_map/ppermute | solution.py:442
  674.5 315.8 %all-gather.15.cloned.1.call-start = ((), (), s32[]{:S(2)}) async-start(), calls=%async_computation.12 | async-start | bytes 10485760 | tf_op jit(solution)/shard_map/all_gather | solution.py:378
  678.0 25.3 %collective-permute-start.29 = (bf16[2,2,256,1280]{3,2,1,0:T(8,128)(2,1)}, bf16[2,2,256,1280]{3,2,1,0:T(8,128)(2,1)}, u32[]{:S(2)}, u32[]{:S(2)}) collective-permute-start(bf16[2,2,256,1280]{3,2,1,0:T(8,128)(2,1)} %dynamic-slice_bitcast_fusion.1), channel_id=1, source_target_pairs={{0,8},{8,0},{16,24},{24,16},{1,9},{9,1},{17,25},{25,17},{2,10},{10... | collective-permute-start | bytes 7864328 | tf_op jit(solution)/shard_map/ppermute | solution.py:414
  693.3 20.3 %collective-permute-start.32 = (bf16[2,2,256,1280]{3,2,1,0:T(8,128)(2,1)}, bf16[2,2,256,1280]{3,2,1,0:T(8,128)(2,1)}, u32[]{:S(2)}, u32[]{:S(2)}) collective-permute-start(bf16[2,2,256,1280]{3,2,1,0:T(8,128)(2,1)} %dynamic-slice_bitcast_fusion), channel_id=1, source_target_pairs={{0,8},{8,0},{16,24},{24,16},{1,9},{9,1},{17,25},{25,17},{2,10},{10... | collective-permute-start | bytes 7864328 | tf_op jit(solution)/shard_map/ppermute | solution.py:414
  700.8 18.3 %collective-permute-start.35 = (bf16[2,2,256,1280]{2,3,1,0:T(8,128)(2,1)}, bf16[2,2,256,1280]{2,3,1,0:T(8,128)(2,1)}, u32[]{:S(2)}, u32[]{:S(2)}) collective-permute-start(bf16[2,2,256,1280]{2,3,1,0:T(8,128)(2,1)} %bitcast.303), channel_id=1, source_target_pairs={{0,8},{8,0},{16,24},{24,16},{1,9},{9,1},{17,25},{25,17},{2,10},{10... | collective-permute-start | bytes 7864328 | tf_op jit(solution)/shard_map/ppermute | solution.py:414
  708.3 32.0 %collective-permute-start.30 = (bf16[1,2,256,1280]{3,2,1,0:T(8,128)(2,1)}, bf16[1,2,256,1280]{3,2,1,0:T(8,128)(2,1)}, u32[]{:S(2)}, u32[]{:S(2)}) collective-permute-start(bf16[1,2,256,1280]{3,2,1,0:T(8,128)(2,1)} %constant_dynamic-slice_fusion.7), channel_id=1, source_target_pairs={{0,16},{8,24},{16,0},{24,8},{1,17},{9,25},{17,1},{25,9},{2,18},{10... | collective-permute-start | bytes 3932168 | tf_op jit(solution)/shard_map/ppermute | solution.py:414
  717.0 51.3 %collective-permute-start.33 = (bf16[1,2,256,1280]{3,2,1,0:T(8,128)(2,1)S(1)}, bf16[1,2,256,1280]{3,2,1,0:T(8,128)(2,1)S(1)}, u32[]{:S(2)}, u32[]{:S(2)}) collective-permute-start(bf16[1,2,256,1280]{3,2,1,0:T(8,128)(2,1)S(1)} %constant_dynamic-slice_fusion.5), channel_id=1, source_target_pairs={{0,16},{8,24},{16,0},{24,8},{1,17},{9,25},{17,1},{25,9},{2,18},{10... | collective-permute-start | bytes 3932168 | tf_op jit(solution)/shard_map/ppermute | solution.py:414
  721.6 73.8 %collective-permute-start.36 = (bf16[1,2,256,1280]{2,3,1,0:T(8,128)(2,1)S(1)}, bf16[1,2,256,1280]{2,3,1,0:T(8,128)(2,1)S(1)}, u32[]{:S(2)}, u32[]{:S(2)}) collective-permute-start(bf16[1,2,256,1280]{2,3,1,0:T(8,128)(2,1)S(1)} %constant_dynamic-slice_fusion.1), channel_id=1, source_target_pairs={{0,16},{8,24},{16,0},{24,8},{1,17},{9,25},{17,1},{25,9},{2,18},{10... | collective-permute-start | bytes 3932168 | tf_op jit(solution)/shard_map/ppermute | solution.py:414
  743.0 77.0 %collective-permute-start.31 = (bf16[1,1,256,1280]{3,2,1,0:T(8,128)(2,1)}, bf16[1,1,256,1280]{3,2,1,0:T(8,128)(2,1)}, u32[]{:S(2)}, u32[]{:S(2)}) collective-permute-start(bf16[1,1,256,1280]{3,2,1,0:T(8,128)(2,1)} %constant_dynamic-slice_fusion.6), channel_id=1, source_target_pairs={{0,4},{4,0},{1,5},{5,1},{2,6},{6,2},{3,7},{7,3},{8,12},{12,8},{9,1... | collective-permute-start | bytes 1966088 | tf_op jit(solution)/shard_map/ppermute | solution.py:414
  769.6 57.9 %collective-permute-start.34 = (bf16[1,1,256,1280]{3,2,1,0:T(8,128)(2,1)}, bf16[1,1,256,1280]{3,2,1,0:T(8,128)(2,1)}, u32[]{:S(2)}, u32[]{:S(2)}) collective-permute-start(bf16[1,1,256,1280]{3,2,1,0:T(8,128)(2,1)} %constant_dynamic-slice_fusion.4), channel_id=1, source_target_pairs={{0,4},{4,0},{1,5},{5,1},{2,6},{6,2},{3,7},{7,3},{8,12},{12,8},{9,1... | collective-permute-start | bytes 1966088 | tf_op jit(solution)/shard_map/ppermute | solution.py:414
  797.8 64.3 %collective-permute-start.37 = (bf16[1,1,256,1280]{2,3,1,0:T(8,128)(2,1)}, bf16[1,1,256,1280]{2,3,1,0:T(8,128)(2,1)}, u32[]{:S(2)}, u32[]{:S(2)}) collective-permute-start(bf16[1,1,256,1280]{2,3,1,0:T(8,128)(2,1)} %constant_dynamic-slice_fusion), channel_id=1, source_target_pairs={{0,4},{4,0},{1,5},{5,1},{2,6},{6,2},{3,7},{7,3},{8,12},{12,8},{9,1... | collective-permute-start | bytes 1966088 | tf_op jit(solution)/shard_map/ppermute | solution.py:414
  803.1 19.4 %collective-permute-start.20 = (bf16[2,2,256,1024]{3,2,1,0:T(8,128)(2,1)}, bf16[2,2,256,1024]{3,2,1,0:T(8,128)(2,1)}, u32[]{:S(2)}, u32[]{:S(2)}) collective-permute-start(bf16[2,2,256,1024]{3,2,1,0:T(8,128)(2,1)} %dynamic-slice_bitcast_fusion.2), channel_id=1, source_target_pairs={{0,8},{8,0},{16,24},{24,16},{1,9},{9,1},{17,25},{25,17},{2,10},{10... | collective-permute-start | bytes 6291464 | tf_op jit(solution)/shard_map/ppermute | solution.py:414
  825.1 35.2 %collective-permute-start.21 = (bf16[1,2,256,1024]{3,2,1,0:T(8,128)(2,1)S(1)}, bf16[1,2,256,1024]{3,2,1,0:T(8,128)(2,1)S(1)}, u32[]{:S(2)}, u32[]{:S(2)}) collective-permute-start(bf16[1,2,256,1024]{3,2,1,0:T(8,128)(2,1)S(1)} %constant_dynamic-slice_fusion.9), channel_id=1, source_target_pairs={{0,16},{8,24},{16,0},{24,8},{1,17},{9,25},{17,1},{25,9},{2,18},{10... | collective-permute-start | bytes 3145736 | tf_op jit(solution)/shard_map/ppermute | solution.py:414
  825.7 33.6 %collective-permute-start.18 = (bf16[1,2,256,400]{2,3,1,0:T(8,128)(2,1)S(1)}, bf16[1,2,256,400]{2,3,1,0:T(8,128)(2,1)S(1)}, u32[]{:S(2)}, u32[]{:S(2)}) collective-permute-start(bf16[1,2,256,400]{2,3,1,0:T(8,128)(2,1)S(1)} %constant_dynamic-slice_fusion.13), channel_id=1, source_target_pairs={{0,16},{8,24},{16,0},{24,8},{1,17},{9,25},{17,1},{25,9},{2,18},{10... | collective-permute-start | bytes 1228808 | tf_op jit(solution)/shard_map/ppermute | solution.py:414
  860.8 16.5 %collective-permute-start.22 = (bf16[1,1,256,1024]{3,2,1,0:T(8,128)(2,1)S(1)}, bf16[1,1,256,1024]{3,2,1,0:T(8,128)(2,1)S(1)}, u32[]{:S(2)}, u32[]{:S(2)}) collective-permute-start(bf16[1,1,256,1024]{3,2,1,0:T(8,128)(2,1)S(1)} %constant_dynamic-slice_fusion.8), channel_id=1, source_target_pairs={{0,4},{4,0},{1,5},{5,1},{2,6},{6,2},{3,7},{7,3},{8,12},{12,8},{9,1... | collective-permute-start | bytes 1572872 | tf_op jit(solution)/shard_map/ppermute | solution.py:414
  867.6 14.6 %collective-permute-start.28 = (f32[16,256]{1,0:T(8,128)S(1)}, f32[16,256]{1,0:T(8,128)S(1)}, u32[]{:S(2)}, u32[]{:S(2)}) collective-permute-start(f32[16,256]{1,0:T(8,128)S(1)} %slice_bitcast_fusion.24), channel_id=1, source_target_pairs={{0,3},{1,0},{2,1},{3,2},{4,7},{5,4},{6,5},{7,6},{8,11},{9,8},{10,9... | collective-permute-start | bytes 49160 | tf_op jit(solution)/shard_map/ppermute | solution.py:433
  890.2 15.0 %collective-permute-start.24 = (bf16[256,256]{0,1:T(8,128)(2,1)S(1)}, bf16[256,256]{0,1:T(8,128)(2,1)S(1)}, u32[]{:S(2)}, u32[]{:S(2)}) collective-permute-start(bf16[256,256]{0,1:T(8,128)(2,1)S(1)} %get-tuple-element.174), channel_id=1, source_target_pairs={{0,2},{1,3},{2,0},{3,1},{4,6},{5,7},{6,4},{7,5},{8,10},{9,11},{10,... | collective-permute-start | bytes 393224 | tf_op jit(solution)/shard_map/ppermute | solution.py:442
  893.7 16.0 %collective-permute-start.25 = (bf16[256,256]{0,1:T(8,128)(2,1)S(1)}, bf16[256,256]{0,1:T(8,128)(2,1)S(1)}, u32[]{:S(2)}, u32[]{:S(2)}) collective-permute-start(bf16[256,256]{0,1:T(8,128)(2,1)S(1)} %get-tuple-element.173), channel_id=1, source_target_pairs={{0,3},{1,0},{2,1},{3,2},{4,7},{5,4},{6,5},{7,6},{8,11},{9,8},{10,9... | collective-permute-start | bytes 393224 | tf_op jit(solution)/shard_map/ppermute | solution.py:442
  (85 other events, 975.6 us)
Sparse Core Ops, SparseCore 0:
  70.2 42.3 all-gather.6
  114.5 37.4 all-gather.10
  153.5 45.9 all-gather.8
  200.9 44.6 all-gather.12
  254.9 75.4 reduce-scatter.4
  332.7 77.2 reduce-scatter.6
  472.3 76.1 reduce-scatter.10
  551.4 85.6 reduce-scatter.8
  674.6 153.8 all-gather.16
  829.9 160.3 all-gather.14

commit v4 on v3

--- a/solution.py
+++ b/solution.py
@@ -390,14 +390,6 @@
     return lax.optimization_barrier((value,) + others)[0]
 
 
-def both_halves(part):
-    if lax.axis_size("context") != 2:
-        return gathered(part, "context", 0)
-    other = lax.ppermute(part, "context", [(0, 1), (1, 0)])
-    low = lax.axis_index("context") == 0
-    return jnp.concatenate([jnp.where(low, part, other), jnp.where(low, other, part)], axis=0)
-
-
 def halving_scatter(terms, axes):
     sizes = [lax.axis_size(axis) for axis in axes]
     blocks = terms.reshape(tuple(sizes) + (-1,) + terms.shape[1:])
@@ -444,9 +436,34 @@
     return out
 
 
-def gather_kernel(count, *refs):
-    sources, targets = refs[:count], refs[count : 2 * count]
-    own_sem, send_sem, recv_sem = refs[2 * count :]
+def remote(source, target, sems, index, device):
+    copy = pltpu.make_async_remote_copy(
+        src_ref=source,
+        dst_ref=target,
+        send_sem=sems[0].at[index],
+        recv_sem=sems[1].at[index],
+        device_id=device,
+        device_id_type=pl.DeviceIdType.MESH,
+    )
+    copy.start()
+    return copy
+
+
+def greet(devices):
+    barrier = pltpu.get_barrier_semaphore()
+    for device in devices:
+        pl.semaphore_signal(barrier, inc=1, device_id=device, device_id_type=pl.DeviceIdType.MESH)
+    pl.semaphore_wait(barrier, len(devices))
+
+
+def aligned(start, size):
+    return pl.ds(pl.multiple_of(start, size), size)
+
+
+def gather_kernel(count, lines, pairs, *refs):
+    arrays = count + lines + pairs
+    sources, targets = refs[:arrays], refs[arrays : 2 * arrays]
+    own_sem, send_sem, recv_sem = refs[2 * arrays : 2 * arrays + 3]
     dp, context = lax.axis_index("dp"), lax.axis_index("context")
     outer, inner = dp // 2, dp % 2
     across, along, beside = (
@@ -454,15 +471,14 @@
         {"context": 1 - context},
         {"dp": dp + 1 - 2 * inner},
     )
-    barrier = pltpu.get_barrier_semaphore()
-    for device in (across, along, beside):
-        pl.semaphore_signal(barrier, inc=1, device_id=device, device_id_type=pl.DeviceIdType.MESH)
-    pl.semaphore_wait(barrier, 3)
+    me, ways = lax.axis_index("tensor"), lax.axis_size("tensor")
+    peers = [{"tensor": lax.rem(me + step, ways)} for step in range(1, ways)] if lines else []
+    greet(([across, along, beside] if count else [along]) + peers)
 
     def place(array, o, k, first=0, parts=1):
         rows = sources[array].shape[0]
         start = ((2 * o + inner) * 2 + k) * rows + first * (rows // parts)
-        return targets[array].at[pl.ds(pl.multiple_of(start, rows // parts), rows // parts), :]
+        return targets[array].at[aligned(start, rows // parts), :]
 
     def send(array, kind, source, target, device):
         copy = pltpu.make_async_remote_copy(
@@ -477,11 +493,27 @@
         return copy
 
     copies, kept = {}, []
+    passed = []
+    for a in range(count + lines, arrays):
+        rows = sources[a].shape[0]
+        mine = targets[a].at[aligned(context * rows, rows), :]
+        passed.append(send(a, 0, sources[a], mine, along))
+        keep = pltpu.make_async_copy(sources[a], mine, own_sem.at[a])
+        keep.start()
+        kept.append(keep)
     for a in range(count):
         mine = place(a, outer, context)
         copies[a, 0] = send(a, 0, sources[a], mine, across)
         copies[a, 1] = send(a, 1, sources[a], mine, along)
         copies[a, 2] = send(a, 2, sources[a], mine, beside)
+        keep = pltpu.make_async_copy(sources[a], mine, own_sem.at[a])
+        keep.start()
+        kept.append(keep)
+    for a in range(count, count + lines):
+        width = sources[a].shape[1]
+        mine = targets[a].at[:, aligned(me * width, width)]
+        for k, peer in enumerate(peers):
+            passed.append(send(a, k, sources[a], mine, peer))
         keep = pltpu.make_async_copy(sources[a], mine, own_sem.at[a])
         keep.start()
         kept.append(keep)
@@ -501,32 +533,155 @@
             copies[a, kind].wait_recv()
             half = place(a, 1 - outer, 1 - context, first, 2)
             copies[a, 7 + first] = send(a, 7 + first, half, half, beside)
+    for keep in kept:
+        keep.wait()
+    for copy in passed:
+        copy.wait()
     for a in range(count):
-        kept[a].wait()
         for kind in (2, 4, 6, 7, 8):
             copies[a, kind].wait_recv()
     for copy in copies.values():
         copy.wait_send()
 
 
-def plane_gather(parts, collective):
-    share = lax.axis_size("dp") * lax.axis_size("context")
+def plane_gather(parts, lines, pairs, collective):
+    share, ways = lax.axis_size("dp") * lax.axis_size("context"), lax.axis_size("tensor")
     if (lax.axis_size("dp"), lax.axis_size("context")) != (4, 2):
-        return [gathered(part, SHARE, 0) for part in parts]
-    count = len(parts)
+        whole = [gathered(part, SHARE, 0) for part in parts] + [jnp.concatenate(list(spread(line)), axis=1) for line in lines]
+        return whole + [gathered(pair, "context", 0) for pair in pairs]
+    arrays = len(parts) + len(lines) + len(pairs)
+    shapes = [(share * part.shape[0], part.shape[1]) for part in parts] + [(line.shape[0], ways * line.shape[1]) for line in lines]
+    shapes += [(2 * pair.shape[0], pair.shape[1]) for pair in pairs]
     return pl.pallas_call(
-        functools.partial(gather_kernel, count),
-        out_shape=tuple(jax.ShapeDtypeStruct((share * part.shape[0],) + part.shape[1:], part.dtype) for part in parts),
-        in_specs=[pl.BlockSpec(memory_space=pltpu.VMEM)] * count,
-        out_specs=(pl.BlockSpec(memory_space=pl.ANY),) * count,
+        functools.partial(gather_kernel, len(parts), len(lines), len(pairs)),
+        out_shape=tuple(jax.ShapeDtypeStruct(shape, bf16) for shape in shapes),
+        in_specs=[pl.BlockSpec(memory_space=pltpu.VMEM)] * arrays,
+        out_specs=(pl.BlockSpec(memory_space=pl.ANY),) * arrays,
         scratch_shapes=[
-            pltpu.SemaphoreType.DMA((count,)),
-            pltpu.SemaphoreType.DMA((count, 9)),
-            pltpu.SemaphoreType.DMA((count, 9)),
+            pltpu.SemaphoreType.DMA((arrays,)),
+            pltpu.SemaphoreType.DMA((arrays, 9)),
+            pltpu.SemaphoreType.DMA((arrays, 9)),
         ],
         compiler_params=pltpu.CompilerParams(collective_id=collective, has_side_effects=True),
         name="plane_gather",
-    )(*parts)
+    )(*parts, *lines, *pairs)
+
+
+def heads_kernel(ways, chunks, grad_ref, out_ref, own_sem, send_sem, recv_sem):
+    me = lax.axis_index("tensor")
+    peers = [lax.rem(me + step, ways) for step in range(1, ways)]
+    greet([{"tensor": peer} for peer in peers])
+    size, width = grad_ref.shape[0] // chunks, grad_ref.shape[1] // ways
+    copies = []
+    for c in range(chunks):
+        rows = pl.ds(c * size, size)
+        target = out_ref.at[aligned((c * ways + me) * size, size), :]
+        for k, peer in enumerate(peers):
+            source = grad_ref.at[rows, aligned(peer * width, width)]
+            copies.append(remote(source, target, (send_sem, recv_sem), c * (ways - 1) + k, {"tensor": peer}))
+        kept = pltpu.make_async_copy(grad_ref.at[rows, aligned(me * width, width)], target, own_sem.at[c])
+        kept.start()
+        copies.append(kept)
+    for copy in copies:
+        copy.wait()
+
+
+def to_heads(grad, chunks, collective):
+    ways = lax.axis_size("tensor")
+    count = chunks * (ways - 1)
+    return pl.pallas_call(
+        functools.partial(heads_kernel, ways, chunks),
+        out_shape=jax.ShapeDtypeStruct((grad.shape[0] * ways, grad.shape[1] // ways), grad.dtype),
+        in_specs=[pl.BlockSpec(memory_space=pltpu.VMEM)],
+        out_specs=pl.BlockSpec(memory_space=pl.ANY),
+        scratch_shapes=[pltpu.SemaphoreType.DMA((chunks,))] + [pltpu.SemaphoreType.DMA((count,))] * 2,
+        compiler_params=pltpu.CompilerParams(collective_id=collective, has_side_effects=True),
+        name="to_heads",
+    )(grad)
+
+
+def tail_kernel(heads, ways, chunks, joint_ref, cos_ref, sin_ref, gain_ref, dq_ref, dkv_ref,
+                grad_ref, part_ref, dgain_ref, got_ref, own_sem, send_sem, recv_sem):
+    D, half = HEAD_DIM, HEAD_DIM // 2
+    rows, count = joint_ref.shape
+    queries = heads * D
+    me, context = lax.axis_index("tensor"), lax.axis_index("context")
+    peers = [lax.rem(me + step, ways) for step in range(1, ways)]
+    along = {"context": 1 - context}
+    greet([along] + [{"tensor": peer} for peer in peers])
+    sems = (send_sem, recv_sem)
+    block = min(count, 512)
+    size = count // chunks // ways
+    copies = [remote(dkv_ref.at[aligned((1 - context) * count, count), :], got_ref, sems, 0, along)]
+
+    def one(first, columns, grad, gain):
+        x = joint_ref[first : first + D, columns]
+        cos, sin = cos_ref[:, columns], sin_ref[:, columns]
+        r = lax.rsqrt(jnp.mean(x * x, axis=0, keepdims=True) + epsilon)
+        n = x * r
+        lo, hi = grad[:half], grad[half:]
+        back = jnp.concatenate([lo * cos + hi * sin, hi * cos - lo * sin], axis=0)
+        scaled = back * gain
+        result = r * (scaled - n * jnp.mean(scaled * n, axis=0, keepdims=True))
+        grad_ref[first : first + D, columns] = result.astype(bf16)
+        return jnp.sum(back * n, axis=1, keepdims=True)
+
+    def hand_out(first, height, index):
+        for c in range(chunks):
+            target = part_ref.at[pl.ds(pl.multiple_of(me * rows + first, 128), height), pl.ds(c * size, size)]
+            for k, peer in enumerate(peers):
+                source = grad_ref.at[pl.ds(first, height), aligned((c * ways + peer) * size, size)]
+                copies.append(remote(source, target, sems, 1 + (index * chunks + c) * (ways - 1) + k, {"tensor": peer}))
+            kept = pltpu.make_async_copy(
+                grad_ref.at[pl.ds(first, height), aligned((c * ways + me) * size, size)], target, own_sem.at[index * chunks + c]
+            )
+            kept.start()
+            copies.append(kept)
+
+    total = jnp.zeros((D, 1), f32)
+    for b in range(count // block):
+        columns = slice(b * block, (b + 1) * block)
+        for h in range(heads):
+            total += one(h * D, columns, dq_ref[h * D : (h + 1) * D, columns], gain_ref[:, 0:1])
+    hand_out(0, queries, 0)
+    copies[0].wait_recv()
+    key_total = jnp.zeros((D, 1), f32)
+    for b in range(count // block):
+        columns = slice(b * block, (b + 1) * block)
+        mine = dkv_ref[aligned(context * count + b * block, block), :].astype(f32)
+        both = (mine + got_ref[columns, :].astype(f32)).T
+        key_total += one(queries, columns, both[:D], gain_ref[:, 1:2])
+        grad_ref[queries + D : queries + 2 * D, columns] = both[D:].astype(bf16)
+    hand_out(queries, 2 * D, 1)
+    dgain_ref[...] = jnp.concatenate([total, key_total], axis=1)
+    copies[0].wait_send()
+    for copy in copies[1:]:
+        copy.wait()
+
+
+def joint_tail(joint, cos, sin, gains, dq, dkv, heads, chunks, collective):
+    rows, count = joint.shape
+    ways = lax.axis_size("tensor")
+    number = 1 + 2 * chunks * (ways - 1)
+    vmem = pl.BlockSpec(memory_space=pltpu.VMEM)
+    return pl.pallas_call(
+        functools.partial(tail_kernel, heads, ways, chunks),
+        out_shape=(
+            jax.ShapeDtypeStruct((rows, count), bf16),
+            jax.ShapeDtypeStruct((ways * rows, count // ways), bf16),
+            jax.ShapeDtypeStruct((HEAD_DIM, 2), f32),
+        ),
+        in_specs=[vmem] * 6,
+        out_specs=(vmem, pl.BlockSpec(memory_space=pl.ANY), vmem),
+        scratch_shapes=[
+            pltpu.VMEM((count, 2 * HEAD_DIM), bf16),
+            pltpu.SemaphoreType.DMA((2 * chunks,)),
+            pltpu.SemaphoreType.DMA((number,)),
+            pltpu.SemaphoreType.DMA((number,)),
+        ],
+        compiler_params=pltpu.CompilerParams(collective_id=collective, has_side_effects=True),
+        name="joint_tail",
+    )(joint, cos, sin, gains, dq, dkv)
 
 
 def rope_tables(positions):
@@ -553,15 +708,12 @@
     packed = jnp.concatenate(
         [qkv_shard, attn_gain[None], ffn_gain[None], jnp.zeros((14, w_qkv.shape[0]), bf16)], axis=0
     )
-    packed_all, gate_all, up_all = plane_gather([packed.T, w_gate, w_up], 0)
+    packed_all, gate_all, out_t, qkv_t = plane_gather([packed.T, w_gate], [w_out.T, w_qkv], [], 0)
     packed_all = packed_all.T
+    up_all = gathered(after(w_up, gate_all), SHARE, 0)
     qkv_mine = packed_all[:columns]
     attn_gain_all = packed_all[columns].astype(f32)
     ffn_gain_all = packed_all[columns + 1].astype(f32)
-    out_t = jnp.concatenate(list(spread(w_out.T)), axis=1)
-    qkv_t = jnp.concatenate(list(spread(after(w_qkv, gate_all))), axis=1)
-    down_all = gathered(after(w_down.T, gate_all), SHARE, 0)
-    out_all = gathered(after(out_t, gate_all), SHARE, 0)
 
     tokens_in = layer_input.reshape(rows, width)
     cot = cotangent.reshape(rows, width)
@@ -570,7 +722,7 @@
     cos, sin = rope_tables(my_pos)
     gains = qk_gain.T
     queries, kv_mine = prep(joint, cos, sin, gains, heads, 512)
-    kv = both_halves(kv_mine)
+    (kv,) = plane_gather([], [], [kv_mine], 1)
     chunk_rows = rows // CHUNKS
     part_rows = chunk_rows // ways
     chunks = [slice(c * chunk_rows, (c + 1) * chunk_rows) for c in range(CHUNKS)]
@@ -581,13 +733,14 @@
     keys = (group_pos, group_seg)
     attended, log_total, attended_all = [], [], []
     for c in range(CHUNKS):
-        arrived = (down_all,) if c == 0 else (out_all,)
         result, total = attention(
-            start + c * chunk_rows, group_seg, after(queries, *arrived), kv, my_pos, my_seg, *keys, QUERY_BLOCK, KEY_BLOCK, c, CHUNKS
+            start + c * chunk_rows, group_seg, after(queries, up_all) if c else queries, kv, my_pos, my_seg, *keys, QUERY_BLOCK, KEY_BLOCK, c, CHUNKS
         )
         attended.append(result)
         log_total.append(total)
         attended_all.append(gathered(result, "tensor", 0))
+
+    out_all, down_all = plane_gather([after(out_t, *attended), w_down.T], [], [], 5)
 
     resid_parts, normed_ffns, acts, gate_grads, up_grads, ffn_in_grads = [], [], [], [], [], []
     previous = attended[-1]
@@ -611,9 +764,7 @@
     act, gate_grad, up_grad, _ = lax.optimization_barrier((act, gate_grad, up_grad, previous))
     ffn_part = dot_nt(act, down_all).astype(bf16)
     grad_down = dot_tn(cot, act).astype(bf16)
-    grad_gate = dot_tn(normed_ffn, gate_grad).astype(bf16)
-    grad_up = dot_tn(normed_ffn, up_grad).astype(bf16)
-    (qkv_all,) = plane_gather([after(qkv_t, ffn_part, grad_down, grad_gate, grad_up)], 1)
+    (qkv_all,) = plane_gather([after(qkv_t, ffn_part, grad_down)], [], [], 4)
     ffn_gain_part, resid_grads, attended_grads, attended_parts, branches = 0.0, [], [], [], []
     for c in range(CHUNKS):
         norm_grad, gain_part = norm_back(ffn_in_grads[c], resid_parts[c], ffn_gain_all)
@@ -622,13 +773,10 @@
         branch = resid_grad.astype(bf16)
         resid_grads.append(resid_grad)
         branches.append(branch)
-        attended_grad = dot_nn(branch, out_all).astype(bf16)
-        attended_grad = swap(jnp.stack(jnp.split(attended_grad, ways, axis=1)))
-        attended_grads.append(attended_grad.reshape(chunk_rows, -1))
+        attended_grads.append(dot_nn(branch, out_all).astype(bf16))
         attended_parts.append(lax.dynamic_slice_in_dim(attended_all[c], mine * part_rows, part_rows, 1))
 
-    attended_grad = jnp.concatenate(attended_grads, axis=0)
-    attended_grad = after(attended_grad, qkv_all)
+    attended_grad = to_heads(after(jnp.concatenate(attended_grads, axis=0), qkv_all), CHUNKS, 2)
     branch, attended_part = jnp.concatenate(branches, axis=0), jnp.concatenate(attended_parts, axis=1)
     grad_out = lax.dot_general(branch, attended_part, (((0,), (1,)), ((), ())), preferred_element_type=f32)
     grad_out = halving_scatter(grad_out.astype(bf16), SHARE)
@@ -637,18 +785,24 @@
         start, group_seg, queries, kv, jnp.concatenate(attended, axis=1), attended_grad, jnp.concatenate(log_total, axis=1),
         my_pos, my_seg, *keys, QUERY_BLOCK, KEY_BLOCK
     )
-    kv_grad = halving_scatter(kv_grad_group, ("context",))
-    ffn_part = after(ffn_part, attended_grad)
     ffn_sums = [scattered(ffn_part[chunk], "tensor", 0).astype(f32) for chunk in chunks]
-    joint_grad, qk_part = unprep(joint, cos, sin, gains, query_grad, kv_grad, heads, 512)
-    tokens = joint_grad.reshape(columns, CHUNKS, ways, part_rows)
-    joint_grad_part = swap(jnp.stack([tokens[:, :, i].reshape(columns, -1) for i in range(ways)]))
-    in_grad = natural(dot_tt(joint_grad_part.reshape(ways * columns, -1), qkv_all))
-    grad_qkv = dot_nn(joint_grad, normed_low)
-    attn_gain_part = jnp.sum(qkv_mine.astype(f32) * grad_qkv, axis=0) / attn_gain_all
+    if lax.axis_size("context") == 2:
+        joint_grad, joint_grad_part, qk_part = joint_tail(
+            joint, cos, sin, gains, query_grad, kv_grad_group, heads, CHUNKS, 3
+        )
+    else:
+        kv_grad = halving_scatter(kv_grad_group, ("context",))
+        joint_grad, qk_part = unprep(joint, cos, sin, gains, query_grad, kv_grad, heads, 512)
+        tokens = joint_grad.reshape(columns, CHUNKS, ways, part_rows)
+        joint_grad_part = swap(jnp.stack([tokens[:, :, i].reshape(columns, -1) for i in range(ways)]))
+        joint_grad_part = joint_grad_part.reshape(ways * columns, -1)
+    in_grad = natural(dot_tt(joint_grad_part, qkv_all))
     own_inputs = jnp.concatenate([own_rows(tokens_in, c) for c in range(CHUNKS)], axis=0).astype(f32)
     norm_grad = norm_back(in_grad, own_inputs, attn_gain_all)[0]
     grad_input = (jnp.concatenate(resid_grads, axis=0) + norm_grad).astype(bf16)
+    gate_grad, up_grad, joint_late, _ = lax.optimization_barrier((gate_grad, up_grad, joint_grad, grad_input))
+    grad_gate = dot_tn(normed_ffn, gate_grad).astype(bf16)
+    grad_up = dot_tn(normed_ffn, up_grad).astype(bf16)
     layer_output = [
         (after(part, query_grad) + ffn_sum).astype(bf16) for part, ffn_sum in zip(resid_parts, ffn_sums, strict=True)
     ]
@@ -659,6 +813,8 @@
     layer_output = all_rows([after(part, grad_input) for part in layer_output])
     grad_input = all_rows(jnp.split(grad_input, CHUNKS, axis=0))
 
+    grad_qkv = dot_nn(joint_late, normed_low)
+    attn_gain_part = jnp.sum(qkv_mine.astype(f32) * grad_qkv, axis=0) / attn_gain_all
     qk_rows = jnp.tile(qk_part.T, (1, width // HEAD_DIM))
     grad_qkv = jnp.concatenate(
         [grad_qkv, attn_gain_part[None], ffn_gain_part[None], qk_rows, jnp.zeros((12, width), f32)], axis=0

time: 1030 us -> 992 us (0.963)
  Pallas kernels: 167 us -> 385 us
  waiting for transfers between devices: 317 us -> 170 us
  starting transfers between devices: 96.1 us -> 32.1 us
  local copies, waits for them, and re-layouts: 121 us -> 91.6 us
    pallas_call x3 -> x6, Pallas kernels: 98.8 us -> 316 us  [the longest x4 161 us: plane_gather(): pl.pallas_call(functools.partial(gather_kernel, len(parts), len(lines), l...]
    ppermute x12 -> x3, waiting for transfers between devices: 75.3 us -> 5.07 us  [swap(): lax.ppermute(sent, 'tensor', [(i, (i + step) % ways) for i in range(ways)])]
    ppermute x16 -> x15, starting transfers between devices: 50.9 us -> 12.5 us  [halving_scatter(): got = lax.ppermute(sent, axis, [(i, i ^ stride) for i in range(size)])]
    all_gather x6 -> x5, waiting for transfers between devices: 104 us -> 71.7 us  [gathered(): return lax.all_gather(part, axes, axis=axis, tiled=True)]
    ppermute x16 -> x15, waiting for transfers between devices: 114 us -> 89.7 us  [halving_scatter(): got = lax.ppermute(sent, axis, [(i, i ^ stride) for i in range(size)])]
    ppermute x7 -> x0, waiting for transfers between devices: 22.6 us -> none  [the longest x6 11.7 us: spread(): lax.ppermute(part, 'tensor', [(i, (i + step) % ways) for i in range(ways)])]
    ppermute x7 -> x0, starting transfers between devices: 11.7 us -> none  [the longest x6 11.1 us: spread(): lax.ppermute(part, 'tensor', [(i, (i + step) % ways) for i in range(ways)])]
    ppermute x12 -> x3, starting transfers between devices: 26.4 us -> 15.6 us  [swap(): lax.ppermute(sent, 'tensor', [(i, (i + step) % ways) for i in range(ways)])]
  transfers between devices with their start and end apart: 48 -> 30, of which waited for: 25 -> 10; matrix products, arithmetic and copies ran while one was open for 37% -> 35% of each run, Pallas kernels for 11% -> 35%
where the time goes in v4:
time: 992 us; the launch traced here: 981 us
  Pallas kernels  385 us (39%)
  matrix products  210 us (21%)
  waiting for transfers between devices  170 us (17%)
  local copies, waits for them, and re-layouts  91.6 us (9%)
  other arithmetic  77 us (8%)
  starting transfers between devices  32.1 us (3%)
  between operations  15.3 us (2%)
    pallas_call x4, Pallas kernels, plane_gather(): pl.pallas_call(functools.partial(gather_kernel, len(parts), len(lines), l...  161 us
    pallas_call x1, Pallas kernels, joint_tail(): pl.pallas_call(functools.partial(tail_kernel, heads, ways, chunks), out_s...  110 us
    ppermute x15, waiting for transfers between devices, halving_scatter(): got = lax.ppermute(sent, axis, [(i, i ^ stride) for i in range(size)])  89.7 us
    dot_general x9, matrix products, dot_nn(): lax.dot_general(a, b, (((1,), (0,)), ((), ())), preferred_element_type=f32)  76.6 us
    all_gather x5, waiting for transfers between devices, gathered(): return lax.all_gather(part, axes, axis=axis, tiled=True)  71.7 us
    dot_general x6, matrix products, dot_nt(): lax.dot_general(a, b, (((1,), (1,)), ((), ())), preferred_element_type=f32)  59.5 us
    pallas_call x1, Pallas kernels, to_heads(): pl.pallas_call(functools.partial(heads_kernel, ways, chunks), out_shape=j...  45.2 us
    dot_general x3, matrix products, dot_tn(): lax.dot_general(a, b, (((0,), (0,)), ((), ())), preferred_element_type=f32)  44.1 us
  transfers between devices with their start and end apart: 30, of which 10 were waited for; matrix products, arithmetic and copies ran while one was open for 35% of the time, Pallas kernels for 35%

profile of v4, /device:TPU:0, one launch (start us, length us, event | category | flops | bytes accessed | tf_op | source)
XLA Modules:
  0.0 981.0 jit_solution(9502827126581105445)
XLA Ops:
  12.2 40.6 %plane_gather.4 = (bf16[2048,400]{1,0:T(8,128)(2,1)}, bf16[2048,1280]{1,0:T(8,128)(2,1)}, bf16[256,1024]{1,0:T(8,128)(2,1)}, bf16[256,1536]{1,0:T(8,128)(2,1)}) custom-call(bf16[256,400]{1,0:T(8,128)(2,1)} %maximum_bitcast_fusion.refs_0_, bf16[256,1280]{1,0:T(8,128)(2,1)} %refs_1_.1, bf16[256,256]{1,0:T(8,128)(2,1)} %bitcast.230, bf16[256,384]{1,0:T(8,128)(2,1)} %refs_3_.1), custom_call_target="tpu_custom_call" | custom-call | tf_op jit(solution)/shard_map/plane_gather/pallas_call | solution.py:555
  74.0 27.3 %plane_gather.5.kv_ref = bf16[4096,128]{1,0:T(8,128)(2,1)} custom-call(bf16[2048,128]{1,0:T(8,128)(2,1)} %get-tuple-element.48.refs_0_), custom_call_target="tpu_custom_call" | custom-call | tf_op jit(solution)/shard_map/plane_gather/pallas_call | solution.py:555
  104.0 9.4 attend.2
  120.9 14.2 %attend.3 = (bf16[256,1024]{1,0:T(8,128)(2,1)}, f32[4,1024]{1,0:T(4,128)}) custom-call(s32[1]{0:T(128)S(6)} %add.320.start_ref, s32[4096]{0:T(1024)} %bitcast.238, bf16[256,2048]{1,0:T(8,128)(2,1)} %get-tuple-element.52.q_ref, bf16[4096,128]{1,0:T(8,128)(2,1)} %plane_gather.5.kv_ref, s32[2048,1]{1,0:T(8,128)} %copy.85.qpos_ref, s32[2048,1]{1,0:T(8,128)} %copy.86.qseg_ref, ...), custom_call_target="tpu_custom_call" | custom-call | flops 4294967296 | bytes 4194304 | tf_op jit(solution)/shard_map/attend/pallas_call | solution.py:198
  135.1 60.6 %plane_gather.6 = (bf16[2048,1024]{1,0:T(8,128)(2,1)}, bf16[2048,1280]{1,0:T(8,128)(2,1)}) custom-call(bf16[256,1024]{1,0:T(8,128)(2,1)} %get-tuple-element.56.refs_0_, bf16[256,1280]{1,0:T(8,128)(2,1)} %bitcast.227), custom_call_target="tpu_custom_call" | custom-call | tf_op jit(solution)/shard_map/plane_gather/pallas_call | solution.py:555
  195.8 10.5 %fusion.75 = f32[1024,1280]{1,0:T(8,128)} fusion(bf16[1024,2048]{1,0:T(8,128)(2,1)} %get-tuple-element.54, bf16[2048,1280]{1,0:T(8,128)(2,1)} %get-tuple-element.57), kind=kOutput, calls=%fused_computation.193 | convolution fusion | flops 5368709120 | bytes 14680064 | tf_op jit(solution)/shard_map/dot_general | solution.py:21
  206.3 9.1 multiply_reduce_fusion.1
  226.1 11.6 %multiply_convert_fusion.3 = (bf16[1024,1280]{1,0:T(8,128)(2,1)S(1)}, bf16[1024,1280]{1,0:T(8,128)(2,1)S(1)}, bf16[1024,1280]{1,0:T(8,128)(2,1)S(1)}) fusion(f32[1024,1280]{1,0:T(8,128)} %fusion.76, f32[1024,1280]{1,0:T(8,128)} %fusion.75, bf16[1024,2048]{1,0:T(8,128)(2,1)S(1)} %multiply_convert_fusion.1, bf16[2048,1280]{1,0:T(8,128)(2,1)} %all-gather.8.cloned.1.call-done), kind=kOutput, calls=%fused_computation.41 | convolution fusion | flops 5389680640 | bytes 27787264 | tf_op jit(solution)/shard_map/dot_general | solution.py:21
  237.7 9.5 fusion.77
  247.2 9.8 add_convert_fusion.1
  257.1 11.4 %fusion.78 = f32[1024,1280]{1,0:T(8,128)} fusion(bf16[1024,2048]{1,0:T(8,128)(2,1)} %get-tuple-element.60, bf16[2048,1280]{1,0:T(8,128)(2,1)} %get-tuple-element.57), kind=kOutput, calls=%fused_computation.196 | convolution fusion | flops 5368709120 | bytes 14680064 | tf_op jit(solution)/shard_map/dot_general | solution.py:21
  280.9 11.3 %fusion.79 = f32[1024,1280]{1,0:T(8,128)} fusion(bf16[1024,2048]{1,0:T(8,128)(2,1)S(1)} %multiply_convert_fusion, bf16[2048,1280]{1,0:T(8,128)(2,1)} %get-tuple-element.50), kind=kOutput, calls=%fused_computation.197 | convolution fusion | flops 5368709120 | bytes 14680064 | tf_op jit(solution)/shard_map/dot_general | solution.py:21
  292.2 12.8 %multiply_convert_fusion.2 = (bf16[1024,1280]{1,0:T(8,128)(2,1)}, bf16[1024,1280]{1,0:T(8,128)(2,1)S(1)}, bf16[1024,1280]{1,0:T(8,128)(2,1)S(1)}) fusion(f32[1024,1280]{1,0:T(8,128)} %fusion.79, f32[1024,1280]{1,0:T(8,128)} %fusion.78, bf16[1024,2048]{1,0:T(8,128)(2,1)S(1)} %multiply_convert_fusion, bf16[2048,1280]{1,0:T(8,128)(2,1)} %all-gather.8.cloned.1.call-done), kind=kOutput, calls=%fused_computation.40 | convolution fusion | flops 5389680640 | bytes 27787264 | tf_op jit(solution)/shard_map/dot_general | solution.py:21
  304.9 9.5 fusion.80
  314.4 9.8 add_convert_fusion
  333.0 15.3 %convolution_convert_fusion = bf16[2048,2048]{1,0:T(8,128)(2,1)S(1)} fusion(bf16[2048,1280]{1,0:T(8,128)(2,1)S(1)} %pad_maximum_fusion.3, bf16[2048,1280]{1,0:T(8,128)(2,1)} %get-tuple-element.57), kind=kOutput, calls=%fused_computation.19 | convolution fusion | flops 10741612544 | bytes 18874368 | tf_op jit(solution)/shard_map/dot_general | solution.py:18
  362.6 16.8 %fusion.8 = bf16[2048,1280]{0,1:T(8,128)(2,1)} fusion(bf16[2048,1280]{1,0:T(8,128)(2,1)} %copy-done.10, bf16[1,2048,2048]{2,1,0:T(8,128)(2,1)} %param.13), kind=kOutput, calls=%fused_computation.22 | convolution fusion | flops 10740039680 | bytes 18874368 | tf_op jit(solution)/shard_map/dot_general | solution.py:24
  379.5 32.8 %plane_gather.7 = bf16[2048,1536]{1,0:T(8,128)(2,1)} custom-call(bf16[256,1536]{1,0:T(8,128)(2,1)} %get-tuple-element.64.refs_0_), custom_call_target="tpu_custom_call" | custom-call | tf_op jit(solution)/shard_map/plane_gather/pallas_call | solution.py:555
  427.9 45.2 %to_heads.1.do_ref = bf16[2048,256]{1,0:T(8,128)(2,1)} custom-call(bf16[512,1024]{1,0:T(8,128)(2,1)} %pad_maximum_fusion.10.grad_ref), custom_call_target="tpu_custom_call" | custom-call | tf_op jit(solution)/shard_map/to_heads/pallas_call | solution.py:592
  473.1 41.0 %attend_grad.1 = (f32[256,2048]{1,0:T(8,128)}, bf16[4096,128]{1,0:T(8,128)(2,1)}) custom-call(s32[1]{0:T(128)} %bitcast.1.start_ref, s32[4096]{0:T(1024)} %bitcast.240, bf16[256,2048]{1,0:T(8,128)(2,1)} %get-tuple-element.52.q_ref, bf16[4096,128]{1,0:T(8,128)(2,1)} %plane_gather.5.kv_ref, bf16[256,2048]{1,0:T(8,128)(2,1)} %pad_maximum_fusion.9.o_ref, ...), custom_call_target="tpu_custom_call" | custom-call | flops 21474836480 | bytes 8388608 | tf_op jit(solution)/shard_map/attend_grad/pallas_call | solution.py:315
  514.1 109.7 %joint_tail.1 = (bf16[384,2048]{1,0:T(8,128)(2,1)}, bf16[1536,512]{1,0:T(8,128)(2,1)}, f32[64,2]{1,0:T(8,128)}) custom-call(f32[384,2048]{1,0:T(8,128)} %fusion.37.joint_ref, f32[32,2048]{1,0:T(8,128)} %get-tuple-element.168.cos_ref, f32[32,2048]{1,0:T(8,128)} %get-tuple-element.167.sin_ref, f32[64,2]{1,0:T(8,128)} %bitcast.232, ...), custom_call_target="tpu_custom_call" | custom-call | tf_op jit(solution)/shard_map/joint_tail/pallas_call | solution.py:667
  623.8 9.5 fusion.24
  645.8 9.8 %reshape_reshape.19 = bf16[2,2,2,256,1280]{3,2,1,0,4:T(2,128)(2,1)} reshape(bf16[2048,1280]{0,1:T(8,128)(2,1)} %fusion.8) | data formatting | bytes 10485760 | tf_op jit(solution)/shard_map/reshape;reshape | solution.py:401
  678.0 25.7 %collective-permute-done.19 = bf16[1,2,256,1280]{2,3,1,0:T(8,128)(2,1)} collective-permute-done((bf16[1,2,256,1280]{2,3,1,0:T(8,128)(2,1)}, bf16[1,2,256,1280]{2,3,1,0:T(8,128)(2,1)}, u32[]{:S(2)}, u32[]{:S(2)}) %collective-permute-start.19) | collective-permute-done | bytes 1310752 | tf_op jit(solution)/shard_map/ppermute | solution.py:406
  708.8 9.2 fusion.74
  736.3 15.4 %convolution_convert_fusion.2 = bf16[2048,1280]{1,0:T(8,128)(2,1)S(1)} fusion(bf16[2048,1280]{1,0:T(8,128)(2,1)} %pad_maximum_fusion.4, bf16[1024,2048]{1,0:T(8,128)(2,1)} %copy-done.16, bf16[1024,2048]{1,0:T(8,128)(2,1)} %copy-done.14), kind=kOutput, calls=%fused_computation.21 | convolution fusion | flops 10756816896 | bytes 18874368 | tf_op jit(solution)/shard_map/dot_general | solution.py:24
  758.0 11.9 %convolution_convert_fusion.1 = bf16[2048,1280]{1,0:T(8,128)(2,1)S(1)} fusion(bf16[2048,1280]{1,0:T(8,128)(2,1)S(1)} %bitcast.209, bf16[1024,2048]{1,0:T(8,128)(2,1)S(1)} %copy-done.17, bf16[1024,2048]{1,0:T(8,128)(2,1)S(1)} %copy-done.15), kind=kOutput, calls=%fused_computation.20 | convolution fusion | flops 10756816896 | bytes 18874368 | tf_op jit(solution)/shard_map/dot_general | solution.py:24
  796.4 17.0 %collective-permute-done.4 = bf16[1,2,256,1024]{3,2,1,0:T(8,128)(2,1)S(1)} collective-permute-done((bf16[1,2,256,1024]{3,2,1,0:T(8,128)(2,1)S(1)}, bf16[1,2,256,1024]{3,2,1,0:T(8,128)(2,1)S(1)}, u32[]{:S(2)}, u32[]{:S(2)}) %collective-permute-start.4) | collective-permute-done | bytes 1048608 | tf_op jit(solution)/shard_map/ppermute | solution.py:406
  833.5 11.2 %collective-permute-start.7 = (bf16[256,256]{0,1:T(8,128)(2,1)S(1)}, bf16[256,256]{0,1:T(8,128)(2,1)S(1)}, u32[]{:S(2)}, u32[]{:S(2)}) collective-permute-start(bf16[256,256]{0,1:T(8,128)(2,1)S(1)} %get-tuple-element.159), channel_id=1, source_target_pairs={{0,2},{1,3},{2,0},{3,1},{4,6},{5,7},{6,4},{7,5},{8,10},{9,11},{10,... | collective-permute-start | bytes 393224 | tf_op jit(solution)/shard_map/ppermute | solution.py:434
  845.4 21.8 %collective-permute-done.16 = bf16[1,2,256,1280]{3,2,1,0:T(8,128)(2,1)S(1)} collective-permute-done((bf16[1,2,256,1280]{3,2,1,0:T(8,128)(2,1)S(1)}, bf16[1,2,256,1280]{3,2,1,0:T(8,128)(2,1)S(1)}, u32[]{:S(2)}, u32[]{:S(2)}) %collective-permute-start.16) | collective-permute-done | bytes 1310752 | tf_op jit(solution)/shard_map/ppermute | solution.py:406
  872.2 11.2 %collective-permute-done.17 = bf16[1,1,256,1280]{3,2,1,0:T(8,128)(2,1)} collective-permute-done((bf16[1,1,256,1280]{3,2,1,0:T(8,128)(2,1)}, bf16[1,1,256,1280]{3,2,1,0:T(8,128)(2,1)}, u32[]{:S(2)}, u32[]{:S(2)}) %collective-permute-start.17) | collective-permute-done | bytes 655392 | tf_op jit(solution)/shard_map/ppermute | solution.py:406
  885.6 71.7 %all-gather.14.cloned.1.call-done = bf16[2,1024,2048]{2,1,0:T(8,128)(2,1)} async-done(((bf16[2,256,2048]{2,1,0:T(8,128)(2,1)}), bf16[2,1024,2048]{2,1,0:T(8,128)(2,1)}) %all-gather.14.cloned.1.call-update) | async-done | bytes 8388624 | tf_op jit(solution)/shard_map/all_gather | solution.py:378
  (312 shorter events, 233.2 us)
Async XLA Ops:
  7.2 113.7 %all-gather.8.cloned.1.call-start = ((), (), s32[]{:S(2)}) async-start(), calls=%async_computation.5 | async-start | bytes 5898240 | tf_op jit(solution)/shard_map/all_gather | solution.py:378
  52.8 153.4 %all-gather.6.cloned.1.call-start = ((), (), s32[]{:S(2)}) async-start(), calls=%async_computation.4 | async-start | bytes 2621440 | tf_op jit(solution)/shard_map/all_gather | solution.py:378
  62.1 40.6 %copy-start.47 = (s32[1,2048]{1,0:T(1,128)}, s32[1,2048]{1,0:T(1,128)S(1)}, u32[]{:S(2)}) copy-start(s32[1,2048]{1,0:T(1,128)S(1)} %get-tuple-element.179.qseg_ref) | copy-start | bytes 24580
  113.4 155.0 %all-gather.10.cloned.1.call-start = ((), (), s32[]{:S(2)}) async-start(), calls=%async_computation.7 | async-start | bytes 2621440 | tf_op jit(solution)/shard_map/all_gather | solution.py:378
  135.1 280.3 %reduce-scatter.5.cloned.1.call-start = ((), (), s32[]{:S(2)}) async-start(), calls=%async_computation.6 | async-start | bytes 5242880 | tf_op jit(solution)/shard_map/reduce_scatter | solution.py:382
  257.0 158.4 %reduce-scatter.7.cloned.1.call-start = ((), (), s32[]{:S(2)}) async-start(), calls=%async_computation.8 | async-start | bytes 5242880 | tf_op jit(solution)/shard_map/reduce_scatter | solution.py:382
  324.2 309.1 %reduce-scatter.11.cloned.1.call-start = ((), (), s32[]{:S(2)}) async-start(), calls=%async_computation.10 | async-start | bytes 5242880 | tf_op jit(solution)/shard_map/reduce_scatter | solution.py:382
  351.8 290.8 %reduce-scatter.9.cloned.1.call-start = ((), (), s32[]{:S(2)}) async-start(), calls=%async_computation.9 | async-start | bytes 5242880 | tf_op jit(solution)/shard_map/reduce_scatter | solution.py:382
  362.6 523.0 %all-gather.12.cloned.1.call-start = ((), (), s32[]{:S(2)}) async-start(), calls=%async_computation.11 | async-start | bytes 10485760 | tf_op jit(solution)/shard_map/all_gather | solution.py:378
  514.1 109.7 %copy-start.45 = (f32[2048]{0:T(1024)S(1)}, f32[2048]{0:T(1024)}, u32[]{:S(2)}) copy-start(f32[2048]{0:T(1024)} %copy-done.44) | copy-start | bytes 24580
  645.8 311.6 %all-gather.14.cloned.1.call-start = ((), (), s32[]{:S(2)}) async-start(), calls=%async_computation.12 | async-start | bytes 10485760 | tf_op jit(solution)/shard_map/all_gather | solution.py:378
  663.2 5.1 collective-permute-start.18
  672.4 31.3 %collective-permute-start.19 = (bf16[1,2,256,1280]{2,3,1,0:T(8,128)(2,1)}, bf16[1,2,256,1280]{2,3,1,0:T(8,128)(2,1)}, u32[]{:S(2)}, u32[]{:S(2)}) collective-permute-start(bf16[1,2,256,1280]{2,3,1,0:T(8,128)(2,1)} %constant_dynamic-slice_fusion.1), channel_id=1, source_target_pairs={{0,16},{8,24},{16,0},{24,8},{1,17},{9,25},{17,1},{25,9},{2,18},{10... | collective-permute-start | bytes 3932168 | tf_op jit(solution)/shard_map/ppermute | solution.py:406
  707.3 65.5 %collective-permute-start.20 = (bf16[1,1,256,1280]{2,3,1,0:T(8,128)(2,1)}, bf16[1,1,256,1280]{2,3,1,0:T(8,128)(2,1)}, u32[]{:S(2)}, u32[]{:S(2)}) collective-permute-start(bf16[1,1,256,1280]{2,3,1,0:T(8,128)(2,1)} %constant_dynamic-slice_fusion), channel_id=1, source_target_pairs={{0,4},{4,0},{1,5},{5,1},{2,6},{6,2},{3,7},{7,3},{8,12},{12,8},{9,1... | collective-permute-start | bytes 1966088 | tf_op jit(solution)/shard_map/ppermute | solution.py:406
  728.8 25.1 %collective-permute-start = (bf16[2,2,256,400]{2,3,1,0:T(8,128)(2,1)S(1)}, bf16[2,2,256,400]{2,3,1,0:T(8,128)(2,1)S(1)}, u32[]{:S(2)}, u32[]{:S(2)}) collective-permute-start(bf16[2,2,256,400]{2,3,1,0:T(8,128)(2,1)S(1)} %bitcast.228), channel_id=1, source_target_pairs={{0,8},{8,0},{16,24},{24,16},{1,9},{9,1},{17,25},{25,17},{2,10},{10... | collective-permute-start | bytes 2457608 | tf_op jit(solution)/shard_map/ppermute | solution.py:406
  732.9 50.8 %collective-permute-start.3 = (bf16[2,2,256,1024]{3,2,1,0:T(8,128)(2,1)}, bf16[2,2,256,1024]{3,2,1,0:T(8,128)(2,1)}, u32[]{:S(2)}, u32[]{:S(2)}) collective-permute-start(bf16[2,2,256,1024]{3,2,1,0:T(8,128)(2,1)} %dynamic-slice_bitcast_fusion.2), channel_id=1, source_target_pairs={{0,8},{8,0},{16,24},{24,16},{1,9},{9,1},{17,25},{25,17},{2,10},{10... | collective-permute-start | bytes 6291464 | tf_op jit(solution)/shard_map/ppermute | solution.py:406
  753.4 38.8 %collective-permute-start.12 = (bf16[2,2,256,1280]{3,2,1,0:T(8,128)(2,1)}, bf16[2,2,256,1280]{3,2,1,0:T(8,128)(2,1)}, u32[]{:S(2)}, u32[]{:S(2)}) collective-permute-start(bf16[2,2,256,1280]{3,2,1,0:T(8,128)(2,1)} %dynamic-slice_bitcast_fusion.1), channel_id=1, source_target_pairs={{0,8},{8,0},{16,24},{24,16},{1,9},{9,1},{17,25},{25,17},{2,10},{10... | collective-permute-start | bytes 7864328 | tf_op jit(solution)/shard_map/ppermute | solution.py:406
  755.6 16.4 %collective-permute-start.1 = (bf16[1,2,256,400]{2,3,1,0:T(8,128)(2,1)S(1)}, bf16[1,2,256,400]{2,3,1,0:T(8,128)(2,1)S(1)}, u32[]{:S(2)}, u32[]{:S(2)}) collective-permute-start(bf16[1,2,256,400]{2,3,1,0:T(8,128)(2,1)S(1)} %constant_dynamic-slice_fusion.13), channel_id=1, source_target_pairs={{0,16},{8,24},{16,0},{24,8},{1,17},{9,25},{17,1},{25,9},{2,18},{10... | collective-permute-start | bytes 1228808 | tf_op jit(solution)/shard_map/ppermute | solution.py:406
  771.6 42.8 %collective-permute-start.15 = (bf16[2,2,256,1280]{3,2,1,0:T(8,128)(2,1)}, bf16[2,2,256,1280]{3,2,1,0:T(8,128)(2,1)}, u32[]{:S(2)}, u32[]{:S(2)}) collective-permute-start(bf16[2,2,256,1280]{3,2,1,0:T(8,128)(2,1)} %dynamic-slice_bitcast_fusion), channel_id=1, source_target_pairs={{0,8},{8,0},{16,24},{24,16},{1,9},{9,1},{17,25},{25,17},{2,10},{10... | collective-permute-start | bytes 7864328 | tf_op jit(solution)/shard_map/ppermute | solution.py:406
  772.2 7.1 collective-permute-start.2
  779.4 7.8 collective-permute-start.11
  782.2 9.4 collective-permute-start.10
  783.7 7.9 collective-permute-start.9
  787.2 26.2 %collective-permute-start.4 = (bf16[1,2,256,1024]{3,2,1,0:T(8,128)(2,1)S(1)}, bf16[1,2,256,1024]{3,2,1,0:T(8,128)(2,1)S(1)}, u32[]{:S(2)}, u32[]{:S(2)}) collective-permute-start(bf16[1,2,256,1024]{3,2,1,0:T(8,128)(2,1)S(1)} %constant_dynamic-slice_fusion.9), channel_id=1, source_target_pairs={{0,16},{8,24},{16,0},{24,8},{1,17},{9,25},{17,1},{25,9},{2,18},{10... | collective-permute-start | bytes 3145736 | tf_op jit(solution)/shard_map/ppermute | solution.py:406
  795.0 50.0 %collective-permute-start.13 = (bf16[1,2,256,1280]{3,2,1,0:T(8,128)(2,1)S(1)}, bf16[1,2,256,1280]{3,2,1,0:T(8,128)(2,1)S(1)}, u32[]{:S(2)}, u32[]{:S(2)}) collective-permute-start(bf16[1,2,256,1280]{3,2,1,0:T(8,128)(2,1)S(1)} %constant_dynamic-slice_fusion.7), channel_id=1, source_target_pairs={{0,16},{8,24},{16,0},{24,8},{1,17},{9,25},{17,1},{25,9},{2,18},{10... | collective-permute-start | bytes 3932168 | tf_op jit(solution)/shard_map/ppermute | solution.py:406
  813.8 9.5 collective-permute-start.5
  817.0 50.3 %collective-permute-start.16 = (bf16[1,2,256,1280]{3,2,1,0:T(8,128)(2,1)S(1)}, bf16[1,2,256,1280]{3,2,1,0:T(8,128)(2,1)S(1)}, u32[]{:S(2)}, u32[]{:S(2)}) collective-permute-start(bf16[1,2,256,1280]{3,2,1,0:T(8,128)(2,1)S(1)} %constant_dynamic-slice_fusion.5), channel_id=1, source_target_pairs={{0,16},{8,24},{16,0},{24,8},{1,17},{9,25},{17,1},{25,9},{2,18},{10... | collective-permute-start | bytes 3932168 | tf_op jit(solution)/shard_map/ppermute | solution.py:406
  823.6 9.8 %collective-permute-start.6 = (bf16[256,256]{0,1:T(8,128)(2,1)S(1)}, bf16[256,256]{0,1:T(8,128)(2,1)S(1)}, u32[]{:S(2)}, u32[]{:S(2)}) collective-permute-start(bf16[256,256]{0,1:T(8,128)(2,1)S(1)} %dynamic-slice_bitcast_fusion.7), channel_id=1, source_target_pairs={{0,1},{1,2},{2,3},{3,0},{4,5},{5,6},{6,7},{7,4},{8,9},{9,10},{10,1... | collective-permute-start | bytes 393224 | tf_op jit(solution)/shard_map/ppermute | solution.py:434
  833.5 35.5 %collective-permute-start.7 = (bf16[256,256]{0,1:T(8,128)(2,1)S(1)}, bf16[256,256]{0,1:T(8,128)(2,1)S(1)}, u32[]{:S(2)}, u32[]{:S(2)}) collective-permute-start(bf16[256,256]{0,1:T(8,128)(2,1)S(1)} %get-tuple-element.159), channel_id=1, source_target_pairs={{0,2},{1,3},{2,0},{3,1},{4,6},{5,7},{6,4},{7,5},{8,10},{9,11},{10,... | collective-permute-start | bytes 393224 | tf_op jit(solution)/shard_map/ppermute | solution.py:434
  844.7 24.2 %collective-permute-start.8 = (bf16[256,256]{0,1:T(8,128)(2,1)S(1)}, bf16[256,256]{0,1:T(8,128)(2,1)S(1)}, u32[]{:S(2)}, u32[]{:S(2)}) collective-permute-start(bf16[256,256]{0,1:T(8,128)(2,1)S(1)} %get-tuple-element.158), channel_id=1, source_target_pairs={{0,3},{1,0},{2,1},{3,2},{4,7},{5,4},{6,5},{7,6},{8,11},{9,8},{10,9... | collective-permute-start | bytes 393224 | tf_op jit(solution)/shard_map/ppermute | solution.py:434
  845.3 24.6 %collective-permute-start.14 = (bf16[1,1,256,1280]{3,2,1,0:T(8,128)(2,1)S(1)}, bf16[1,1,256,1280]{3,2,1,0:T(8,128)(2,1)}, u32[]{:S(2)}, u32[]{:S(2)}) collective-permute-start(bf16[1,1,256,1280]{3,2,1,0:T(8,128)(2,1)S(1)} %constant_dynamic-slice_fusion.6), channel_id=1, source_target_pairs={{0,4},{4,0},{1,5},{5,1},{2,6},{6,2},{3,7},{7,3},{8,12},{12,8},{9,1... | collective-permute-start | bytes 1966088 | tf_op jit(solution)/shard_map/ppermute | solution.py:406
  868.5 14.9 %collective-permute-start.17 = (bf16[1,1,256,1280]{3,2,1,0:T(8,128)(2,1)}, bf16[1,1,256,1280]{3,2,1,0:T(8,128)(2,1)}, u32[]{:S(2)}, u32[]{:S(2)}) collective-permute-start(bf16[1,1,256,1280]{3,2,1,0:T(8,128)(2,1)} %constant_dynamic-slice_fusion.4), channel_id=1, source_target_pairs={{0,4},{4,0},{1,5},{5,1},{2,6},{6,2},{3,7},{7,3},{8,12},{12,8},{9,1... | collective-permute-start | bytes 1966088 | tf_op jit(solution)/shard_map/ppermute | solution.py:406
  (61 other events, 520.3 us)
Sparse Core Ops, SparseCore 0:
  52.9 50.5 all-gather.7
  113.6 52.8 all-gather.5
  168.0 44.3 all-gather.9
  257.1 73.5 reduce-scatter.4
  332.9 77.2 reduce-scatter.6
  412.4 94.0 reduce-scatter.10
  508.9 104.9 reduce-scatter.8
  645.9 150.9 all-gather.11
  798.4 158.8 all-gather.13

commit v5 on v4

--- a/solution.py
+++ b/solution.py
@@ -233,8 +233,8 @@
     return a, b, x - a - b
 
 
-def bwd_kernel(heads, bq, bk, start_ref, seg_ref, q_ref, kv_ref, o_ref, do_ref, l_ref, qpos_ref, qseg_ref, kpos_ref, kseg_ref,
-               dq_ref, dkv_ref, kaug, vaug, qst, dst, qs, ds, dacc, dkv):
+def bwd_kernel(heads, bq, bk, final, start_ref, seg_ref, q_ref, kv_ref, o_ref, do_ref, l_ref, qpos_ref, qseg_ref, kpos_ref, kseg_ref, *rest):
+    carried, (dq_ref, dkv_ref, kaug, vaug, qst, dst, qs, ds, dacc, dkv) = rest[:-10], rest[-10:]
     qi = pl.program_id(0)
     nk = kv_ref.shape[0] // bk
     D = HEAD_DIM
@@ -245,7 +245,7 @@
         kv = kv_ref[...].astype(f32)
         kaug[...] = jnp.where(lane < D, kv, jnp.where(lane < D + 3, -1.0, 0.0)).astype(bf16)
         vaug[...] = jnp.where(lane >= D, kv, jnp.where(lane < 3, -1.0, 0.0)).astype(bf16)
-        dkv[...] = jnp.zeros_like(dkv)
+        dkv[...] = carried[0][...] if carried else jnp.zeros_like(dkv)
 
     row = lax.broadcasted_iota(jnp.int32, (D, bq), 0)
 
@@ -303,20 +303,24 @@
     @pl.when(qi == pl.num_programs(0) - 1)
     def _():
         lane = lax.broadcasted_iota(jnp.int32, dkv.shape, 1)
-        dkv_ref[...] = (dkv[...] * jnp.where(lane < D, LN2, 1.0)).astype(bf16)
-
-
-def attention_grad(start, seg, q, kv, o, do, l, qpos, qseg, kpos, kseg, bq, bk):
+        scale = jnp.where(lane < D, LN2, 1.0) if final else 1.0
+        dkv_ref[...] = (dkv[...] * scale).astype(dkv_ref.dtype)
+
+
+def attention_grad(start, seg, q, kv, o, do, l, qpos, qseg, kpos, kseg, carried, bq, bk, part, parts):
     heads = q.shape[0] // HEAD_DIM
-    count, total = q.shape[1], kv.shape[0]
+    count, total = q.shape[1] // parts, kv.shape[0]
     bq, bk = min(bq, count), min(bk, total)
+    first = part * (count // bq)
+    final = part == parts - 1
     whole = lambda *shape: pl.BlockSpec(shape, lambda i, *_: (0,) * len(shape))
-    wide = pl.BlockSpec((q.shape[0], bq), lambda i, *_: (0, i))
+    wide = pl.BlockSpec((q.shape[0], bq), lambda i, *_: (0, i + first))
+    near = pl.BlockSpec((q.shape[0], bq), lambda i, *_: (0, i))
     return pl.pallas_call(
-        functools.partial(bwd_kernel, heads, bq, bk),
+        functools.partial(bwd_kernel, heads, bq, bk, final),
         out_shape=(
-            jax.ShapeDtypeStruct(q.shape, f32),
-            jax.ShapeDtypeStruct(kv.shape, bf16),
+            jax.ShapeDtypeStruct((q.shape[0], count), f32),
+            jax.ShapeDtypeStruct(kv.shape, bf16 if final else f32),
         ),
         grid_spec=pltpu.PrefetchScalarGridSpec(
             num_scalar_prefetch=2,
@@ -324,15 +328,16 @@
             in_specs=[
                 wide,
                 whole(*kv.shape),
-                wide,
-                pl.BlockSpec((bq, q.shape[0]), lambda i, *_: (i, 0)),
+                near,
+                pl.BlockSpec((bq, q.shape[0]), lambda i, *_: (i + first, 0)),
                 pl.BlockSpec((heads, bq), lambda i, *_: (0, i)),
-                pl.BlockSpec((1, bq), lambda i, *_: (0, i)),
-                pl.BlockSpec((1, bq), lambda i, *_: (0, i)),
+                pl.BlockSpec((1, bq), lambda i, *_: (0, i + first)),
+                pl.BlockSpec((1, bq), lambda i, *_: (0, i + first)),
                 whole(total, 1),
                 whole(total, 1),
-            ],
-            out_specs=(wide, whole(*kv.shape)),
+            ]
+            + [whole(*kv.shape)] * len(carried),
+            out_specs=(near, whole(*kv.shape)),
             scratch_shapes=[
                 pltpu.VMEM(kv.shape, bf16),
                 pltpu.VMEM(kv.shape, bf16),
@@ -346,7 +351,7 @@
         ),
         cost_estimate=pl.CostEstimate(flops=heads * count * total * 640, bytes_accessed=8 << 20, transcendentals=heads * count * total // 2),
         name="attend_grad",
-    )(start, seg, q, kv, o, do, l, qpos.reshape(1, -1), qseg.reshape(1, -1), kpos.reshape(-1, 1), kseg.reshape(-1, 1))
+    )(start, seg, q, kv, o, do, l, qpos.reshape(1, -1), qseg.reshape(1, -1), kpos.reshape(-1, 1), kseg.reshape(-1, 1), *carried)
 
 
 HEADS = 16
@@ -460,8 +465,8 @@
     return pl.ds(pl.multiple_of(start, size), size)
 
 
-def gather_kernel(count, lines, pairs, *refs):
-    arrays = count + lines + pairs
+def gather_kernel(count, lines, pairs, shuffles, chunks, *refs):
+    arrays = count + lines + pairs + shuffles
     sources, targets = refs[:arrays], refs[arrays : 2 * arrays]
     own_sem, send_sem, recv_sem = refs[2 * arrays : 2 * arrays + 3]
     dp, context = lax.axis_index("dp"), lax.axis_index("context")
@@ -472,7 +477,7 @@
         {"dp": dp + 1 - 2 * inner},
     )
     me, ways = lax.axis_index("tensor"), lax.axis_size("tensor")
-    peers = [{"tensor": lax.rem(me + step, ways)} for step in range(1, ways)] if lines else []
+    peers = [{"tensor": lax.rem(me + step, ways)} for step in range(1, ways)] if lines or shuffles else []
     greet(([across, along, beside] if count else [along]) + peers)
 
     def place(array, o, k, first=0, parts=1):
@@ -494,7 +499,18 @@
 
     copies, kept = {}, []
     passed = []
-    for a in range(count + lines, arrays):
+    for a in range(count + lines + pairs, arrays):
+        size, width = sources[a].shape[0] // chunks, sources[a].shape[1] // ways
+        for c in range(chunks):
+            rows = pl.ds(c * size, size)
+            target = targets[a].at[aligned((c * ways + me) * size, size), :]
+            for k, peer in enumerate(peers):
+                source = sources[a].at[rows, aligned(peer["tensor"] * width, width)]
+                passed.append(send(a, c * (ways - 1) + k, source, target, peer))
+            keep = pltpu.make_async_copy(sources[a].at[rows, aligned(me * width, width)], target, own_sem.at[a + c])
+            keep.start()
+            kept.append(keep)
+    for a in range(count + lines, count + lines + pairs):
         rows = sources[a].shape[0]
         mine = targets[a].at[aligned(context * rows, rows), :]
         passed.append(send(a, 0, sources[a], mine, along))
@@ -544,60 +560,32 @@
         copy.wait_send()
 
 
-def plane_gather(parts, lines, pairs, collective):
+def plane_gather(parts, lines, pairs, collective, shuffles=(), chunks=1):
     share, ways = lax.axis_size("dp") * lax.axis_size("context"), lax.axis_size("tensor")
     if (lax.axis_size("dp"), lax.axis_size("context")) != (4, 2):
         whole = [gathered(part, SHARE, 0) for part in parts] + [jnp.concatenate(list(spread(line)), axis=1) for line in lines]
-        return whole + [gathered(pair, "context", 0) for pair in pairs]
-    arrays = len(parts) + len(lines) + len(pairs)
+        whole += [gathered(pair, "context", 0) for pair in pairs]
+        for grad in shuffles:
+            blocks = grad.reshape(chunks, grad.shape[0] // chunks, ways, -1).transpose(2, 0, 1, 3)
+            whole.append(swap(blocks).transpose(1, 0, 2, 3).reshape(ways * grad.shape[0], -1))
+        return whole
+    arrays = len(parts) + len(lines) + len(pairs) + len(shuffles)
     shapes = [(share * part.shape[0], part.shape[1]) for part in parts] + [(line.shape[0], ways * line.shape[1]) for line in lines]
     shapes += [(2 * pair.shape[0], pair.shape[1]) for pair in pairs]
+    shapes += [(ways * grad.shape[0], grad.shape[1] // ways) for grad in shuffles]
     return pl.pallas_call(
-        functools.partial(gather_kernel, len(parts), len(lines), len(pairs)),
+        functools.partial(gather_kernel, len(parts), len(lines), len(pairs), len(shuffles), chunks),
         out_shape=tuple(jax.ShapeDtypeStruct(shape, bf16) for shape in shapes),
         in_specs=[pl.BlockSpec(memory_space=pltpu.VMEM)] * arrays,
         out_specs=(pl.BlockSpec(memory_space=pl.ANY),) * arrays,
         scratch_shapes=[
-            pltpu.SemaphoreType.DMA((arrays,)),
+            pltpu.SemaphoreType.DMA((arrays + chunks,)),
             pltpu.SemaphoreType.DMA((arrays, 9)),
             pltpu.SemaphoreType.DMA((arrays, 9)),
         ],
         compiler_params=pltpu.CompilerParams(collective_id=collective, has_side_effects=True),
         name="plane_gather",
-    )(*parts, *lines, *pairs)
-
-
-def heads_kernel(ways, chunks, grad_ref, out_ref, own_sem, send_sem, recv_sem):
-    me = lax.axis_index("tensor")
-    peers = [lax.rem(me + step, ways) for step in range(1, ways)]
-    greet([{"tensor": peer} for peer in peers])
-    size, width = grad_ref.shape[0] // chunks, grad_ref.shape[1] // ways
-    copies = []
-    for c in range(chunks):
-        rows = pl.ds(c * size, size)
-        target = out_ref.at[aligned((c * ways + me) * size, size), :]
-        for k, peer in enumerate(peers):
-            source = grad_ref.at[rows, aligned(peer * width, width)]
-            copies.append(remote(source, target, (send_sem, recv_sem), c * (ways - 1) + k, {"tensor": peer}))
-        kept = pltpu.make_async_copy(grad_ref.at[rows, aligned(me * width, width)], target, own_sem.at[c])
-        kept.start()
-        copies.append(kept)
-    for copy in copies:
-        copy.wait()
-
-
-def to_heads(grad, chunks, collective):
-    ways = lax.axis_size("tensor")
-    count = chunks * (ways - 1)
-    return pl.pallas_call(
-        functools.partial(heads_kernel, ways, chunks),
-        out_shape=jax.ShapeDtypeStruct((grad.shape[0] * ways, grad.shape[1] // ways), grad.dtype),
-        in_specs=[pl.BlockSpec(memory_space=pltpu.VMEM)],
-        out_specs=pl.BlockSpec(memory_space=pl.ANY),
-        scratch_shapes=[pltpu.SemaphoreType.DMA((chunks,))] + [pltpu.SemaphoreType.DMA((count,))] * 2,
-        compiler_params=pltpu.CompilerParams(collective_id=collective, has_side_effects=True),
-        name="to_heads",
-    )(grad)
+    )(*parts, *lines, *pairs, *shuffles)
 
 
 def tail_kernel(heads, ways, chunks, joint_ref, cos_ref, sin_ref, gain_ref, dq_ref, dkv_ref,
@@ -710,7 +698,6 @@
     )
     packed_all, gate_all, out_t, qkv_t = plane_gather([packed.T, w_gate], [w_out.T, w_qkv], [], 0)
     packed_all = packed_all.T
-    up_all = gathered(after(w_up, gate_all), SHARE, 0)
     qkv_mine = packed_all[:columns]
     attn_gain_all = packed_all[columns].astype(f32)
     ffn_gain_all = packed_all[columns + 1].astype(f32)
@@ -723,6 +710,7 @@
     gains = qk_gain.T
     queries, kv_mine = prep(joint, cos, sin, gains, heads, 512)
     (kv,) = plane_gather([], [], [kv_mine], 1)
+    up_all = gathered(after(w_up, kv), SHARE, 0)
     chunk_rows = rows // CHUNKS
     part_rows = chunk_rows // ways
     chunks = [slice(c * chunk_rows, (c + 1) * chunk_rows) for c in range(CHUNKS)]
@@ -734,18 +722,18 @@
     attended, log_total, attended_all = [], [], []
     for c in range(CHUNKS):
         result, total = attention(
-            start + c * chunk_rows, group_seg, after(queries, up_all) if c else queries, kv, my_pos, my_seg, *keys, QUERY_BLOCK, KEY_BLOCK, c, CHUNKS
+            start + c * chunk_rows, group_seg, queries, kv, my_pos, my_seg, *keys, QUERY_BLOCK, KEY_BLOCK, c, CHUNKS
         )
         attended.append(result)
         log_total.append(total)
         attended_all.append(gathered(result, "tensor", 0))
 
-    out_all, down_all = plane_gather([after(out_t, *attended), w_down.T], [], [], 5)
+    out_all, down_all = plane_gather([after(out_t, up_all, *attended), w_down.T], [], [], 5)
 
     resid_parts, normed_ffns, acts, gate_grads, up_grads, ffn_in_grads = [], [], [], [], [], []
     previous = attended[-1]
     for c, chunk in enumerate(chunks):
-        act_grad = dot_nn(after(cot[chunk], previous), down_all)
+        act_grad = dot_nn(cot[chunk], after(down_all, previous))
         resid = tokens_in[chunk].astype(f32) + natural(dot_tt(after(attended_all[c], act_grad), out_all))
         normed_ffn = (unit_rows(resid)[0] * ffn_gain_all).astype(bf16)
         gate, up = dot_nn(normed_ffn, gate_all), dot_nn(normed_ffn, up_all)
@@ -764,7 +752,8 @@
     act, gate_grad, up_grad, _ = lax.optimization_barrier((act, gate_grad, up_grad, previous))
     ffn_part = dot_nt(act, down_all).astype(bf16)
     grad_down = dot_tn(cot, act).astype(bf16)
-    (qkv_all,) = plane_gather([after(qkv_t, ffn_part, grad_down)], [], [], 4)
+    grad_gate = dot_tn(normed_ffn, gate_grad).astype(bf16)
+    grad_up = dot_tn(normed_ffn, up_grad).astype(bf16)
     ffn_gain_part, resid_grads, attended_grads, attended_parts, branches = 0.0, [], [], [], []
     for c in range(CHUNKS):
         norm_grad, gain_part = norm_back(ffn_in_grads[c], resid_parts[c], ffn_gain_all)
@@ -776,16 +765,27 @@
         attended_grads.append(dot_nn(branch, out_all).astype(bf16))
         attended_parts.append(lax.dynamic_slice_in_dim(attended_all[c], mine * part_rows, part_rows, 1))
 
-    attended_grad = to_heads(after(jnp.concatenate(attended_grads, axis=0), qkv_all), CHUNKS, 2)
+    attended_grad = after(jnp.concatenate(attended_grads, axis=0), ffn_part, grad_down, grad_gate, grad_up)
+    qkv_all, attended_grad = plane_gather([qkv_t], [], [], 2, [attended_grad], CHUNKS)
     branch, attended_part = jnp.concatenate(branches, axis=0), jnp.concatenate(attended_parts, axis=1)
     grad_out = lax.dot_general(branch, attended_part, (((0,), (1,)), ((), ())), preferred_element_type=f32)
-    grad_out = halving_scatter(grad_out.astype(bf16), SHARE)
-    grad_out = swap(jnp.stack([part.T for part in jnp.split(grad_out, ways, axis=1)]))
-    query_grad, kv_grad_group = attention_grad(
-        start, group_seg, queries, kv, jnp.concatenate(attended, axis=1), attended_grad, jnp.concatenate(log_total, axis=1),
-        my_pos, my_seg, *keys, QUERY_BLOCK, KEY_BLOCK
-    )
-    ffn_sums = [scattered(ffn_part[chunk], "tensor", 0).astype(f32) for chunk in chunks]
+    grad_out = grad_out.astype(bf16)
+    query_grads, carried, layer_parts, kept_part = [], [], [], ffn_part
+    for c, chunk in enumerate(chunks):
+        query_grad, kv_grad_group = attention_grad(
+            start + c * chunk_rows, group_seg, queries, kv, attended[c], attended_grad, log_total[c],
+            my_pos, my_seg, *keys, carried, QUERY_BLOCK, KEY_BLOCK, c, CHUNKS
+        )
+        query_grads.append(query_grad)
+        if c < CHUNKS - 1:
+            ffn_sum = scattered(kept_part[chunk], "tensor", 0).astype(f32)
+            layer_parts.append((after(resid_parts[c], query_grad) + ffn_sum).astype(bf16))
+            carried = [after(kv_grad_group, layer_parts[-1])]
+            kept_part = after(ffn_part, layer_parts[-1])
+    query_grad = jnp.concatenate(query_grads, axis=1)
+    ffn_sum = scattered(kept_part[chunks[-1]], "tensor", 0).astype(f32)
+    layer_parts.append((after(resid_parts[-1], query_grad) + ffn_sum).astype(bf16))
+    layer_firsts = [gathered(part, "tensor", 0) for part in layer_parts[:-1]]
     if lax.axis_size("context") == 2:
         joint_grad, joint_grad_part, qk_part = joint_tail(
             joint, cos, sin, gains, query_grad, kv_grad_group, heads, CHUNKS, 3
@@ -800,18 +800,14 @@
     own_inputs = jnp.concatenate([own_rows(tokens_in, c) for c in range(CHUNKS)], axis=0).astype(f32)
     norm_grad = norm_back(in_grad, own_inputs, attn_gain_all)[0]
     grad_input = (jnp.concatenate(resid_grads, axis=0) + norm_grad).astype(bf16)
-    gate_grad, up_grad, joint_late, _ = lax.optimization_barrier((gate_grad, up_grad, joint_grad, grad_input))
-    grad_gate = dot_tn(normed_ffn, gate_grad).astype(bf16)
-    grad_up = dot_tn(normed_ffn, up_grad).astype(bf16)
-    layer_output = [
-        (after(part, query_grad) + ffn_sum).astype(bf16) for part, ffn_sum in zip(resid_parts, ffn_sums, strict=True)
-    ]
-
-    def all_rows(parts):
-        return gathered(jnp.stack(parts), "tensor", 1).reshape(layer_input.shape)
-
-    layer_output = all_rows([after(part, grad_input) for part in layer_output])
-    grad_input = all_rows(jnp.split(grad_input, CHUNKS, axis=0))
+    late = lax.optimization_barrier((joint_grad, grad_input, grad_down, grad_gate, grad_up, grad_out))
+    joint_late, _, grad_down, grad_gate, grad_up, grad_out = late
+    grad_out = halving_scatter(grad_out, SHARE)
+    grad_out = swap(jnp.stack([part.T for part in jnp.split(grad_out, ways, axis=1)]))
+    grad_input = after(jnp.stack(jnp.split(grad_input, CHUNKS, axis=0)), *layer_firsts)
+    layer_last = gathered(after(layer_parts[-1], grad_input), "tensor", 0)
+    layer_output = jnp.concatenate(layer_firsts + [layer_last], axis=0).reshape(layer_input.shape)
+    grad_input = gathered(grad_input, "tensor", 1).reshape(layer_input.shape)
 
     grad_qkv = dot_nn(joint_late, normed_low)
     attn_gain_part = jnp.sum(qkv_mine.astype(f32) * grad_qkv, axis=0) / attn_gain_all

time: 992 us -> 961 us (0.969)
  Pallas kernels: 385 us -> 313 us
  waiting for transfers between devices: 170 us -> 212 us
    reduce_scatter x4, waiting for transfers between devices: 0.01 us -> 76.4 us  [scattered(): lax.psum_scatter(part.astype(bf16), axes, scatter_dimension=axis, tiled=T...]
    pallas_call x2, Pallas kernels: 86.2 us -> 47.3 us  [attention_grad(): pl.pallas_call(functools.partial(bwd_kernel, heads, bq, bk, final), out_s...]
    all_gather x5 -> x6, waiting for transfers between devices: 71.7 us -> 36.5 us  [gathered(): return lax.all_gather(part, axes, axis=axis, tiled=True)]
    pallas_call x1, Pallas kernels: 110 us -> 87.2 us  [joint_tail(): pl.pallas_call(functools.partial(tail_kernel, heads, ways, chunks), out_s...]
    ppermute x3, waiting for transfers between devices: 5.07 us -> 18.3 us  [swap(): lax.ppermute(sent, 'tensor', [(i, (i + step) % ways) for i in range(ways)])]
    pallas_call x4, Pallas kernels: 161 us -> 150 us  [plane_gather(): pl.pallas_call(functools.partial(gather_kernel, len(parts), len(lines), l...]
    unnamed x133 -> x125, local copies, waits for them, and re-layouts: 33.5 us -> 26.2 us
  transfers between devices with their start and end apart: 30 -> 31, of which waited for: 10 -> 15; matrix products, arithmetic and copies ran while one was open for 35% -> 35% of each run, Pallas kernels for 35% -> 27%
where the time goes in v5:
time: 961 us; the launch traced here: 951 us
  Pallas kernels  313 us (33%)
  matrix products  216 us (22%)
  waiting for transfers between devices  212 us (22%)
  local copies, waits for them, and re-layouts  88.5 us (9%)
  other arithmetic  77.1 us (8%)
  starting transfers between devices  28.6 us (3%)
  between operations  15.8 us (2%)
    pallas_call x4, Pallas kernels, plane_gather(): pl.pallas_call(functools.partial(gather_kernel, len(parts), len(lines), l...  150 us
    pallas_call x1, Pallas kernels, joint_tail(): pl.pallas_call(functools.partial(tail_kernel, heads, ways, chunks), out_s...  87.2 us
    ppermute x15, waiting for transfers between devices, halving_scatter(): got = lax.ppermute(sent, axis, [(i, i ^ stride) for i in range(size)])  80.9 us
    dot_general x9, matrix products, dot_nn(): lax.dot_general(a, b, (((1,), (0,)), ((), ())), preferred_element_type=f32)  76.5 us
    reduce_scatter x4, waiting for transfers between devices, scattered(): lax.psum_scatter(part.astype(bf16), axes, scatter_dimension=axis, tiled=T...  76.4 us
    dot_general x6, matrix products, dot_nt(): lax.dot_general(a, b, (((1,), (1,)), ((), ())), preferred_element_type=f32)  58.8 us
    dot_general x3, matrix products, dot_tn(): lax.dot_general(a, b, (((0,), (0,)), ((), ())), preferred_element_type=f32)  48.7 us
    pallas_call x2, Pallas kernels, attention_grad(): pl.pallas_call(functools.partial(bwd_kernel, heads, bq, bk, final), out_s...  47.3 us
  transfers between devices with their start and end apart: 31, of which 15 were waited for; matrix products, arithmetic and copies ran while one was open for 35% of the time, Pallas kernels for 27%

profile of v5, /device:TPU:0, one launch (start us, length us, event | category | flops | bytes accessed | tf_op | source)
XLA Modules:
  0.0 950.6 jit_solution(9095228349187741815)
XLA Ops:
  12.2 40.6 %plane_gather.4 = (bf16[2048,400]{1,0:T(8,128)(2,1)}, bf16[2048,1280]{1,0:T(8,128)(2,1)}, bf16[256,1024]{1,0:T(8,128)(2,1)}, bf16[256,1536]{1,0:T(8,128)(2,1)}) custom-call(bf16[256,400]{1,0:T(8,128)(2,1)} %maximum_bitcast_fusion.1.refs_0_, bf16[256,1280]{1,0:T(8,128)(2,1)} %refs_1_.1, bf16[256,256]{1,0:T(8,128)(2,1)} %bitcast.228, bf16[256,384]{1,0:T(8,128)(2,1)} %refs_3_.1), custom_call_target="tpu_custom_call" | custom-call | tf_op jit(solution)/shard_map/plane_gather/pallas_call | solution.py:576
  75.8 15.6 %plane_gather.5.kv_ref = bf16[4096,128]{1,0:T(8,128)(2,1)} custom-call(bf16[2048,128]{1,0:T(8,128)(2,1)} %get-tuple-element.54.refs_0_), custom_call_target="tpu_custom_call" | custom-call | tf_op jit(solution)/shard_map/plane_gather/pallas_call | solution.py:576
  94.1 9.4 attend.2
  103.8 14.4 %attend.3 = (bf16[256,1024]{1,0:T(8,128)(2,1)}, f32[4,1024]{1,0:T(4,128)}) custom-call(s32[1]{0:T(128)S(6)} %add.321.start_ref, s32[4096]{0:T(1024)} %bitcast.236, bf16[256,2048]{1,0:T(8,128)(2,1)} %get-tuple-element.53.q_ref, bf16[4096,128]{1,0:T(8,128)(2,1)} %plane_gather.5.kv_ref, s32[2048,1]{1,0:T(8,128)} %copy.89.qpos_ref, s32[2048,1]{1,0:T(8,128)} %copy.90.qseg_ref, ...), custom_call_target="tpu_custom_call" | custom-call | flops 4294967296 | bytes 4194304 | tf_op jit(solution)/shard_map/attend/pallas_call | solution.py:198
  119.3 11.5 %all-gather.9.cloned.1.call-done = bf16[2048,1280]{1,0:T(8,128)(2,1)} async-done(((bf16[256,1280]{1,0:T(8,128)(2,1)}), bf16[2048,1280]{1,0:T(8,128)(2,1)}) %all-gather.9.cloned.1.call-update) | async-done | bytes 5242896 | tf_op jit(solution)/shard_map/all_gather | solution.py:383
  130.8 49.3 %plane_gather.6 = (bf16[2048,1024]{1,0:T(8,128)(2,1)}, bf16[2048,1280]{1,0:T(8,128)(2,1)}) custom-call(bf16[256,1024]{1,0:T(8,128)(2,1)} %get-tuple-element.59.refs_0_, bf16[256,1280]{1,0:T(8,128)(2,1)} %bitcast.225), custom_call_target="tpu_custom_call" | custom-call | tf_op jit(solution)/shard_map/plane_gather/pallas_call | solution.py:576
  180.1 10.5 %convolution_bitcast_fusion.1 = f32[1024,1280]{1,0:T(8,128)} fusion(bf16[2048,1280]{1,0:T(8,128)(2,1)} %get-tuple-element.66, bf16[1,2048,2048]{2,1,0:T(8,128)(2,1)} %param.13), kind=kOutput, calls=%fused_computation.52 | convolution fusion | flops 5368709120 | bytes 14680064 | tf_op jit(solution)/shard_map/dot_general | solution.py:21
  210.3 11.9 %multiply_convert_fusion.3 = (bf16[1024,1280]{1,0:T(8,128)(2,1)S(1)}, bf16[1024,1280]{1,0:T(8,128)(2,1)S(1)}, bf16[1024,1280]{1,0:T(8,128)(2,1)S(1)}) fusion(f32[1024,1280]{1,0:T(8,128)} %fusion.78, f32[1024,1280]{1,0:T(8,128)} %convolution_bitcast_fusion.1, bf16[1024,2048]{1,0:T(8,128)(2,1)S(1)} %multiply_convert_fusion.1, ...), kind=kOutput, calls=%fused_computation.42 | convolution fusion | flops 5389680640 | bytes 27787264 | tf_op jit(solution)/shard_map/dot_general | solution.py:21
  227.9 9.7 %add_convert_fusion.1 = bf16[1024,2048]{1,0:T(8,128)(2,1)} fusion(f32[1024,2048]{1,0:T(8,128)S(1)} %fusion.79, bf16[1024,1280]{1,0:T(8,128)(2,1)S(1)} %get-tuple-element.152, bf16[2048,1280]{1,0:T(8,128)(2,1)} %all-gather.9.cloned.1.call-done), kind=kOutput, calls=%fused_computation.14 | convolution fusion | flops 5372903424 | bytes 20447232 | tf_op jit(solution)/shard_map/dot_general | solution.py:18
  237.7 10.7 %convolution_bitcast_fusion = f32[1024,1280]{1,0:T(8,128)} fusion(bf16[2048,1280]{1,0:T(8,128)(2,1)} %get-tuple-element.66, bf16[1,2048,2048]{2,1,0:T(8,128)(2,1)} %param.13), kind=kOutput, calls=%fused_computation.51 | convolution fusion | flops 5368709120 | bytes 14680064 | tf_op jit(solution)/shard_map/dot_general | solution.py:21
  260.8 11.3 %fusion.80 = f32[1024,1280]{1,0:T(8,128)} fusion(bf16[1024,2048]{1,0:T(8,128)(2,1)S(1)} %multiply_convert_fusion, bf16[2048,1280]{1,0:T(8,128)(2,1)} %get-tuple-element.65), kind=kOutput, calls=%fused_computation.198 | convolution fusion | flops 5368709120 | bytes 14680064 | tf_op jit(solution)/shard_map/dot_general | solution.py:21
  272.1 12.7 %multiply_convert_fusion.2 = (bf16[1024,1280]{1,0:T(8,128)(2,1)}, bf16[1024,1280]{1,0:T(8,128)(2,1)S(1)}, bf16[1024,1280]{1,0:T(8,128)(2,1)S(1)}) fusion(f32[1024,1280]{1,0:T(8,128)} %fusion.80, f32[1024,1280]{1,0:T(8,128)} %convolution_bitcast_fusion, bf16[1024,2048]{1,0:T(8,128)(2,1)S(1)} %multiply_convert_fusion, ...), kind=kOutput, calls=%fused_computation.41 | convolution fusion | flops 5389680640 | bytes 27787264 | tf_op jit(solution)/shard_map/dot_general | solution.py:21
  284.8 9.5 fusion.81
  294.3 9.9 %add_convert_fusion = bf16[1024,2048]{1,0:T(8,128)(2,1)} fusion(f32[1024,2048]{1,0:T(8,128)S(1)} %fusion.81, bf16[1024,1280]{1,0:T(8,128)(2,1)S(1)} %get-tuple-element.155, bf16[2048,1280]{1,0:T(8,128)(2,1)} %all-gather.9.cloned.1.call-done), kind=kOutput, calls=%fused_computation.11 | convolution fusion | flops 5372903424 | bytes 20447232 | tf_op jit(solution)/shard_map/dot_general | solution.py:18
  317.5 15.2 %convolution_convert_fusion = bf16[2048,2048]{1,0:T(8,128)(2,1)S(1)} fusion(bf16[2048,1280]{1,0:T(8,128)(2,1)S(1)} %pad_maximum_fusion.3, bf16[2048,1280]{1,0:T(8,128)(2,1)} %get-tuple-element.66), kind=kOutput, calls=%fused_computation.20 | convolution fusion | flops 10741612544 | bytes 18874368 | tf_op jit(solution)/shard_map/dot_general | solution.py:18
  344.6 15.7 %convolution_convert_fusion.2 = bf16[2048,1280]{1,0:T(8,128)(2,1)} fusion(bf16[2048,1280]{1,0:T(8,128)(2,1)} %pad_maximum_fusion.4, bf16[1024,2048]{1,0:T(8,128)(2,1)S(1)} %copy-done.18, bf16[1024,2048]{1,0:T(8,128)(2,1)S(1)} %copy-done.15), kind=kOutput, calls=%fused_computation.22 | convolution fusion | flops 10756816896 | bytes 18874368 | tf_op jit(solution)/shard_map/dot_general | solution.py:24
  360.4 17.0 %fusion.8 = bf16[2048,1280]{0,1:T(8,128)(2,1)} fusion(bf16[2048,1280]{1,0:T(8,128)(2,1)} %copy-done.11, bf16[1,2048,2048]{2,1,0:T(8,128)(2,1)} %param.13), kind=kOutput, calls=%fused_computation.23 | convolution fusion | flops 10740039680 | bytes 18874368 | tf_op jit(solution)/shard_map/dot_general | solution.py:24
  377.4 15.9 %convolution_convert_fusion.1 = bf16[2048,1280]{1,0:T(8,128)(2,1)} fusion(bf16[2048,1280]{1,0:T(8,128)(2,1)} %pad_maximum_fusion.5, bf16[1024,2048]{1,0:T(8,128)(2,1)S(1)} %copy-done.19, bf16[1024,2048]{1,0:T(8,128)(2,1)S(1)} %copy-done.16), kind=kOutput, calls=%fused_computation.21 | convolution fusion | flops 10756816896 | bytes 18874368 | tf_op jit(solution)/shard_map/dot_general | solution.py:24
  405.7 44.7 %plane_gather.7 = (bf16[2048,1536]{1,0:T(8,128)(2,1)}, bf16[2048,256]{1,0:T(8,128)(2,1)}) custom-call(bf16[256,1536]{1,0:T(8,128)(2,1)} %get-tuple-element.64.refs_0_, bf16[512,1024]{1,0:T(8,128)(2,1)} %pad_maximum_fusion.8.refs_1_), custom_call_target="tpu_custom_call" | custom-call | tf_op jit(solution)/shard_map/plane_gather/pallas_call | solution.py:576
  450.5 17.5 %attend_grad.2 = (f32[256,1024]{1,0:T(8,128)}, f32[4096,128]{1,0:T(8,128)}) custom-call(s32[1]{0:T(128)} %bitcast.1.start_ref, s32[4096]{0:T(1024)} %bitcast.238, bf16[256,2048]{1,0:T(8,128)(2,1)} %get-tuple-element.53.q_ref, bf16[4096,128]{1,0:T(8,128)(2,1)} %plane_gather.5.kv_ref, bf16[256,1024]{1,0:T(8,128)(2,1)} %get-tuple-element.55.o_ref, ...), custom_call_target="tpu_custom_call" | custom-call | flops 10737418240 | bytes 8388608 | tf_op jit(solution)/shard_map/attend_grad/pallas_call | solution.py:319
  468.0 20.5 %reduce-scatter.9.cloned.1.call-done = bf16[256,2048]{1,0:T(8,128)(2,1)} async-done(((bf16[1024,2048]{1,0:T(8,128)(2,1)}), bf16[256,2048]{1,0:T(8,128)(2,1)}) %reduce-scatter.9.cloned.1.call-update) | async-done | bytes 1048592 | tf_op jit(solution)/shard_map/reduce_scatter | solution.py:387
  500.9 29.8 %attend_grad.3 = (f32[256,1024]{1,0:T(8,128)}, bf16[4096,128]{1,0:T(8,128)(2,1)}) custom-call(s32[1]{0:T(128)S(6)} %add.321.start_ref, s32[4096]{0:T(1024)} %bitcast.239, bf16[256,2048]{1,0:T(8,128)(2,1)} %get-tuple-element.53.q_ref, bf16[4096,128]{1,0:T(8,128)(2,1)} %plane_gather.5.kv_ref, bf16[256,1024]{1,0:T(8,128)(2,1)} %get-tuple-element.58.o_ref, ...), custom_call_target="tpu_custom_call" | custom-call | flops 10737418240 | bytes 8388608 | tf_op jit(solution)/shard_map/attend_grad/pallas_call | solution.py:319
  533.0 87.2 %joint_tail.1 = (bf16[384,2048]{1,0:T(8,128)(2,1)}, bf16[1536,512]{1,0:T(8,128)(2,1)}, f32[64,2]{1,0:T(8,128)}) custom-call(f32[384,2048]{1,0:T(8,128)} %fusion.41.joint_ref, f32[32,2048]{1,0:T(8,128)} %get-tuple-element.176.cos_ref, f32[32,2048]{1,0:T(8,128)} %get-tuple-element.175.sin_ref, f32[64,2]{1,0:T(8,128)} %bitcast.230, ...), custom_call_target="tpu_custom_call" | custom-call | tf_op jit(solution)/shard_map/joint_tail/pallas_call | solution.py:655
  633.2 55.9 %reduce-scatter.11.cloned.1.call-done = bf16[256,2048]{1,0:T(8,128)(2,1)} async-done(((bf16[1024,2048]{1,0:T(8,128)(2,1)}), bf16[256,2048]{1,0:T(8,128)(2,1)}) %reduce-scatter.11.cloned.1.call-update) | async-done | bytes 1048592 | tf_op jit(solution)/shard_map/reduce_scatter | solution.py:387
  699.8 9.7 %fusion.77 = (bf16[384,2048]{1,0:T(8,128)(2,1)}, f32[384,2048]{1,0:T(8,128)}) fusion(bf16[384,2048]{1,0:T(8,128)(2,1)S(1)} %copy-done.50, bf16[1,2048,2048]{2,1,0:T(8,128)(2,1)} %param.12, f32[2048]{0:T(1024)S(1)} %copy-done.41, f32[2048]{0:T(1024)S(1)} %copy-done.47), kind=kOutput, calls=%fused_computation.195 | convolution fusion | flops 3238789120 | bytes 14696448 | tf_op jit(solution)/shard_map/dot_general | solution.py:21
  744.0 9.5 reshape_reshape.19
  781.8 16.2 %collective-permute-done.4 = bf16[1,2,256,1024]{3,2,1,0:T(8,128)(2,1)S(1)} collective-permute-done((bf16[1,2,256,1024]{3,2,1,0:T(8,128)(2,1)S(1)}, bf16[1,2,256,1024]{3,2,1,0:T(8,128)(2,1)S(1)}, u32[]{:S(2)}, u32[]{:S(2)}) %collective-permute-start.4) | collective-permute-done | bytes 1048608 | tf_op jit(solution)/shard_map/ppermute | solution.py:411
  800.7 11.1 %collective-permute-done.5 = bf16[1,1,256,1024]{3,2,1,0:T(8,128)(2,1)S(1)} collective-permute-done((bf16[1,1,256,1024]{3,2,1,0:T(8,128)(2,1)S(1)}, bf16[1,1,256,1024]{3,2,1,0:T(8,128)(2,1)S(1)}, u32[]{:S(2)}, u32[]{:S(2)}) %collective-permute-start.5) | collective-permute-done | bytes 524320 | tf_op jit(solution)/shard_map/ppermute | solution.py:411
  829.4 9.5 %collective-permute-done.7 = bf16[256,256]{0,1:T(8,128)(2,1)S(1)} collective-permute-done((bf16[256,256]{0,1:T(8,128)(2,1)S(1)}, bf16[256,256]{0,1:T(8,128)(2,1)S(1)}, u32[]{:S(2)}, u32[]{:S(2)}) %collective-permute-start.7) | collective-permute-done | bytes 131104 | tf_op jit(solution)/shard_map/ppermute | solution.py:439
  857.6 24.3 %collective-permute-done.19 = bf16[1,2,256,1280]{2,3,1,0:T(8,128)(2,1)} collective-permute-done((bf16[1,2,256,1280]{2,3,1,0:T(8,128)(2,1)}, bf16[1,2,256,1280]{2,3,1,0:T(8,128)(2,1)}, u32[]{:S(2)}, u32[]{:S(2)}) %collective-permute-start.19) | collective-permute-done | bytes 1310752 | tf_op jit(solution)/shard_map/ppermute | solution.py:411
  887.8 12.4 %collective-permute-done.20 = bf16[1,1,256,1280]{2,3,1,0:T(8,128)(2,1)S(1)} collective-permute-done((bf16[1,1,256,1280]{2,3,1,0:T(8,128)(2,1)S(1)}, bf16[1,1,256,1280]{2,3,1,0:T(8,128)(2,1)S(1)}, u32[]{:S(2)}, u32[]{:S(2)}) %collective-permute-start.20) | collective-permute-done | bytes 655392 | tf_op jit(solution)/shard_map/ppermute | solution.py:411
  909.9 25.0 %all-gather.17.cloned.1.call-done = bf16[2,1024,2048]{2,1,0:T(8,128)(2,1)} async-done(((bf16[2,256,2048]{2,1,0:T(8,128)(2,1)}), bf16[2,1024,2048]{2,1,0:T(8,128)(2,1)}) %all-gather.17.cloned.1.call-update) | async-done | bytes 8388624 | tf_op jit(solution)/shard_map/all_gather | solution.py:383
  (306 shorter events, 271.0 us)
Async XLA Ops:
  7.2 123.6 %all-gather.9.cloned.1.call-start = ((), (), s32[]{:S(2)}) async-start(), calls=%async_computation.5 | async-start | bytes 5898240 | tf_op jit(solution)/shard_map/all_gather | solution.py:383
  91.4 99.2 %all-gather.7.cloned.1.call-start = ((), (), s32[]{:S(2)}) async-start(), calls=%async_computation.4 | async-start | bytes 2621440 | tf_op jit(solution)/shard_map/all_gather | solution.py:383
  103.5 144.9 %all-gather.11.cloned.1.call-start = ((), (), s32[]{:S(2)}) async-start(), calls=%async_computation.7 | async-start | bytes 2621440 | tf_op jit(solution)/shard_map/all_gather | solution.py:383
  118.2 275.2 %reduce-scatter.5.cloned.1.call-start = ((), (), s32[]{:S(2)}) async-start(), calls=%async_computation.6 | async-start | bytes 5242880 | tf_op jit(solution)/shard_map/reduce_scatter | solution.py:387
  237.6 155.8 %reduce-scatter.7.cloned.1.call-start = ((), (), s32[]{:S(2)}) async-start(), calls=%async_computation.8 | async-start | bytes 5242880 | tf_op jit(solution)/shard_map/reduce_scatter | solution.py:387
  304.2 184.3 %reduce-scatter.9.cloned.1.call-start = ((), (), s32[]{:S(2)}) async-start(), calls=%async_computation.9 | async-start | bytes 5242880 | tf_op jit(solution)/shard_map/reduce_scatter | solution.py:387
  360.4 272.8 %all-gather.13.cloned.1.call-start = ((), (), s32[]{:S(2)}) async-start(), calls=%async_computation.10 | async-start | bytes 5242880 | tf_op jit(solution)/shard_map/all_gather | solution.py:383
  491.6 197.4 %reduce-scatter.11.cloned.1.call-start = ((), (), s32[]{:S(2)}) async-start(), calls=%async_computation.11 | async-start | bytes 5242880 | tf_op jit(solution)/shard_map/reduce_scatter | solution.py:387
  496.5 404.9 %all-gather.15.cloned.1.call-start = ((), (), s32[]{:S(2)}) async-start(), calls=%async_computation.12 | async-start | bytes 5242880 | tf_op jit(solution)/shard_map/all_gather | solution.py:383
  530.7 89.5 %copy-start.41 = (f32[2048]{0:T(1024)S(1)}, f32[2048]{0:T(1024)}, u32[]{:S(2)}) copy-start(f32[2048]{0:T(1024)} %copy-done.40) | copy-start | bytes 24580
  691.5 243.4 %all-gather.17.cloned.1.call-start = ((), (), s32[]{:S(2)}) async-start(), calls=%async_computation.13 | async-start | bytes 10485760 | tf_op jit(solution)/shard_map/all_gather | solution.py:383
  718.9 2.4 collective-permute-start
  722.3 11.7 %collective-permute-start.1 = (bf16[1,2,256,400]{2,3,1,0:T(8,128)(2,1)}, bf16[1,2,256,400]{2,3,1,0:T(8,128)(2,1)S(1)}, u32[]{:S(2)}, u32[]{:S(2)}) collective-permute-start(bf16[1,2,256,400]{2,3,1,0:T(8,128)(2,1)} %constant_dynamic-slice_fusion.11), channel_id=1, source_target_pairs={{0,16},{8,24},{16,0},{24,8},{1,17},{9,25},{17,1},{25,9},{2,18},{10... | collective-permute-start | bytes 1228808 | tf_op jit(solution)/shard_map/ppermute | solution.py:411
  727.5 46.2 %collective-permute-start.12 = (bf16[2,2,256,1280]{3,2,1,0:T(8,128)(2,1)}, bf16[2,2,256,1280]{3,2,1,0:T(8,128)(2,1)}, u32[]{:S(2)}, u32[]{:S(2)}) collective-permute-start(bf16[2,2,256,1280]{3,2,1,0:T(8,128)(2,1)} %dynamic-slice_bitcast_fusion.1), channel_id=1, source_target_pairs={{0,8},{8,0},{16,24},{24,16},{1,9},{9,1},{17,25},{25,17},{2,10},{10... | collective-permute-start | bytes 7864328 | tf_op jit(solution)/shard_map/ppermute | solution.py:411
  729.0 40.1 %collective-permute-start.3 = (bf16[2,2,256,1024]{3,2,1,0:T(8,128)(2,1)}, bf16[2,2,256,1024]{3,2,1,0:T(8,128)(2,1)S(1)}, u32[]{:S(2)}, u32[]{:S(2)}) collective-permute-start(bf16[2,2,256,1024]{3,2,1,0:T(8,128)(2,1)} %dynamic-slice_bitcast_fusion.2), channel_id=1, source_target_pairs={{0,8},{8,0},{16,24},{24,16},{1,9},{9,1},{17,25},{25,17},{2,10},{10... | collective-permute-start | bytes 6291464 | tf_op jit(solution)/shard_map/ppermute | solution.py:411
  734.1 6.5 collective-permute-start.2
  739.2 37.6 %collective-permute-start.15 = (bf16[2,2,256,1280]{3,2,1,0:T(8,128)(2,1)}, bf16[2,2,256,1280]{3,2,1,0:T(8,128)(2,1)}, u32[]{:S(2)}, u32[]{:S(2)}) collective-permute-start(bf16[2,2,256,1280]{3,2,1,0:T(8,128)(2,1)} %dynamic-slice_bitcast_fusion), channel_id=1, source_target_pairs={{0,8},{8,0},{16,24},{24,16},{1,9},{9,1},{17,25},{25,17},{2,10},{10... | collective-permute-start | bytes 7864328 | tf_op jit(solution)/shard_map/ppermute | solution.py:411
  741.3 12.5 %collective-permute-start.11 = (f32[16,256]{1,0:T(8,128)}, f32[16,256]{1,0:T(8,128)S(1)}, u32[]{:S(2)}, u32[]{:S(2)}) collective-permute-start(f32[16,256]{1,0:T(8,128)} %slice_bitcast_fusion.6), channel_id=1, source_target_pairs={{0,3},{1,0},{2,1},{3,2},{4,7},{5,4},{6,5},{7,6},{8,11},{9,8},{10,9... | collective-permute-start | bytes 49160 | tf_op jit(solution)/shard_map/ppermute | solution.py:430
  753.5 13.8 %collective-permute-start.10 = (f32[16,256]{1,0:T(8,128)}, f32[16,256]{1,0:T(8,128)}, u32[]{:S(2)}, u32[]{:S(2)}) collective-permute-start(f32[16,256]{1,0:T(8,128)} %slice_bitcast_fusion.6), channel_id=1, source_target_pairs={{0,2},{1,3},{2,0},{3,1},{4,6},{5,7},{6,4},{7,5},{8,10},{9,11},{10,... | collective-permute-start | bytes 49160 | tf_op jit(solution)/shard_map/ppermute | solution.py:430
  753.8 13.5 %collective-permute-start.9 = (f32[16,256]{1,0:T(8,128)}, f32[16,256]{1,0:T(8,128)}, u32[]{:S(2)}, u32[]{:S(2)}) collective-permute-start(f32[16,256]{1,0:T(8,128)} %slice_bitcast_fusion.6), channel_id=1, source_target_pairs={{0,1},{1,2},{2,3},{3,0},{4,5},{5,6},{6,7},{7,4},{8,9},{9,10},{10,1... | collective-permute-start | bytes 49160 | tf_op jit(solution)/shard_map/ppermute | solution.py:430
  767.2 32.9 %collective-permute-start.18 = (bf16[2,2,256,1280]{2,3,1,0:T(8,128)(2,1)}, bf16[2,2,256,1280]{2,3,1,0:T(8,128)(2,1)S(1)}, u32[]{:S(2)}, u32[]{:S(2)}) collective-permute-start(bf16[2,2,256,1280]{2,3,1,0:T(8,128)(2,1)} %bitcast.224), channel_id=1, source_target_pairs={{0,8},{8,0},{16,24},{24,16},{1,9},{9,1},{17,25},{25,17},{2,10},{10... | collective-permute-start | bytes 7864328 | tf_op jit(solution)/shard_map/ppermute | solution.py:411
  772.0 26.0 %collective-permute-start.4 = (bf16[1,2,256,1024]{3,2,1,0:T(8,128)(2,1)S(1)}, bf16[1,2,256,1024]{3,2,1,0:T(8,128)(2,1)S(1)}, u32[]{:S(2)}, u32[]{:S(2)}) collective-permute-start(bf16[1,2,256,1024]{3,2,1,0:T(8,128)(2,1)S(1)} %constant_dynamic-slice_fusion.9), channel_id=1, source_target_pairs={{0,16},{8,24},{16,0},{24,8},{1,17},{9,25},{17,1},{25,9},{2,18},{10... | collective-permute-start | bytes 3145736 | tf_op jit(solution)/shard_map/ppermute | solution.py:411
  776.1 51.9 %collective-permute-start.13 = (bf16[1,2,256,1280]{3,2,1,0:T(8,128)(2,1)S(1)}, bf16[1,2,256,1280]{3,2,1,0:T(8,128)(2,1)S(1)}, u32[]{:S(2)}, u32[]{:S(2)}) collective-permute-start(bf16[1,2,256,1280]{3,2,1,0:T(8,128)(2,1)S(1)} %constant_dynamic-slice_fusion.7), channel_id=1, source_target_pairs={{0,16},{8,24},{16,0},{24,8},{1,17},{9,25},{17,1},{25,9},{2,18},{10... | collective-permute-start | bytes 3932168 | tf_op jit(solution)/shard_map/ppermute | solution.py:411
  780.5 73.8 %collective-permute-start.16 = (bf16[1,2,256,1280]{3,2,1,0:T(8,128)(2,1)}, bf16[1,2,256,1280]{3,2,1,0:T(8,128)(2,1)}, u32[]{:S(2)}, u32[]{:S(2)}) collective-permute-start(bf16[1,2,256,1280]{3,2,1,0:T(8,128)(2,1)} %constant_dynamic-slice_fusion.5), channel_id=1, source_target_pairs={{0,16},{8,24},{16,0},{24,8},{1,17},{9,25},{17,1},{25,9},{2,18},{10... | collective-permute-start | bytes 3932168 | tf_op jit(solution)/shard_map/ppermute | solution.py:411
  798.5 13.3 %collective-permute-start.5 = (bf16[1,1,256,1024]{3,2,1,0:T(8,128)(2,1)S(1)}, bf16[1,1,256,1024]{3,2,1,0:T(8,128)(2,1)S(1)}, u32[]{:S(2)}, u32[]{:S(2)}) collective-permute-start(bf16[1,1,256,1024]{3,2,1,0:T(8,128)(2,1)S(1)} %constant_dynamic-slice_fusion.8), channel_id=1, source_target_pairs={{0,4},{4,0},{1,5},{5,1},{2,6},{6,2},{3,7},{7,3},{8,12},{12,8},{9,1... | collective-permute-start | bytes 1572872 | tf_op jit(solution)/shard_map/ppermute | solution.py:411
  812.1 10.3 %collective-permute-start.6 = (bf16[256,256]{0,1:T(8,128)(2,1)S(1)}, bf16[256,256]{0,1:T(8,128)(2,1)S(1)}, u32[]{:S(2)}, u32[]{:S(2)}) collective-permute-start(bf16[256,256]{0,1:T(8,128)(2,1)S(1)} %dynamic-slice_bitcast_fusion.7), channel_id=1, source_target_pairs={{0,1},{1,2},{2,3},{3,0},{4,5},{5,6},{6,7},{7,4},{8,9},{9,10},{10,1... | collective-permute-start | bytes 393224 | tf_op jit(solution)/shard_map/ppermute | solution.py:439
  814.7 67.3 %collective-permute-start.19 = (bf16[1,2,256,1280]{2,3,1,0:T(8,128)(2,1)}, bf16[1,2,256,1280]{2,3,1,0:T(8,128)(2,1)}, u32[]{:S(2)}, u32[]{:S(2)}) collective-permute-start(bf16[1,2,256,1280]{2,3,1,0:T(8,128)(2,1)} %constant_dynamic-slice_fusion.1), channel_id=1, source_target_pairs={{0,16},{8,24},{16,0},{24,8},{1,17},{9,25},{17,1},{25,9},{2,18},{10... | collective-permute-start | bytes 3932168 | tf_op jit(solution)/shard_map/ppermute | solution.py:411
  822.4 16.5 %collective-permute-start.7 = (bf16[256,256]{0,1:T(8,128)(2,1)S(1)}, bf16[256,256]{0,1:T(8,128)(2,1)S(1)}, u32[]{:S(2)}, u32[]{:S(2)}) collective-permute-start(bf16[256,256]{0,1:T(8,128)(2,1)S(1)} %get-tuple-element.167), channel_id=1, source_target_pairs={{0,2},{1,3},{2,0},{3,1},{4,6},{5,7},{6,4},{7,5},{8,10},{9,11},{10,... | collective-permute-start | bytes 393224 | tf_op jit(solution)/shard_map/ppermute | solution.py:439
  826.0 15.7 %collective-permute-start.8 = (bf16[256,256]{0,1:T(8,128)(2,1)S(1)}, bf16[256,256]{0,1:T(8,128)(2,1)S(1)}, u32[]{:S(2)}, u32[]{:S(2)}) collective-permute-start(bf16[256,256]{0,1:T(8,128)(2,1)S(1)} %get-tuple-element.166), channel_id=1, source_target_pairs={{0,3},{1,0},{2,1},{3,2},{4,7},{5,4},{6,5},{7,6},{8,11},{9,8},{10,9... | collective-permute-start | bytes 393224 | tf_op jit(solution)/shard_map/ppermute | solution.py:439
  843.9 41.5 %collective-permute-start.14 = (bf16[1,1,256,1280]{3,2,1,0:T(8,128)(2,1)S(1)}, bf16[1,1,256,1280]{3,2,1,0:T(8,128)(2,1)S(1)}, u32[]{:S(2)}, u32[]{:S(2)}) collective-permute-start(bf16[1,1,256,1280]{3,2,1,0:T(8,128)(2,1)S(1)} %constant_dynamic-slice_fusion.6), channel_id=1, source_target_pairs={{0,4},{4,0},{1,5},{5,1},{2,6},{6,2},{3,7},{7,3},{8,12},{12,8},{9,1... | collective-permute-start | bytes 1966088 | tf_op jit(solution)/shard_map/ppermute | solution.py:411
  856.0 30.7 %collective-permute-start.17 = (bf16[1,1,256,1280]{3,2,1,0:T(8,128)(2,1)S(1)}, bf16[1,1,256,1280]{3,2,1,0:T(8,128)(2,1)S(1)}, u32[]{:S(2)}, u32[]{:S(2)}) collective-permute-start(bf16[1,1,256,1280]{3,2,1,0:T(8,128)(2,1)S(1)} %constant_dynamic-slice_fusion.4), channel_id=1, source_target_pairs={{0,4},{4,0},{1,5},{5,1},{2,6},{6,2},{3,7},{7,3},{8,12},{12,8},{9,1... | collective-permute-start | bytes 1966088 | tf_op jit(solution)/shard_map/ppermute | solution.py:411
  883.7 16.4 %collective-permute-start.20 = (bf16[1,1,256,1280]{2,3,1,0:T(8,128)(2,1)S(1)}, bf16[1,1,256,1280]{2,3,1,0:T(8,128)(2,1)S(1)}, u32[]{:S(2)}, u32[]{:S(2)}) collective-permute-start(bf16[1,1,256,1280]{2,3,1,0:T(8,128)(2,1)S(1)} %constant_dynamic-slice_fusion), channel_id=1, source_target_pairs={{0,4},{4,0},{1,5},{5,1},{2,6},{6,2},{3,7},{7,3},{8,12},{12,8},{9,1... | collective-permute-start | bytes 1966088 | tf_op jit(solution)/shard_map/ppermute | solution.py:411
  (58 other events, 595.4 us)
Sparse Core Ops, SparseCore 0:
  91.5 39.2 all-gather.8
  132.4 46.0 all-gather.6
  180.0 44.6 all-gather.10
  237.8 74.8 reduce-scatter.4
  314.9 77.2 reduce-scatter.6
  394.3 94.0 reduce-scatter.8
  491.7 120.3 all-gather.12
  614.6 74.4 reduce-scatter.10
  691.7 82.5 all-gather.14
  775.7 159.1 all-gather.16

commit v6 on v5

--- a/solution.py
+++ b/solution.py
@@ -696,7 +696,8 @@
     packed = jnp.concatenate(
         [qkv_shard, attn_gain[None], ffn_gain[None], jnp.zeros((14, w_qkv.shape[0]), bf16)], axis=0
     )
-    packed_all, gate_all, out_t, qkv_t = plane_gather([packed.T, w_gate], [w_out.T, w_qkv], [], 0)
+    gate_all = gathered(w_gate, SHARE, 0)
+    (packed_all,) = plane_gather([packed.T], [], [], 0)
     packed_all = packed_all.T
     qkv_mine = packed_all[:columns]
     attn_gain_all = packed_all[columns].astype(f32)
@@ -709,8 +710,9 @@
     cos, sin = rope_tables(my_pos)
     gains = qk_gain.T
     queries, kv_mine = prep(joint, cos, sin, gains, heads, 512)
-    (kv,) = plane_gather([], [], [kv_mine], 1)
+    out_t, kv = plane_gather([], [w_out.T], [kv_mine], 1)
     up_all = gathered(after(w_up, kv), SHARE, 0)
+    queries = after(queries, gate_all)
     chunk_rows = rows // CHUNKS
     part_rows = chunk_rows // ways
     chunks = [slice(c * chunk_rows, (c + 1) * chunk_rows) for c in range(CHUNKS)]
@@ -728,7 +730,7 @@
         log_total.append(total)
         attended_all.append(gathered(result, "tensor", 0))
 
-    out_all, down_all = plane_gather([after(out_t, up_all, *attended), w_down.T], [], [], 5)
+    out_all, down_all, qkv_t = plane_gather([after(out_t, up_all, *attended), w_down.T], [w_qkv], [], 5)
 
     resid_parts, normed_ffns, acts, gate_grads, up_grads, ffn_in_grads = [], [], [], [], [], []
     previous = attended[-1]
@@ -752,8 +754,6 @@
     act, gate_grad, up_grad, _ = lax.optimization_barrier((act, gate_grad, up_grad, previous))
     ffn_part = dot_nt(act, down_all).astype(bf16)
     grad_down = dot_tn(cot, act).astype(bf16)
-    grad_gate = dot_tn(normed_ffn, gate_grad).astype(bf16)
-    grad_up = dot_tn(normed_ffn, up_grad).astype(bf16)
     ffn_gain_part, resid_grads, attended_grads, attended_parts, branches = 0.0, [], [], [], []
     for c in range(CHUNKS):
         norm_grad, gain_part = norm_back(ffn_in_grads[c], resid_parts[c], ffn_gain_all)
@@ -765,7 +765,7 @@
         attended_grads.append(dot_nn(branch, out_all).astype(bf16))
         attended_parts.append(lax.dynamic_slice_in_dim(attended_all[c], mine * part_rows, part_rows, 1))
 
-    attended_grad = after(jnp.concatenate(attended_grads, axis=0), ffn_part, grad_down, grad_gate, grad_up)
+    attended_grad = after(jnp.concatenate(attended_grads, axis=0), ffn_part, grad_down)
     qkv_all, attended_grad = plane_gather([qkv_t], [], [], 2, [attended_grad], CHUNKS)
     branch, attended_part = jnp.concatenate(branches, axis=0), jnp.concatenate(attended_parts, axis=1)
     grad_out = lax.dot_general(branch, attended_part, (((0,), (1,)), ((), ())), preferred_element_type=f32)
@@ -800,6 +800,9 @@
     own_inputs = jnp.concatenate([own_rows(tokens_in, c) for c in range(CHUNKS)], axis=0).astype(f32)
     norm_grad = norm_back(in_grad, own_inputs, attn_gain_all)[0]
     grad_input = (jnp.concatenate(resid_grads, axis=0) + norm_grad).astype(bf16)
+    gate_grad, up_grad, _ = lax.optimization_barrier((gate_grad, up_grad, joint_grad))
+    grad_gate = dot_tn(normed_ffn, gate_grad).astype(bf16)
+    grad_up = dot_tn(normed_ffn, up_grad).astype(bf16)
     late = lax.optimization_barrier((joint_grad, grad_input, grad_down, grad_gate, grad_up, grad_out))
     joint_late, _, grad_down, grad_gate, grad_up, grad_out = late
     grad_out = halving_scatter(grad_out, SHARE)

time: 961 us -> 950 us (0.989)
  Pallas kernels: 313 us -> 295 us
  waiting for transfers between devices: 212 us -> 200 us
  local copies, waits for them, and re-layouts: 88.5 us -> 100 us
    all_gather x6 -> x7, waiting for transfers between devices: 36.5 us -> 20.5 us  [gathered(): return lax.all_gather(part, axes, axis=axis, tiled=True)]
    pallas_call x4, Pallas kernels: 150 us -> 135 us  [plane_gather(): pl.pallas_call(functools.partial(gather_kernel, len(parts), len(lines), l...]
    unnamed x125 -> x113, local copies, waits for them, and re-layouts: 26.2 us -> 27.8 us
  transfers between devices with their start and end apart: 31 -> 32, of which waited for: 15 -> 16; matrix products, arithmetic and copies ran while one was open for 35% -> 40% of each run, Pallas kernels for 27% -> 31%
where the time goes in v6:
time: 950 us; the launch traced here: 940 us
  Pallas kernels  295 us (31%)
  matrix products  219 us (23%)
  waiting for transfers between devices  200 us (21%)
  local copies, waits for them, and re-layouts  100 us (11%)
  other arithmetic  84.4 us (9%)
  starting transfers between devices  27.4 us (3%)
  between operations  15.1 us (2%)
    pallas_call x4, Pallas kernels, plane_gather(): pl.pallas_call(functools.partial(gather_kernel, len(parts), len(lines), l...  135 us
    pallas_call x1, Pallas kernels, joint_tail(): pl.pallas_call(functools.partial(tail_kernel, heads, ways, chunks), out_s...  83.6 us
    ppermute x15, waiting for transfers between devices, halving_scatter(): got = lax.ppermute(sent, axis, [(i, i ^ stride) for i in range(size)])  83.6 us
    reduce_scatter x4, waiting for transfers between devices, scattered(): lax.psum_scatter(part.astype(bf16), axes, scatter_dimension=axis, tiled=T...  78 us
    dot_general x9, matrix products, dot_nn(): lax.dot_general(a, b, (((1,), (0,)), ((), ())), preferred_element_type=f32)  75.9 us
    dot_general x6, matrix products, dot_nt(): lax.dot_general(a, b, (((1,), (1,)), ((), ())), preferred_element_type=f32)  61.1 us
    dot_general x3, matrix products, dot_tn(): lax.dot_general(a, b, (((0,), (0,)), ((), ())), preferred_element_type=f32)  49.9 us
    pallas_call x2, Pallas kernels, attention_grad(): pl.pallas_call(functools.partial(bwd_kernel, heads, bq, bk, final), out_s...  47.6 us
  transfers between devices with their start and end apart: 32, of which 16 were waited for; matrix products, arithmetic and copies ran while one was open for 40% of the time, Pallas kernels for 31%

profile of v6, /device:TPU:0, one launch (start us, length us, event | category | flops | bytes accessed | tf_op | source)
XLA Modules:
  0.0 939.9 jit_solution(15635990089677234282)
XLA Ops:
  11.3 21.1 %plane_gather.4 = bf16[2048,400]{1,0:T(8,128)(2,1)} custom-call(bf16[256,400]{1,0:T(8,128)(2,1)} %maximum_bitcast_fusion.1.refs_0_), custom_call_target="tpu_custom_call" | custom-call | tf_op jit(solution)/shard_map/plane_gather/pallas_call | solution.py:576
  56.8 18.4 %plane_gather.5 = (bf16[256,1024]{1,0:T(8,128)(2,1)}, bf16[4096,128]{1,0:T(8,128)(2,1)}) custom-call(bf16[256,256]{1,0:T(8,128)(2,1)} %bitcast.229, bf16[2048,128]{1,0:T(8,128)(2,1)} %get-tuple-element.56.refs_1_), custom_call_target="tpu_custom_call" | custom-call | tf_op jit(solution)/shard_map/plane_gather/pallas_call | solution.py:576
  88.8 14.2 %attend.3 = (bf16[256,1024]{1,0:T(8,128)(2,1)}, f32[4,1024]{1,0:T(4,128)}) custom-call(s32[1]{0:T(128)S(6)} %add.321.start_ref, s32[4096]{0:T(1024)} %bitcast.234, bf16[256,2048]{1,0:T(8,128)(2,1)} %get-tuple-element.55.q_ref, bf16[4096,128]{1,0:T(8,128)(2,1)} %get-tuple-element.57.kv_ref, s32[2048,1]{1,0:T(8,128)} %copy.89.qpos_ref, ...), custom_call_target="tpu_custom_call" | custom-call | flops 4294967296 | bytes 4194304 | tf_op jit(solution)/shard_map/attend/pallas_call | solution.py:198
  103.0 12.0 %all-gather.12.cloned.1.call-done = bf16[2048,1280]{1,0:T(8,128)(2,1)} async-done(((bf16[256,1280]{1,0:T(8,128)(2,1)}), bf16[2048,1280]{1,0:T(8,128)(2,1)}) %all-gather.12.cloned.1.call-update) | async-done | bytes 5242896 | tf_op jit(solution)/shard_map/all_gather | solution.py:383
  115.0 49.7 %plane_gather.6 = (bf16[2048,1024]{1,0:T(8,128)(2,1)}, bf16[2048,1280]{1,0:T(8,128)(2,1)}, bf16[256,1536]{1,0:T(8,128)(2,1)}) custom-call(bf16[256,1024]{1,0:T(8,128)(2,1)} %get-tuple-element.62.refs_0_, bf16[256,1280]{1,0:T(8,128)(2,1)} %bitcast.226, bf16[256,384]{1,0:T(8,128)(2,1)} %refs_2_.1), custom_call_target="tpu_custom_call" | custom-call | tf_op jit(solution)/shard_map/plane_gather/pallas_call | solution.py:576
  164.7 10.5 %convolution_bitcast_fusion.1 = f32[1024,1280]{1,0:T(8,128)} fusion(bf16[2048,1280]{1,0:T(8,128)(2,1)} %get-tuple-element.68, bf16[1,2048,2048]{2,1,0:T(8,128)(2,1)} %param.13), kind=kOutput, calls=%fused_computation.52 | convolution fusion | flops 5368709120 | bytes 14680064 | tf_op jit(solution)/shard_map/dot_general | solution.py:21
  194.9 11.7 %multiply_convert_fusion.3 = (bf16[1024,1280]{1,0:T(8,128)(2,1)S(1)}, bf16[1024,1280]{1,0:T(8,128)(2,1)S(1)}, bf16[1024,1280]{1,0:T(8,128)(2,1)S(1)}) fusion(f32[1024,1280]{1,0:T(8,128)} %fusion.78, f32[1024,1280]{1,0:T(8,128)} %convolution_bitcast_fusion.1, bf16[1024,2048]{1,0:T(8,128)(2,1)S(1)} %multiply_convert_fusion.1, ...), kind=kOutput, calls=%fused_computation.42 | convolution fusion | flops 5389680640 | bytes 27787264 | tf_op jit(solution)/shard_map/dot_general | solution.py:21
  206.7 9.5 %fusion.79 = f32[1024,2048]{1,0:T(8,128)S(1)} fusion(bf16[1024,1280]{1,0:T(8,128)(2,1)S(1)} %get-tuple-element.155, bf16[2048,1280]{1,0:T(8,128)(2,1)} %all-gather.8.cloned.1.call-done), kind=kOutput, calls=%fused_computation.197 | convolution fusion | flops 5368709120 | bytes 16252928 | tf_op jit(solution)/shard_map/dot_general | solution.py:18
  216.2 9.8 %add_convert_fusion.1 = bf16[1024,2048]{1,0:T(8,128)(2,1)} fusion(f32[1024,2048]{1,0:T(8,128)S(1)} %fusion.79, bf16[1024,1280]{1,0:T(8,128)(2,1)S(1)} %get-tuple-element.156, bf16[2048,1280]{1,0:T(8,128)(2,1)} %all-gather.12.cloned.1.call-done), kind=kOutput, calls=%fused_computation.14 | convolution fusion | flops 5372903424 | bytes 20447232 | tf_op jit(solution)/shard_map/dot_general | solution.py:18
  226.0 10.8 %convolution_bitcast_fusion = f32[1024,1280]{1,0:T(8,128)} fusion(bf16[2048,1280]{1,0:T(8,128)(2,1)} %get-tuple-element.68, bf16[1,2048,2048]{2,1,0:T(8,128)(2,1)} %param.13), kind=kOutput, calls=%fused_computation.51 | convolution fusion | flops 5368709120 | bytes 14680064 | tf_op jit(solution)/shard_map/dot_general | solution.py:21
  249.2 11.3 %fusion.80 = f32[1024,1280]{1,0:T(8,128)} fusion(bf16[1024,2048]{1,0:T(8,128)(2,1)S(1)} %multiply_convert_fusion, bf16[2048,1280]{1,0:T(8,128)(2,1)} %all-gather.8.cloned.1.call-done), kind=kOutput, calls=%fused_computation.198 | convolution fusion | flops 5368709120 | bytes 14680064 | tf_op jit(solution)/shard_map/dot_general | solution.py:21
  260.5 12.7 %multiply_convert_fusion.2 = (bf16[1024,1280]{1,0:T(8,128)(2,1)}, bf16[1024,1280]{1,0:T(8,128)(2,1)S(1)}, bf16[1024,1280]{1,0:T(8,128)(2,1)S(1)}) fusion(f32[1024,1280]{1,0:T(8,128)} %fusion.80, f32[1024,1280]{1,0:T(8,128)} %convolution_bitcast_fusion, bf16[1024,2048]{1,0:T(8,128)(2,1)S(1)} %multiply_convert_fusion, ...), kind=kOutput, calls=%fused_computation.41 | convolution fusion | flops 5389680640 | bytes 27787264 | tf_op jit(solution)/shard_map/dot_general | solution.py:21
  273.2 9.5 %fusion.81 = f32[1024,2048]{1,0:T(8,128)S(1)} fusion(bf16[1024,1280]{1,0:T(8,128)(2,1)S(1)} %get-tuple-element.158, bf16[2048,1280]{1,0:T(8,128)(2,1)} %all-gather.8.cloned.1.call-done), kind=kOutput, calls=%fused_computation.199 | convolution fusion | flops 5368709120 | bytes 16252928 | tf_op jit(solution)/shard_map/dot_general | solution.py:18
  282.7 9.9 %add_convert_fusion = bf16[1024,2048]{1,0:T(8,128)(2,1)} fusion(f32[1024,2048]{1,0:T(8,128)S(1)} %fusion.81, bf16[1024,1280]{1,0:T(8,128)(2,1)S(1)} %get-tuple-element.159, bf16[2048,1280]{1,0:T(8,128)(2,1)} %all-gather.12.cloned.1.call-done), kind=kOutput, calls=%fused_computation.11 | convolution fusion | flops 5372903424 | bytes 20447232 | tf_op jit(solution)/shard_map/dot_general | solution.py:18
  299.5 10.8 %pad_maximum_fusion.3 = (bf16[2048,1280]{1,0:T(8,128)(2,1)S(1)}, bf16[2048,1280]{1,0:T(8,128)(2,1)}) fusion(bf16[1024,1280]{1,0:T(8,128)(2,1)S(1)} %copy-done.25, bf16[1024,1280]{1,0:T(8,128)(2,1)S(1)} %get-tuple-element.154, bf16[1024,1280]{1,0:T(8,128)(2,1)S(1)} %copy-done.27, bf16[1024,1280]{1,0:T(8,128)(2,1)S(1)} %copy-done.23), kind=kLoop, calls=%fused_computation.32 | loop fusion | flops 20971520 | bytes 20971520 | tf_op jit(solution)/shard_map/concatenate | solution.py:752
  310.3 15.3 %convolution_convert_fusion = bf16[2048,2048]{1,0:T(8,128)(2,1)S(1)} fusion(bf16[2048,1280]{1,0:T(8,128)(2,1)S(1)} %get-tuple-element.70, bf16[2048,1280]{1,0:T(8,128)(2,1)} %get-tuple-element.68), kind=kOutput, calls=%fused_computation.20 | convolution fusion | flops 10741612544 | bytes 18874368 | tf_op jit(solution)/shard_map/dot_general | solution.py:18
  340.5 16.9 %fusion.8 = bf16[2048,1280]{0,1:T(8,128)(2,1)} fusion(bf16[2048,1280]{1,0:T(8,128)(2,1)} %copy-done.13, bf16[1,2048,2048]{2,1,0:T(8,128)(2,1)} %param.13), kind=kOutput, calls=%fused_computation.23 | convolution fusion | flops 10740039680 | bytes 18874368 | tf_op jit(solution)/shard_map/dot_general | solution.py:24
  357.4 23.7 %reduce-scatter.7.cloned.1.call-done = bf16[256,2048]{1,0:T(8,128)(2,1)} async-done(((bf16[1024,2048]{1,0:T(8,128)(2,1)}), bf16[256,2048]{1,0:T(8,128)(2,1)}) %reduce-scatter.7.cloned.1.call-update) | async-done | bytes 1048592 | tf_op jit(solution)/shard_map/reduce_scatter | solution.py:387
  393.3 46.2 %plane_gather.7 = (bf16[2048,1536]{1,0:T(8,128)(2,1)}, bf16[2048,256]{1,0:T(8,128)(2,1)}) custom-call(bf16[256,1536]{1,0:T(8,128)(2,1)} %get-tuple-element.67.refs_0_, bf16[512,1024]{1,0:T(8,128)(2,1)} %pad_maximum_fusion.8.refs_1_), custom_call_target="tpu_custom_call" | custom-call | tf_op jit(solution)/shard_map/plane_gather/pallas_call | solution.py:576
  439.5 18.0 %attend_grad.2 = (f32[256,1024]{1,0:T(8,128)}, f32[4096,128]{1,0:T(8,128)}) custom-call(s32[1]{0:T(128)} %bitcast.1.start_ref, s32[4096]{0:T(1024)} %bitcast.236, bf16[256,2048]{1,0:T(8,128)(2,1)} %get-tuple-element.55.q_ref, bf16[4096,128]{1,0:T(8,128)(2,1)} %get-tuple-element.57.kv_ref, bf16[256,1024]{1,0:T(8,128)(2,1)} %get-tuple-element.58.o_ref, ...), custom_call_target="tpu_custom_call" | custom-call | flops 10737418240 | bytes 8388608 | tf_op jit(solution)/shard_map/attend_grad/pallas_call | solution.py:319
  457.5 20.0 %reduce-scatter.9.cloned.1.call-done = bf16[256,2048]{1,0:T(8,128)(2,1)} async-done(((bf16[1024,2048]{1,0:T(8,128)(2,1)}), bf16[256,2048]{1,0:T(8,128)(2,1)}) %reduce-scatter.9.cloned.1.call-update) | async-done | bytes 1048592 | tf_op jit(solution)/shard_map/reduce_scatter | solution.py:387
  493.6 29.6 %attend_grad.3 = (f32[256,1024]{1,0:T(8,128)}, bf16[4096,128]{1,0:T(8,128)(2,1)}) custom-call(s32[1]{0:T(128)S(6)} %add.321.start_ref, s32[4096]{0:T(1024)} %bitcast.237, bf16[256,2048]{1,0:T(8,128)(2,1)} %get-tuple-element.55.q_ref, bf16[4096,128]{1,0:T(8,128)(2,1)} %get-tuple-element.57.kv_ref, bf16[256,1024]{1,0:T(8,128)(2,1)} %get-tuple-element.61.o_ref, ...), custom_call_target="tpu_custom_call" | custom-call | flops 10737418240 | bytes 8388608 | tf_op jit(solution)/shard_map/attend_grad/pallas_call | solution.py:319
  525.6 83.6 %joint_tail.1 = (bf16[384,2048]{1,0:T(8,128)(2,1)}, bf16[1536,512]{1,0:T(8,128)(2,1)}, f32[64,2]{1,0:T(8,128)}) custom-call(f32[384,2048]{1,0:T(8,128)} %fusion.41.joint_ref, f32[32,2048]{1,0:T(8,128)} %get-tuple-element.180.cos_ref, f32[32,2048]{1,0:T(8,128)} %get-tuple-element.179.sin_ref, f32[64,2]{1,0:T(8,128)} %bitcast.231, ...), custom_call_target="tpu_custom_call" | custom-call | tf_op jit(solution)/shard_map/joint_tail/pallas_call | solution.py:655
  628.5 16.2 %convolution_convert_fusion.2 = bf16[2048,1280]{1,0:T(8,128)(2,1)} fusion(bf16[2048,1280]{1,0:T(8,128)(2,1)} %get-tuple-element.90, bf16[1024,2048]{1,0:T(8,128)(2,1)S(1)} %copy-done.18, bf16[1024,2048]{1,0:T(8,128)(2,1)S(1)} %copy-done.16), kind=kOutput, calls=%fused_computation.22 | convolution fusion | flops 10756816896 | bytes 18874368 | tf_op jit(solution)/shard_map/dot_general | solution.py:24
  644.7 34.2 %reduce-scatter.11.cloned.1.call-done = bf16[256,2048]{1,0:T(8,128)(2,1)} async-done(((bf16[1024,2048]{1,0:T(8,128)(2,1)}), bf16[256,2048]{1,0:T(8,128)(2,1)}) %reduce-scatter.11.cloned.1.call-update) | async-done | bytes 1048592 | tf_op jit(solution)/shard_map/reduce_scatter | solution.py:387
  681.5 16.8 %convolution_convert_fusion.1 = bf16[2048,1280]{1,0:T(8,128)(2,1)} fusion(bf16[2048,1280]{1,0:T(8,128)(2,1)} %pad_maximum_fusion.5, bf16[1024,2048]{1,0:T(8,128)(2,1)} %copy-done.17, bf16[1024,2048]{1,0:T(8,128)(2,1)} %copy-done.15), kind=kOutput, calls=%fused_computation.21 | convolution fusion | flops 10756816896 | bytes 18874368 | tf_op jit(solution)/shard_map/dot_general | solution.py:24
  749.9 9.5 %reshape_reshape.19 = bf16[2,2,2,256,1280]{3,2,1,0,4:T(2,128)(2,1)} reshape(bf16[2048,1280]{0,1:T(8,128)(2,1)} %fusion.8) | data formatting | bytes 10485760 | tf_op jit(solution)/shard_map/reshape;reshape | solution.py:406
  788.0 16.3 %collective-permute-done.4 = bf16[1,2,256,1024]{3,2,1,0:T(8,128)(2,1)S(1)} collective-permute-done((bf16[1,2,256,1024]{3,2,1,0:T(8,128)(2,1)S(1)}, bf16[1,2,256,1024]{3,2,1,0:T(8,128)(2,1)S(1)}, u32[]{:S(2)}, u32[]{:S(2)}) %collective-permute-start.4) | collective-permute-done | bytes 1048608 | tf_op jit(solution)/shard_map/ppermute | solution.py:411
  806.9 11.2 %collective-permute-done.5 = bf16[1,1,256,1024]{3,2,1,0:T(8,128)(2,1)S(1)} collective-permute-done((bf16[1,1,256,1024]{3,2,1,0:T(8,128)(2,1)S(1)}, bf16[1,1,256,1024]{3,2,1,0:T(8,128)(2,1)S(1)}, u32[]{:S(2)}, u32[]{:S(2)}) %collective-permute-start.5) | collective-permute-done | bytes 524320 | tf_op jit(solution)/shard_map/ppermute | solution.py:411
  849.9 10.6 %collective-permute-done.16 = bf16[1,2,256,1280]{3,2,1,0:T(8,128)(2,1)} collective-permute-done((bf16[1,2,256,1280]{3,2,1,0:T(8,128)(2,1)}, bf16[1,2,256,1280]{3,2,1,0:T(8,128)(2,1)}, u32[]{:S(2)}, u32[]{:S(2)}) %collective-permute-start.16) | collective-permute-done | bytes 1310752 | tf_op jit(solution)/shard_map/ppermute | solution.py:411
  863.8 24.5 %collective-permute-done.19 = bf16[1,2,256,1280]{2,3,1,0:T(8,128)(2,1)} collective-permute-done((bf16[1,2,256,1280]{2,3,1,0:T(8,128)(2,1)}, bf16[1,2,256,1280]{2,3,1,0:T(8,128)(2,1)}, u32[]{:S(2)}, u32[]{:S(2)}) %collective-permute-start.19) | collective-permute-done | bytes 1310752 | tf_op jit(solution)/shard_map/ppermute | solution.py:411
  893.9 12.5 %collective-permute-done.20 = bf16[1,1,256,1280]{2,3,1,0:T(8,128)(2,1)S(1)} collective-permute-done((bf16[1,1,256,1280]{2,3,1,0:T(8,128)(2,1)S(1)}, bf16[1,1,256,1280]{2,3,1,0:T(8,128)(2,1)S(1)}, u32[]{:S(2)}, u32[]{:S(2)}) %collective-permute-start.20) | collective-permute-done | bytes 655392 | tf_op jit(solution)/shard_map/ppermute | solution.py:411
  (296 shorter events, 297.9 us)
Async XLA Ops:
  7.2 70.8 %all-gather.8.cloned.1.call-start = ((), (), s32[]{:S(2)}) async-start(), calls=%async_computation.4 | async-start | bytes 5898240 | tf_op jit(solution)/shard_map/all_gather | solution.py:383
  7.9 107.1 %all-gather.12.cloned.1.call-start = ((), (), s32[]{:S(2)}) async-start(), calls=%async_computation.6 | async-start | bytes 5898240 | tf_op jit(solution)/shard_map/all_gather | solution.py:383
  75.2 99.9 %all-gather.10.cloned.1.call-start = ((), (), s32[]{:S(2)}) async-start(), calls=%async_computation.5 | async-start | bytes 2621440 | tf_op jit(solution)/shard_map/all_gather | solution.py:383
  87.4 149.4 %all-gather.14.cloned.1.call-start = ((), (), s32[]{:S(2)}) async-start(), calls=%async_computation.8 | async-start | bytes 2621440 | tf_op jit(solution)/shard_map/all_gather | solution.py:383
  102.9 254.4 %reduce-scatter.5.cloned.1.call-start = ((), (), s32[]{:S(2)}) async-start(), calls=%async_computation.7 | async-start | bytes 5242880 | tf_op jit(solution)/shard_map/reduce_scatter | solution.py:387
  226.0 155.2 %reduce-scatter.7.cloned.1.call-start = ((), (), s32[]{:S(2)}) async-start(), calls=%async_computation.9 | async-start | bytes 5242880 | tf_op jit(solution)/shard_map/reduce_scatter | solution.py:387
  292.6 185.0 %reduce-scatter.9.cloned.1.call-start = ((), (), s32[]{:S(2)}) async-start(), calls=%async_computation.10 | async-start | bytes 5242880 | tf_op jit(solution)/shard_map/reduce_scatter | solution.py:387
  331.2 313.5 %all-gather.16.cloned.1.call-start = ((), (), s32[]{:S(2)}) async-start(), calls=%async_computation.11 | async-start | bytes 5242880 | tf_op jit(solution)/shard_map/all_gather | solution.py:383
  480.7 198.3 %reduce-scatter.11.cloned.1.call-start = ((), (), s32[]{:S(2)}) async-start(), calls=%async_computation.12 | async-start | bytes 5242880 | tf_op jit(solution)/shard_map/reduce_scatter | solution.py:387
  485.5 422.1 %all-gather.18.cloned.1.call-start = ((), (), s32[]{:S(2)}) async-start(), calls=%async_computation.13 | async-start | bytes 5242880 | tf_op jit(solution)/shard_map/all_gather | solution.py:383
  681.5 243.2 %all-gather.20.cloned.1.call-start = ((), (), s32[]{:S(2)}) async-start(), calls=%async_computation.14 | async-start | bytes 10485760 | tf_op jit(solution)/shard_map/all_gather | solution.py:383
  724.9 2.4 collective-permute-start
  728.2 11.7 %collective-permute-start.1 = (bf16[1,2,256,400]{2,3,1,0:T(8,128)(2,1)}, bf16[1,2,256,400]{2,3,1,0:T(8,128)(2,1)S(1)}, u32[]{:S(2)}, u32[]{:S(2)}) collective-permute-start(bf16[1,2,256,400]{2,3,1,0:T(8,128)(2,1)} %constant_dynamic-slice_fusion.11), channel_id=1, source_target_pairs={{0,16},{8,24},{16,0},{24,8},{1,17},{9,25},{17,1},{25,9},{2,18},{10... | collective-permute-start | bytes 1228808 | tf_op jit(solution)/shard_map/ppermute | solution.py:411
  733.3 46.4 %collective-permute-start.12 = (bf16[2,2,256,1280]{3,2,1,0:T(8,128)(2,1)}, bf16[2,2,256,1280]{3,2,1,0:T(8,128)(2,1)}, u32[]{:S(2)}, u32[]{:S(2)}) collective-permute-start(bf16[2,2,256,1280]{3,2,1,0:T(8,128)(2,1)} %dynamic-slice_bitcast_fusion.1), channel_id=1, source_target_pairs={{0,8},{8,0},{16,24},{24,16},{1,9},{9,1},{17,25},{25,17},{2,10},{10... | collective-permute-start | bytes 7864328 | tf_op jit(solution)/shard_map/ppermute | solution.py:411
  734.8 40.4 %collective-permute-start.3 = (bf16[2,2,256,1024]{3,2,1,0:T(8,128)(2,1)}, bf16[2,2,256,1024]{3,2,1,0:T(8,128)(2,1)S(1)}, u32[]{:S(2)}, u32[]{:S(2)}) collective-permute-start(bf16[2,2,256,1024]{3,2,1,0:T(8,128)(2,1)} %dynamic-slice_bitcast_fusion.2), channel_id=1, source_target_pairs={{0,8},{8,0},{16,24},{24,16},{1,9},{9,1},{17,25},{25,17},{2,10},{10... | collective-permute-start | bytes 6291464 | tf_op jit(solution)/shard_map/ppermute | solution.py:411
  740.1 6.5 collective-permute-start.2
  745.1 38.1 %collective-permute-start.15 = (bf16[2,2,256,1280]{3,2,1,0:T(8,128)(2,1)}, bf16[2,2,256,1280]{3,2,1,0:T(8,128)(2,1)}, u32[]{:S(2)}, u32[]{:S(2)}) collective-permute-start(bf16[2,2,256,1280]{3,2,1,0:T(8,128)(2,1)} %dynamic-slice_bitcast_fusion), channel_id=1, source_target_pairs={{0,8},{8,0},{16,24},{24,16},{1,9},{9,1},{17,25},{25,17},{2,10},{10... | collective-permute-start | bytes 7864328 | tf_op jit(solution)/shard_map/ppermute | solution.py:411
  747.2 12.5 %collective-permute-start.11 = (f32[16,256]{1,0:T(8,128)}, f32[16,256]{1,0:T(8,128)S(1)}, u32[]{:S(2)}, u32[]{:S(2)}) collective-permute-start(f32[16,256]{1,0:T(8,128)} %slice_bitcast_fusion.6), channel_id=1, source_target_pairs={{0,3},{1,0},{2,1},{3,2},{4,7},{5,4},{6,5},{7,6},{8,11},{9,8},{10,9... | collective-permute-start | bytes 49160 | tf_op jit(solution)/shard_map/ppermute | solution.py:430
  759.4 13.9 %collective-permute-start.10 = (f32[16,256]{1,0:T(8,128)}, f32[16,256]{1,0:T(8,128)}, u32[]{:S(2)}, u32[]{:S(2)}) collective-permute-start(f32[16,256]{1,0:T(8,128)} %slice_bitcast_fusion.6), channel_id=1, source_target_pairs={{0,2},{1,3},{2,0},{3,1},{4,6},{5,7},{6,4},{7,5},{8,10},{9,11},{10,... | collective-permute-start | bytes 49160 | tf_op jit(solution)/shard_map/ppermute | solution.py:430
  759.7 13.6 %collective-permute-start.9 = (f32[16,256]{1,0:T(8,128)}, f32[16,256]{1,0:T(8,128)}, u32[]{:S(2)}, u32[]{:S(2)}) collective-permute-start(f32[16,256]{1,0:T(8,128)} %slice_bitcast_fusion.6), channel_id=1, source_target_pairs={{0,1},{1,2},{2,3},{3,0},{4,5},{5,6},{6,7},{7,4},{8,9},{9,10},{10,1... | collective-permute-start | bytes 49160 | tf_op jit(solution)/shard_map/ppermute | solution.py:430
  773.3 33.0 %collective-permute-start.18 = (bf16[2,2,256,1280]{2,3,1,0:T(8,128)(2,1)}, bf16[2,2,256,1280]{2,3,1,0:T(8,128)(2,1)S(1)}, u32[]{:S(2)}, u32[]{:S(2)}) collective-permute-start(bf16[2,2,256,1280]{2,3,1,0:T(8,128)(2,1)} %bitcast.225), channel_id=1, source_target_pairs={{0,8},{8,0},{16,24},{24,16},{1,9},{9,1},{17,25},{25,17},{2,10},{10... | collective-permute-start | bytes 7864328 | tf_op jit(solution)/shard_map/ppermute | solution.py:411
  778.3 26.0 %collective-permute-start.4 = (bf16[1,2,256,1024]{3,2,1,0:T(8,128)(2,1)S(1)}, bf16[1,2,256,1024]{3,2,1,0:T(8,128)(2,1)S(1)}, u32[]{:S(2)}, u32[]{:S(2)}) collective-permute-start(bf16[1,2,256,1024]{3,2,1,0:T(8,128)(2,1)S(1)} %constant_dynamic-slice_fusion.9), channel_id=1, source_target_pairs={{0,16},{8,24},{16,0},{24,8},{1,17},{9,25},{17,1},{25,9},{2,18},{10... | collective-permute-start | bytes 3145736 | tf_op jit(solution)/shard_map/ppermute | solution.py:411
  782.2 51.9 %collective-permute-start.13 = (bf16[1,2,256,1280]{3,2,1,0:T(8,128)(2,1)S(1)}, bf16[1,2,256,1280]{3,2,1,0:T(8,128)(2,1)S(1)}, u32[]{:S(2)}, u32[]{:S(2)}) collective-permute-start(bf16[1,2,256,1280]{3,2,1,0:T(8,128)(2,1)S(1)} %constant_dynamic-slice_fusion.7), channel_id=1, source_target_pairs={{0,16},{8,24},{16,0},{24,8},{1,17},{9,25},{17,1},{25,9},{2,18},{10... | collective-permute-start | bytes 3932168 | tf_op jit(solution)/shard_map/ppermute | solution.py:411
  786.9 73.7 %collective-permute-start.16 = (bf16[1,2,256,1280]{3,2,1,0:T(8,128)(2,1)}, bf16[1,2,256,1280]{3,2,1,0:T(8,128)(2,1)}, u32[]{:S(2)}, u32[]{:S(2)}) collective-permute-start(bf16[1,2,256,1280]{3,2,1,0:T(8,128)(2,1)} %constant_dynamic-slice_fusion.5), channel_id=1, source_target_pairs={{0,16},{8,24},{16,0},{24,8},{1,17},{9,25},{17,1},{25,9},{2,18},{10... | collective-permute-start | bytes 3932168 | tf_op jit(solution)/shard_map/ppermute | solution.py:411
  804.8 13.3 %collective-permute-start.5 = (bf16[1,1,256,1024]{3,2,1,0:T(8,128)(2,1)S(1)}, bf16[1,1,256,1024]{3,2,1,0:T(8,128)(2,1)S(1)}, u32[]{:S(2)}, u32[]{:S(2)}) collective-permute-start(bf16[1,1,256,1024]{3,2,1,0:T(8,128)(2,1)S(1)} %constant_dynamic-slice_fusion.8), channel_id=1, source_target_pairs={{0,4},{4,0},{1,5},{5,1},{2,6},{6,2},{3,7},{7,3},{8,12},{12,8},{9,1... | collective-permute-start | bytes 1572872 | tf_op jit(solution)/shard_map/ppermute | solution.py:411
  818.4 10.2 %collective-permute-start.6 = (bf16[256,256]{0,1:T(8,128)(2,1)S(1)}, bf16[256,256]{0,1:T(8,128)(2,1)S(1)}, u32[]{:S(2)}, u32[]{:S(2)}) collective-permute-start(bf16[256,256]{0,1:T(8,128)(2,1)S(1)} %dynamic-slice_bitcast_fusion.7), channel_id=1, source_target_pairs={{0,1},{1,2},{2,3},{3,0},{4,5},{5,6},{6,7},{7,4},{8,9},{9,10},{10,1... | collective-permute-start | bytes 393224 | tf_op jit(solution)/shard_map/ppermute | solution.py:439
  820.8 67.5 %collective-permute-start.19 = (bf16[1,2,256,1280]{2,3,1,0:T(8,128)(2,1)}, bf16[1,2,256,1280]{2,3,1,0:T(8,128)(2,1)}, u32[]{:S(2)}, u32[]{:S(2)}) collective-permute-start(bf16[1,2,256,1280]{2,3,1,0:T(8,128)(2,1)} %constant_dynamic-slice_fusion.1), channel_id=1, source_target_pairs={{0,16},{8,24},{16,0},{24,8},{1,17},{9,25},{17,1},{25,9},{2,18},{10... | collective-permute-start | bytes 3932168 | tf_op jit(solution)/shard_map/ppermute | solution.py:411
  828.7 14.4 %collective-permute-start.7 = (bf16[256,256]{0,1:T(8,128)(2,1)S(1)}, bf16[256,256]{0,1:T(8,128)(2,1)S(1)}, u32[]{:S(2)}, u32[]{:S(2)}) collective-permute-start(bf16[256,256]{0,1:T(8,128)(2,1)S(1)} %get-tuple-element.171), channel_id=1, source_target_pairs={{0,2},{1,3},{2,0},{3,1},{4,6},{5,7},{6,4},{7,5},{8,10},{9,11},{10,... | collective-permute-start | bytes 393224 | tf_op jit(solution)/shard_map/ppermute | solution.py:439
  833.5 12.5 %collective-permute-start.8 = (bf16[256,256]{0,1:T(8,128)(2,1)S(1)}, bf16[256,256]{0,1:T(8,128)(2,1)S(1)}, u32[]{:S(2)}, u32[]{:S(2)}) collective-permute-start(bf16[256,256]{0,1:T(8,128)(2,1)S(1)} %get-tuple-element.170), channel_id=1, source_target_pairs={{0,3},{1,0},{2,1},{3,2},{4,7},{5,4},{6,5},{7,6},{8,11},{9,8},{10,9... | collective-permute-start | bytes 393224 | tf_op jit(solution)/shard_map/ppermute | solution.py:439
  848.2 43.3 %collective-permute-start.14 = (bf16[1,1,256,1280]{3,2,1,0:T(8,128)(2,1)S(1)}, bf16[1,1,256,1280]{3,2,1,0:T(8,128)(2,1)S(1)}, u32[]{:S(2)}, u32[]{:S(2)}) collective-permute-start(bf16[1,1,256,1280]{3,2,1,0:T(8,128)(2,1)S(1)} %constant_dynamic-slice_fusion.6), channel_id=1, source_target_pairs={{0,4},{4,0},{1,5},{5,1},{2,6},{6,2},{3,7},{7,3},{8,12},{12,8},{9,1... | collective-permute-start | bytes 1966088 | tf_op jit(solution)/shard_map/ppermute | solution.py:411
  862.3 30.5 %collective-permute-start.17 = (bf16[1,1,256,1280]{3,2,1,0:T(8,128)(2,1)S(1)}, bf16[1,1,256,1280]{3,2,1,0:T(8,128)(2,1)S(1)}, u32[]{:S(2)}, u32[]{:S(2)}) collective-permute-start(bf16[1,1,256,1280]{3,2,1,0:T(8,128)(2,1)S(1)} %constant_dynamic-slice_fusion.4), channel_id=1, source_target_pairs={{0,4},{4,0},{1,5},{5,1},{2,6},{6,2},{3,7},{7,3},{8,12},{12,8},{9,1... | collective-permute-start | bytes 1966088 | tf_op jit(solution)/shard_map/ppermute | solution.py:411
  890.0 16.4 %collective-permute-start.20 = (bf16[1,1,256,1280]{2,3,1,0:T(8,128)(2,1)S(1)}, bf16[1,1,256,1280]{2,3,1,0:T(8,128)(2,1)S(1)}, u32[]{:S(2)}, u32[]{:S(2)}) collective-permute-start(bf16[1,1,256,1280]{2,3,1,0:T(8,128)(2,1)S(1)} %constant_dynamic-slice_fusion), channel_id=1, source_target_pairs={{0,4},{4,0},{1,5},{5,1},{2,6},{6,2},{3,7},{7,3},{8,12},{12,8},{9,1... | collective-permute-start | bytes 1966088 | tf_op jit(solution)/shard_map/ppermute | solution.py:411
  (53 other events, 612.3 us)
Sparse Core Ops, SparseCore 0:
  9.9 46.6 all-gather.7
  75.4 39.5 all-gather.11
  116.6 57.1 all-gather.9
  175.2 45.9 all-gather.13
  226.1 75.4 reduce-scatter.4
  303.8 77.2 reduce-scatter.6
  383.4 94.0 reduce-scatter.8
  480.8 120.2 all-gather.15
  604.1 74.8 reduce-scatter.10
  681.6 82.2 all-gather.17
  765.5 159.1 all-gather.19

commit v7 on v6

--- a/solution.py
+++ b/solution.py
@@ -710,7 +710,8 @@
     cos, sin = rope_tables(my_pos)
     gains = qk_gain.T
     queries, kv_mine = prep(joint, cos, sin, gains, heads, 512)
-    out_t, kv = plane_gather([], [w_out.T], [kv_mine], 1)
+    (kv,) = plane_gather([], [], [kv_mine], 1)
+    out_t = jnp.concatenate(list(spread(after(w_out.T, kv))), axis=1)
     up_all = gathered(after(w_up, kv), SHARE, 0)
     queries = after(queries, gate_all)
     chunk_rows = rows // CHUNKS

time: 950 us -> 963 us (1.014)
  starting transfers between devices: 27.4 us -> 42.5 us
  waiting for transfers between devices: 200 us -> 190 us
    ppermute x0 -> x3, starting transfers between devices: none -> 15.3 us  [spread(): lax.ppermute(part, 'tensor', [(i, (i + step) % ways) for i in range(ways)])]
    all_gather x7, waiting for transfers between devices: 20.5 us -> 8.53 us  [gathered(): return lax.all_gather(part, axes, axis=axis, tiled=True)]
    unnamed x113 -> x115, local copies, waits for them, and re-layouts: 27.8 us -> 26.3 us
  transfers between devices with their start and end apart: 32 -> 35, of which waited for: 16 -> 16; matrix products, arithmetic and copies ran while one was open for 40% -> 40% of each run, Pallas kernels for 31% -> 32%
where the time goes in v7:
time: 963 us; the launch traced here: 952 us
  Pallas kernels  302 us (31%)
  matrix products  219 us (23%)
  waiting for transfers between devices  190 us (20%)
  local copies, waits for them, and re-layouts  98.6 us (10%)
  other arithmetic  84.5 us (9%)
  starting transfers between devices  42.5 us (4%)
  between operations  15.2 us (2%)
    pallas_call x4, Pallas kernels, plane_gather(): pl.pallas_call(functools.partial(gather_kernel, len(parts), len(lines), l...  144 us
    ppermute x15, waiting for transfers between devices, halving_scatter(): got = lax.ppermute(sent, axis, [(i, i ^ stride) for i in range(size)])  83.6 us
    pallas_call x1, Pallas kernels, joint_tail(): pl.pallas_call(functools.partial(tail_kernel, heads, ways, chunks), out_s...  83.1 us
    reduce_scatter x4, waiting for transfers between devices, scattered(): lax.psum_scatter(part.astype(bf16), axes, scatter_dimension=axis, tiled=T...  77.8 us
    dot_general x9, matrix products, dot_nn(): lax.dot_general(a, b, (((1,), (0,)), ((), ())), preferred_element_type=f32)  76.1 us
    dot_general x6, matrix products, dot_nt(): lax.dot_general(a, b, (((1,), (1,)), ((), ())), preferred_element_type=f32)  61 us
    dot_general x3, matrix products, dot_tn(): lax.dot_general(a, b, (((0,), (0,)), ((), ())), preferred_element_type=f32)  49.9 us
    pallas_call x2, Pallas kernels, attention_grad(): pl.pallas_call(functools.partial(bwd_kernel, heads, bq, bk, final), out_s...  47.6 us
  transfers between devices with their start and end apart: 35, of which 16 were waited for; matrix products, arithmetic and copies ran while one was open for 40% of the time, Pallas kernels for 32%

profile of v7, /device:TPU:0, one launch (start us, length us, event | category | flops | bytes accessed | tf_op | source)
XLA Modules:
  0.0 951.9 jit_solution(10981066604360381862)
XLA Ops:
  11.3 21.1 %plane_gather.4 = bf16[2048,400]{1,0:T(8,128)(2,1)} custom-call(bf16[256,400]{1,0:T(8,128)(2,1)} %maximum_bitcast_fusion.1.refs_0_), custom_call_target="tpu_custom_call" | custom-call | tf_op jit(solution)/shard_map/plane_gather/pallas_call | solution.py:576
  54.6 15.6 %plane_gather.5.kv_ref = bf16[4096,128]{1,0:T(8,128)(2,1)} custom-call(bf16[2048,128]{1,0:T(8,128)(2,1)} %get-tuple-element.55.refs_0_), custom_call_target="tpu_custom_call" | custom-call | tf_op jit(solution)/shard_map/plane_gather/pallas_call | solution.py:576
  86.7 11.1 %collective-permute-start.2 = (bf16[256,256]{1,0:T(8,128)(2,1)S(1)}, bf16[256,256]{1,0:T(8,128)(2,1)S(1)}, u32[]{:S(2)}, u32[]{:S(2)}) collective-permute-start(bf16[256,256]{1,0:T(8,128)(2,1)S(1)} %bitcast.247), channel_id=1, source_target_pairs={{0,3},{1,0},{2,1},{3,2},{4,7},{5,4},{6,5},{7,6},{8,11},{9,8},{10,9... | collective-permute-start | bytes 393224 | tf_op jit(solution)/shard_map/ppermute | solution.py:421
  102.4 14.2 %attend.3 = (bf16[256,1024]{1,0:T(8,128)(2,1)}, f32[4,1024]{1,0:T(4,128)}) custom-call(s32[1]{0:T(128)S(6)} %add.337.start_ref, s32[4096]{0:T(1024)} %bitcast.253, bf16[256,2048]{1,0:T(8,128)(2,1)} %get-tuple-element.54.q_ref, bf16[4096,128]{1,0:T(8,128)(2,1)} %plane_gather.5.kv_ref, s32[2048,1]{1,0:T(8,128)} %copy.88.qpos_ref, s32[2048,1]{1,0:T(8,128)} %copy.89.qseg_ref, ...), custom_call_target="tpu_custom_call" | custom-call | flops 4294967296 | bytes 4194304 | tf_op jit(solution)/shard_map/attend/pallas_call | solution.py:198
  116.7 60.8 %plane_gather.6 = (bf16[2048,1024]{1,0:T(8,128)(2,1)}, bf16[2048,1280]{1,0:T(8,128)(2,1)}, bf16[256,1536]{1,0:T(8,128)(2,1)}) custom-call(bf16[256,1024]{1,0:T(8,128)(2,1)} %pad_maximum_fusion.9.refs_0_, bf16[256,1280]{1,0:T(8,128)(2,1)} %bitcast.242, bf16[256,384]{1,0:T(8,128)(2,1)} %refs_2_.1), custom_call_target="tpu_custom_call" | custom-call | tf_op jit(solution)/shard_map/plane_gather/pallas_call | solution.py:576
  177.6 10.5 %convolution_bitcast_fusion.1 = f32[1024,1280]{1,0:T(8,128)} fusion(bf16[2048,1280]{1,0:T(8,128)(2,1)} %get-tuple-element.66, bf16[1,2048,2048]{2,1,0:T(8,128)(2,1)} %param.13), kind=kOutput, calls=%fused_computation.52 | convolution fusion | flops 5368709120 | bytes 14680064 | tf_op jit(solution)/shard_map/dot_general | solution.py:21
  207.9 11.7 %multiply_convert_fusion.3 = (bf16[1024,1280]{1,0:T(8,128)(2,1)S(1)}, bf16[1024,1280]{1,0:T(8,128)(2,1)S(1)}, bf16[1024,1280]{1,0:T(8,128)(2,1)S(1)}) fusion(f32[1024,1280]{1,0:T(8,128)} %fusion.78, f32[1024,1280]{1,0:T(8,128)} %convolution_bitcast_fusion.1, bf16[1024,2048]{1,0:T(8,128)(2,1)S(1)} %multiply_convert_fusion.1, ...), kind=kOutput, calls=%fused_computation.42 | convolution fusion | flops 5389680640 | bytes 27787264 | tf_op jit(solution)/shard_map/dot_general | solution.py:21
  219.6 9.5 fusion.79
  229.1 9.7 %add_convert_fusion.1 = bf16[1024,2048]{1,0:T(8,128)(2,1)} fusion(f32[1024,2048]{1,0:T(8,128)S(1)} %fusion.79, bf16[1024,1280]{1,0:T(8,128)(2,1)S(1)} %get-tuple-element.154, bf16[2048,1280]{1,0:T(8,128)(2,1)} %all-gather.12.cloned.1.call-done), kind=kOutput, calls=%fused_computation.14 | convolution fusion | flops 5372903424 | bytes 20447232 | tf_op jit(solution)/shard_map/dot_general | solution.py:18
  239.0 10.9 %convolution_bitcast_fusion = f32[1024,1280]{1,0:T(8,128)} fusion(bf16[2048,1280]{1,0:T(8,128)(2,1)} %get-tuple-element.66, bf16[1,2048,2048]{2,1,0:T(8,128)(2,1)} %param.13), kind=kOutput, calls=%fused_computation.51 | convolution fusion | flops 5368709120 | bytes 14680064 | tf_op jit(solution)/shard_map/dot_general | solution.py:21
  262.2 11.4 %fusion.80 = f32[1024,1280]{1,0:T(8,128)} fusion(bf16[1024,2048]{1,0:T(8,128)(2,1)S(1)} %multiply_convert_fusion, bf16[2048,1280]{1,0:T(8,128)(2,1)} %all-gather.8.cloned.1.call-done), kind=kOutput, calls=%fused_computation.207 | convolution fusion | flops 5368709120 | bytes 14680064 | tf_op jit(solution)/shard_map/dot_general | solution.py:21
  273.6 12.7 %multiply_convert_fusion.2 = (bf16[1024,1280]{1,0:T(8,128)(2,1)}, bf16[1024,1280]{1,0:T(8,128)(2,1)S(1)}, bf16[1024,1280]{1,0:T(8,128)(2,1)S(1)}) fusion(f32[1024,1280]{1,0:T(8,128)} %fusion.80, f32[1024,1280]{1,0:T(8,128)} %convolution_bitcast_fusion, bf16[1024,2048]{1,0:T(8,128)(2,1)S(1)} %multiply_convert_fusion, ...), kind=kOutput, calls=%fused_computation.41 | convolution fusion | flops 5389680640 | bytes 27787264 | tf_op jit(solution)/shard_map/dot_general | solution.py:21
  286.3 9.5 fusion.81
  295.8 9.8 %add_convert_fusion = bf16[1024,2048]{1,0:T(8,128)(2,1)} fusion(f32[1024,2048]{1,0:T(8,128)S(1)} %fusion.81, bf16[1024,1280]{1,0:T(8,128)(2,1)S(1)} %get-tuple-element.157, bf16[2048,1280]{1,0:T(8,128)(2,1)} %all-gather.12.cloned.1.call-done), kind=kOutput, calls=%fused_computation.11 | convolution fusion | flops 5372903424 | bytes 20447232 | tf_op jit(solution)/shard_map/dot_general | solution.py:18
  312.5 10.8 %pad_maximum_fusion.3 = (bf16[2048,1280]{1,0:T(8,128)(2,1)S(1)}, bf16[2048,1280]{1,0:T(8,128)(2,1)}) fusion(bf16[1024,1280]{1,0:T(8,128)(2,1)S(1)} %copy-done.25, bf16[1024,1280]{1,0:T(8,128)(2,1)S(1)} %get-tuple-element.152, bf16[1024,1280]{1,0:T(8,128)(2,1)S(1)} %copy-done.27, bf16[1024,1280]{1,0:T(8,128)(2,1)S(1)} %copy-done.23), kind=kLoop, calls=%fused_computation.32 | loop fusion | flops 20971520 | bytes 20971520 | tf_op jit(solution)/shard_map/concatenate | solution.py:753
  323.2 15.4 %convolution_convert_fusion = bf16[2048,2048]{1,0:T(8,128)(2,1)S(1)} fusion(bf16[2048,1280]{1,0:T(8,128)(2,1)S(1)} %get-tuple-element.68, bf16[2048,1280]{1,0:T(8,128)(2,1)} %get-tuple-element.66), kind=kOutput, calls=%fused_computation.20 | convolution fusion | flops 10741612544 | bytes 18874368 | tf_op jit(solution)/shard_map/dot_general | solution.py:18
  353.5 16.9 %fusion.8 = bf16[2048,1280]{0,1:T(8,128)(2,1)} fusion(bf16[2048,1280]{1,0:T(8,128)(2,1)} %copy-done.13, bf16[1,2048,2048]{2,1,0:T(8,128)(2,1)} %param.13), kind=kOutput, calls=%fused_computation.23 | convolution fusion | flops 10740039680 | bytes 18874368 | tf_op jit(solution)/shard_map/dot_general | solution.py:24
  370.4 24.2 %reduce-scatter.7.cloned.1.call-done = bf16[256,2048]{1,0:T(8,128)(2,1)} async-done(((bf16[1024,2048]{1,0:T(8,128)(2,1)}), bf16[256,2048]{1,0:T(8,128)(2,1)}) %reduce-scatter.7.cloned.1.call-update) | async-done | bytes 1048592 | tf_op jit(solution)/shard_map/reduce_scatter | solution.py:387
  406.8 46.2 %plane_gather.7 = (bf16[2048,1536]{1,0:T(8,128)(2,1)}, bf16[2048,256]{1,0:T(8,128)(2,1)}) custom-call(bf16[256,1536]{1,0:T(8,128)(2,1)} %get-tuple-element.65.refs_0_, bf16[512,1024]{1,0:T(8,128)(2,1)} %pad_maximum_fusion.8.refs_1_), custom_call_target="tpu_custom_call" | custom-call | tf_op jit(solution)/shard_map/plane_gather/pallas_call | solution.py:576
  453.0 18.0 %attend_grad.2 = (f32[256,1024]{1,0:T(8,128)}, f32[4096,128]{1,0:T(8,128)}) custom-call(s32[1]{0:T(128)} %bitcast.1.start_ref, s32[4096]{0:T(1024)} %bitcast.255, bf16[256,2048]{1,0:T(8,128)(2,1)} %get-tuple-element.54.q_ref, bf16[4096,128]{1,0:T(8,128)(2,1)} %plane_gather.5.kv_ref, bf16[256,1024]{1,0:T(8,128)(2,1)} %get-tuple-element.56.o_ref, ...), custom_call_target="tpu_custom_call" | custom-call | flops 10737418240 | bytes 8388608 | tf_op jit(solution)/shard_map/attend_grad/pallas_call | solution.py:319
  470.9 20.1 %reduce-scatter.9.cloned.1.call-done = bf16[256,2048]{1,0:T(8,128)(2,1)} async-done(((bf16[1024,2048]{1,0:T(8,128)(2,1)}), bf16[256,2048]{1,0:T(8,128)(2,1)}) %reduce-scatter.9.cloned.1.call-update) | async-done | bytes 1048592 | tf_op jit(solution)/shard_map/reduce_scatter | solution.py:387
  507.2 29.6 %attend_grad.3 = (f32[256,1024]{1,0:T(8,128)}, bf16[4096,128]{1,0:T(8,128)(2,1)}) custom-call(s32[1]{0:T(128)S(6)} %add.337.start_ref, s32[4096]{0:T(1024)} %bitcast.256, bf16[256,2048]{1,0:T(8,128)(2,1)} %get-tuple-element.54.q_ref, bf16[4096,128]{1,0:T(8,128)(2,1)} %plane_gather.5.kv_ref, bf16[256,1024]{1,0:T(8,128)(2,1)} %get-tuple-element.59.o_ref, ...), custom_call_target="tpu_custom_call" | custom-call | flops 10737418240 | bytes 8388608 | tf_op jit(solution)/shard_map/attend_grad/pallas_call | solution.py:319
  539.1 83.1 %joint_tail.1 = (bf16[384,2048]{1,0:T(8,128)(2,1)}, bf16[1536,512]{1,0:T(8,128)(2,1)}, f32[64,2]{1,0:T(8,128)}) custom-call(f32[384,2048]{1,0:T(8,128)} %fusion.41.joint_ref, f32[32,2048]{1,0:T(8,128)} %get-tuple-element.182.cos_ref, f32[32,2048]{1,0:T(8,128)} %get-tuple-element.181.sin_ref, f32[64,2]{1,0:T(8,128)} %bitcast.250, ...), custom_call_target="tpu_custom_call" | custom-call | tf_op jit(solution)/shard_map/joint_tail/pallas_call | solution.py:655
  641.2 16.2 %convolution_convert_fusion.2 = bf16[2048,1280]{1,0:T(8,128)(2,1)} fusion(bf16[2048,1280]{1,0:T(8,128)(2,1)} %get-tuple-element.88, bf16[1024,2048]{1,0:T(8,128)(2,1)S(1)} %copy-done.18, bf16[1024,2048]{1,0:T(8,128)(2,1)S(1)} %copy-done.16), kind=kOutput, calls=%fused_computation.22 | convolution fusion | flops 10756816896 | bytes 18874368 | tf_op jit(solution)/shard_map/dot_general | solution.py:24
  657.4 33.5 %reduce-scatter.11.cloned.1.call-done = bf16[256,2048]{1,0:T(8,128)(2,1)} async-done(((bf16[1024,2048]{1,0:T(8,128)(2,1)}), bf16[256,2048]{1,0:T(8,128)(2,1)}) %reduce-scatter.11.cloned.1.call-update) | async-done | bytes 1048592 | tf_op jit(solution)/shard_map/reduce_scatter | solution.py:387
  693.5 16.8 %convolution_convert_fusion.1 = bf16[2048,1280]{1,0:T(8,128)(2,1)} fusion(bf16[2048,1280]{1,0:T(8,128)(2,1)} %pad_maximum_fusion.5, bf16[1024,2048]{1,0:T(8,128)(2,1)} %copy-done.17, bf16[1024,2048]{1,0:T(8,128)(2,1)} %copy-done.15), kind=kOutput, calls=%fused_computation.21 | convolution fusion | flops 10756816896 | bytes 18874368 | tf_op jit(solution)/shard_map/dot_general | solution.py:24
  761.9 9.5 reshape_reshape.19
  799.9 16.3 %collective-permute-done.7 = bf16[1,2,256,1024]{3,2,1,0:T(8,128)(2,1)S(1)} collective-permute-done((bf16[1,2,256,1024]{3,2,1,0:T(8,128)(2,1)S(1)}, bf16[1,2,256,1024]{3,2,1,0:T(8,128)(2,1)S(1)}, u32[]{:S(2)}, u32[]{:S(2)}) %collective-permute-start.7) | collective-permute-done | bytes 1048608 | tf_op jit(solution)/shard_map/ppermute | solution.py:411
  818.8 11.2 %collective-permute-done.8 = bf16[1,1,256,1024]{3,2,1,0:T(8,128)(2,1)S(1)} collective-permute-done((bf16[1,1,256,1024]{3,2,1,0:T(8,128)(2,1)S(1)}, bf16[1,1,256,1024]{3,2,1,0:T(8,128)(2,1)S(1)}, u32[]{:S(2)}, u32[]{:S(2)}) %collective-permute-start.8) | collective-permute-done | bytes 524320 | tf_op jit(solution)/shard_map/ppermute | solution.py:411
  861.8 10.7 %collective-permute-done.19 = bf16[1,2,256,1280]{3,2,1,0:T(8,128)(2,1)} collective-permute-done((bf16[1,2,256,1280]{3,2,1,0:T(8,128)(2,1)}, bf16[1,2,256,1280]{3,2,1,0:T(8,128)(2,1)}, u32[]{:S(2)}, u32[]{:S(2)}) %collective-permute-start.19) | collective-permute-done | bytes 1310752 | tf_op jit(solution)/shard_map/ppermute | solution.py:411
  875.7 24.5 %collective-permute-done.22 = bf16[1,2,256,1280]{2,3,1,0:T(8,128)(2,1)} collective-permute-done((bf16[1,2,256,1280]{2,3,1,0:T(8,128)(2,1)}, bf16[1,2,256,1280]{2,3,1,0:T(8,128)(2,1)}, u32[]{:S(2)}, u32[]{:S(2)}) %collective-permute-start.22) | collective-permute-done | bytes 1310752 | tf_op jit(solution)/shard_map/ppermute | solution.py:411
  905.9 12.5 %collective-permute-done.23 = bf16[1,1,256,1280]{2,3,1,0:T(8,128)(2,1)S(1)} collective-permute-done((bf16[1,1,256,1280]{2,3,1,0:T(8,128)(2,1)S(1)}, bf16[1,1,256,1280]{2,3,1,0:T(8,128)(2,1)S(1)}, u32[]{:S(2)}, u32[]{:S(2)}) %collective-permute-start.23) | collective-permute-done | bytes 655392 | tf_op jit(solution)/shard_map/ppermute | solution.py:411
  (311 shorter events, 302.9 us)
Async XLA Ops:
  7.2 65.8 %all-gather.8.cloned.1.call-start = ((), (), s32[]{:S(2)}) async-start(), calls=%async_computation.4 | async-start | bytes 5898240 | tf_op jit(solution)/shard_map/all_gather | solution.py:383
  7.9 108.8 %all-gather.12.cloned.1.call-start = ((), (), s32[]{:S(2)}) async-start(), calls=%async_computation.6 | async-start | bytes 5898240 | tf_op jit(solution)/shard_map/all_gather | solution.py:383
  70.2 117.9 %all-gather.10.cloned.1.call-start = ((), (), s32[]{:S(2)}) async-start(), calls=%async_computation.5 | async-start | bytes 2621440 | tf_op jit(solution)/shard_map/all_gather | solution.py:383
  82.3 167.5 %all-gather.14.cloned.1.call-start = ((), (), s32[]{:S(2)}) async-start(), calls=%async_computation.8 | async-start | bytes 2621440 | tf_op jit(solution)/shard_map/all_gather | solution.py:383
  82.5 16.5 %collective-permute-start = (bf16[256,256]{1,0:T(8,128)(2,1)S(1)}, bf16[256,256]{1,0:T(8,128)(2,1)S(1)}, u32[]{:S(2)}, u32[]{:S(2)}) collective-permute-start(bf16[256,256]{1,0:T(8,128)(2,1)S(1)} %bitcast.245), channel_id=1, source_target_pairs={{0,1},{1,2},{2,3},{3,0},{4,5},{5,6},{6,7},{7,4},{8,9},{9,10},{10,1... | collective-permute-start | bytes 393224 | tf_op jit(solution)/shard_map/ppermute | solution.py:421
  84.0 15.0 %collective-permute-start.1 = (bf16[256,256]{1,0:T(8,128)(2,1)S(1)}, bf16[256,256]{1,0:T(8,128)(2,1)S(1)}, u32[]{:S(2)}, u32[]{:S(2)}) collective-permute-start(bf16[256,256]{1,0:T(8,128)(2,1)S(1)} %bitcast.246), channel_id=1, source_target_pairs={{0,2},{1,3},{2,0},{3,1},{4,6},{5,7},{6,4},{7,5},{8,10},{9,11},{10,... | collective-permute-start | bytes 393224 | tf_op jit(solution)/shard_map/ppermute | solution.py:421
  86.7 14.8 %collective-permute-start.2 = (bf16[256,256]{1,0:T(8,128)(2,1)S(1)}, bf16[256,256]{1,0:T(8,128)(2,1)S(1)}, u32[]{:S(2)}, u32[]{:S(2)}) collective-permute-start(bf16[256,256]{1,0:T(8,128)(2,1)S(1)} %bitcast.247), channel_id=1, source_target_pairs={{0,3},{1,0},{2,1},{3,2},{4,7},{5,4},{6,5},{7,6},{8,11},{9,8},{10,9... | collective-permute-start | bytes 393224 | tf_op jit(solution)/shard_map/ppermute | solution.py:421
  116.6 253.7 %reduce-scatter.5.cloned.1.call-start = ((), (), s32[]{:S(2)}) async-start(), calls=%async_computation.7 | async-start | bytes 5242880 | tf_op jit(solution)/shard_map/reduce_scatter | solution.py:387
  238.9 155.7 %reduce-scatter.7.cloned.1.call-start = ((), (), s32[]{:S(2)}) async-start(), calls=%async_computation.9 | async-start | bytes 5242880 | tf_op jit(solution)/shard_map/reduce_scatter | solution.py:387
  305.6 185.4 %reduce-scatter.9.cloned.1.call-start = ((), (), s32[]{:S(2)}) async-start(), calls=%async_computation.10 | async-start | bytes 5242880 | tf_op jit(solution)/shard_map/reduce_scatter | solution.py:387
  344.3 313.1 %all-gather.16.cloned.1.call-start = ((), (), s32[]{:S(2)}) async-start(), calls=%async_computation.11 | async-start | bytes 5242880 | tf_op jit(solution)/shard_map/all_gather | solution.py:383
  494.2 196.7 %reduce-scatter.11.cloned.1.call-start = ((), (), s32[]{:S(2)}) async-start(), calls=%async_computation.12 | async-start | bytes 5242880 | tf_op jit(solution)/shard_map/reduce_scatter | solution.py:387
  499.0 420.6 %all-gather.18.cloned.1.call-start = ((), (), s32[]{:S(2)}) async-start(), calls=%async_computation.13 | async-start | bytes 5242880 | tf_op jit(solution)/shard_map/all_gather | solution.py:383
  693.4 243.2 %all-gather.20.cloned.1.call-start = ((), (), s32[]{:S(2)}) async-start(), calls=%async_computation.14 | async-start | bytes 10485760 | tf_op jit(solution)/shard_map/all_gather | solution.py:383
  740.2 11.7 %collective-permute-start.4 = (bf16[1,2,256,400]{2,3,1,0:T(8,128)(2,1)}, bf16[1,2,256,400]{2,3,1,0:T(8,128)(2,1)S(1)}, u32[]{:S(2)}, u32[]{:S(2)}) collective-permute-start(bf16[1,2,256,400]{2,3,1,0:T(8,128)(2,1)} %constant_dynamic-slice_fusion.11), channel_id=1, source_target_pairs={{0,16},{8,24},{16,0},{24,8},{1,17},{9,25},{17,1},{25,9},{2,18},{10... | collective-permute-start | bytes 1228808 | tf_op jit(solution)/shard_map/ppermute | solution.py:411
  745.3 46.4 %collective-permute-start.15 = (bf16[2,2,256,1280]{3,2,1,0:T(8,128)(2,1)}, bf16[2,2,256,1280]{3,2,1,0:T(8,128)(2,1)}, u32[]{:S(2)}, u32[]{:S(2)}) collective-permute-start(bf16[2,2,256,1280]{3,2,1,0:T(8,128)(2,1)} %dynamic-slice_bitcast_fusion.1), channel_id=1, source_target_pairs={{0,8},{8,0},{16,24},{24,16},{1,9},{9,1},{17,25},{25,17},{2,10},{10... | collective-permute-start | bytes 7864328 | tf_op jit(solution)/shard_map/ppermute | solution.py:411
  746.8 40.4 %collective-permute-start.6 = (bf16[2,2,256,1024]{3,2,1,0:T(8,128)(2,1)}, bf16[2,2,256,1024]{3,2,1,0:T(8,128)(2,1)S(1)}, u32[]{:S(2)}, u32[]{:S(2)}) collective-permute-start(bf16[2,2,256,1024]{3,2,1,0:T(8,128)(2,1)} %dynamic-slice_bitcast_fusion.2), channel_id=1, source_target_pairs={{0,8},{8,0},{16,24},{24,16},{1,9},{9,1},{17,25},{25,17},{2,10},{10... | collective-permute-start | bytes 6291464 | tf_op jit(solution)/shard_map/ppermute | solution.py:411
  757.1 38.1 %collective-permute-start.18 = (bf16[2,2,256,1280]{3,2,1,0:T(8,128)(2,1)}, bf16[2,2,256,1280]{3,2,1,0:T(8,128)(2,1)}, u32[]{:S(2)}, u32[]{:S(2)}) collective-permute-start(bf16[2,2,256,1280]{3,2,1,0:T(8,128)(2,1)} %dynamic-slice_bitcast_fusion), channel_id=1, source_target_pairs={{0,8},{8,0},{16,24},{24,16},{1,9},{9,1},{17,25},{25,17},{2,10},{10... | collective-permute-start | bytes 7864328 | tf_op jit(solution)/shard_map/ppermute | solution.py:411
  759.2 12.5 %collective-permute-start.14 = (f32[16,256]{1,0:T(8,128)}, f32[16,256]{1,0:T(8,128)S(1)}, u32[]{:S(2)}, u32[]{:S(2)}) collective-permute-start(f32[16,256]{1,0:T(8,128)} %slice_bitcast_fusion.10), channel_id=1, source_target_pairs={{0,3},{1,0},{2,1},{3,2},{4,7},{5,4},{6,5},{7,6},{8,11},{9,8},{10,9... | collective-permute-start | bytes 49160 | tf_op jit(solution)/shard_map/ppermute | solution.py:430
  771.4 13.9 %collective-permute-start.13 = (f32[16,256]{1,0:T(8,128)}, f32[16,256]{1,0:T(8,128)}, u32[]{:S(2)}, u32[]{:S(2)}) collective-permute-start(f32[16,256]{1,0:T(8,128)} %slice_bitcast_fusion.10), channel_id=1, source_target_pairs={{0,2},{1,3},{2,0},{3,1},{4,6},{5,7},{6,4},{7,5},{8,10},{9,11},{10,... | collective-permute-start | bytes 49160 | tf_op jit(solution)/shard_map/ppermute | solution.py:430
  771.7 13.6 %collective-permute-start.12 = (f32[16,256]{1,0:T(8,128)}, f32[16,256]{1,0:T(8,128)}, u32[]{:S(2)}, u32[]{:S(2)}) collective-permute-start(f32[16,256]{1,0:T(8,128)} %slice_bitcast_fusion.10), channel_id=1, source_target_pairs={{0,1},{1,2},{2,3},{3,0},{4,5},{5,6},{6,7},{7,4},{8,9},{9,10},{10,1... | collective-permute-start | bytes 49160 | tf_op jit(solution)/shard_map/ppermute | solution.py:430
  785.2 32.9 %collective-permute-start.21 = (bf16[2,2,256,1280]{2,3,1,0:T(8,128)(2,1)}, bf16[2,2,256,1280]{2,3,1,0:T(8,128)(2,1)S(1)}, u32[]{:S(2)}, u32[]{:S(2)}) collective-permute-start(bf16[2,2,256,1280]{2,3,1,0:T(8,128)(2,1)} %bitcast.241), channel_id=1, source_target_pairs={{0,8},{8,0},{16,24},{24,16},{1,9},{9,1},{17,25},{25,17},{2,10},{10... | collective-permute-start | bytes 7864328 | tf_op jit(solution)/shard_map/ppermute | solution.py:411
  790.2 26.0 %collective-permute-start.7 = (bf16[1,2,256,1024]{3,2,1,0:T(8,128)(2,1)S(1)}, bf16[1,2,256,1024]{3,2,1,0:T(8,128)(2,1)S(1)}, u32[]{:S(2)}, u32[]{:S(2)}) collective-permute-start(bf16[1,2,256,1024]{3,2,1,0:T(8,128)(2,1)S(1)} %constant_dynamic-slice_fusion.9), channel_id=1, source_target_pairs={{0,16},{8,24},{16,0},{24,8},{1,17},{9,25},{17,1},{25,9},{2,18},{10... | collective-permute-start | bytes 3145736 | tf_op jit(solution)/shard_map/ppermute | solution.py:411
  794.2 51.9 %collective-permute-start.16 = (bf16[1,2,256,1280]{3,2,1,0:T(8,128)(2,1)S(1)}, bf16[1,2,256,1280]{3,2,1,0:T(8,128)(2,1)S(1)}, u32[]{:S(2)}, u32[]{:S(2)}) collective-permute-start(bf16[1,2,256,1280]{3,2,1,0:T(8,128)(2,1)S(1)} %constant_dynamic-slice_fusion.7), channel_id=1, source_target_pairs={{0,16},{8,24},{16,0},{24,8},{1,17},{9,25},{17,1},{25,9},{2,18},{10... | collective-permute-start | bytes 3932168 | tf_op jit(solution)/shard_map/ppermute | solution.py:411
  798.8 73.7 %collective-permute-start.19 = (bf16[1,2,256,1280]{3,2,1,0:T(8,128)(2,1)}, bf16[1,2,256,1280]{3,2,1,0:T(8,128)(2,1)}, u32[]{:S(2)}, u32[]{:S(2)}) collective-permute-start(bf16[1,2,256,1280]{3,2,1,0:T(8,128)(2,1)} %constant_dynamic-slice_fusion.5), channel_id=1, source_target_pairs={{0,16},{8,24},{16,0},{24,8},{1,17},{9,25},{17,1},{25,9},{2,18},{10... | collective-permute-start | bytes 3932168 | tf_op jit(solution)/shard_map/ppermute | solution.py:411
  816.7 13.3 %collective-permute-start.8 = (bf16[1,1,256,1024]{3,2,1,0:T(8,128)(2,1)S(1)}, bf16[1,1,256,1024]{3,2,1,0:T(8,128)(2,1)S(1)}, u32[]{:S(2)}, u32[]{:S(2)}) collective-permute-start(bf16[1,1,256,1024]{3,2,1,0:T(8,128)(2,1)S(1)} %constant_dynamic-slice_fusion.8), channel_id=1, source_target_pairs={{0,4},{4,0},{1,5},{5,1},{2,6},{6,2},{3,7},{7,3},{8,12},{12,8},{9,1... | collective-permute-start | bytes 1572872 | tf_op jit(solution)/shard_map/ppermute | solution.py:411
  832.7 67.5 %collective-permute-start.22 = (bf16[1,2,256,1280]{2,3,1,0:T(8,128)(2,1)}, bf16[1,2,256,1280]{2,3,1,0:T(8,128)(2,1)}, u32[]{:S(2)}, u32[]{:S(2)}) collective-permute-start(bf16[1,2,256,1280]{2,3,1,0:T(8,128)(2,1)} %constant_dynamic-slice_fusion.1), channel_id=1, source_target_pairs={{0,16},{8,24},{16,0},{24,8},{1,17},{9,25},{17,1},{25,9},{2,18},{10... | collective-permute-start | bytes 3932168 | tf_op jit(solution)/shard_map/ppermute | solution.py:411
  840.6 14.4 %collective-permute-start.10 = (bf16[256,256]{0,1:T(8,128)(2,1)S(1)}, bf16[256,256]{0,1:T(8,128)(2,1)S(1)}, u32[]{:S(2)}, u32[]{:S(2)}) collective-permute-start(bf16[256,256]{0,1:T(8,128)(2,1)S(1)} %get-tuple-element.169), channel_id=1, source_target_pairs={{0,2},{1,3},{2,0},{3,1},{4,6},{5,7},{6,4},{7,5},{8,10},{9,11},{10,... | collective-permute-start | bytes 393224 | tf_op jit(solution)/shard_map/ppermute | solution.py:439
  845.5 12.5 %collective-permute-start.11 = (bf16[256,256]{0,1:T(8,128)(2,1)S(1)}, bf16[256,256]{0,1:T(8,128)(2,1)S(1)}, u32[]{:S(2)}, u32[]{:S(2)}) collective-permute-start(bf16[256,256]{0,1:T(8,128)(2,1)S(1)} %get-tuple-element.168), channel_id=1, source_target_pairs={{0,3},{1,0},{2,1},{3,2},{4,7},{5,4},{6,5},{7,6},{8,11},{9,8},{10,9... | collective-permute-start | bytes 393224 | tf_op jit(solution)/shard_map/ppermute | solution.py:439
  860.2 43.3 %collective-permute-start.17 = (bf16[1,1,256,1280]{3,2,1,0:T(8,128)(2,1)S(1)}, bf16[1,1,256,1280]{3,2,1,0:T(8,128)(2,1)S(1)}, u32[]{:S(2)}, u32[]{:S(2)}) collective-permute-start(bf16[1,1,256,1280]{3,2,1,0:T(8,128)(2,1)S(1)} %constant_dynamic-slice_fusion.6), channel_id=1, source_target_pairs={{0,4},{4,0},{1,5},{5,1},{2,6},{6,2},{3,7},{7,3},{8,12},{12,8},{9,1... | collective-permute-start | bytes 1966088 | tf_op jit(solution)/shard_map/ppermute | solution.py:411
  874.2 30.5 %collective-permute-start.20 = (bf16[1,1,256,1280]{3,2,1,0:T(8,128)(2,1)S(1)}, bf16[1,1,256,1280]{3,2,1,0:T(8,128)(2,1)S(1)}, u32[]{:S(2)}, u32[]{:S(2)}) collective-permute-start(bf16[1,1,256,1280]{3,2,1,0:T(8,128)(2,1)S(1)} %constant_dynamic-slice_fusion.4), channel_id=1, source_target_pairs={{0,4},{4,0},{1,5},{5,1},{2,6},{6,2},{3,7},{7,3},{8,12},{12,8},{9,1... | collective-permute-start | bytes 1966088 | tf_op jit(solution)/shard_map/ppermute | solution.py:411
  902.0 16.4 %collective-permute-start.23 = (bf16[1,1,256,1280]{2,3,1,0:T(8,128)(2,1)S(1)}, bf16[1,1,256,1280]{2,3,1,0:T(8,128)(2,1)S(1)}, u32[]{:S(2)}, u32[]{:S(2)}) collective-permute-start(bf16[1,1,256,1280]{2,3,1,0:T(8,128)(2,1)S(1)} %constant_dynamic-slice_fusion), channel_id=1, source_target_pairs={{0,4},{4,0},{1,5},{5,1},{2,6},{6,2},{3,7},{7,3},{8,12},{12,8},{9,1... | collective-permute-start | bytes 1966088 | tf_op jit(solution)/shard_map/ppermute | solution.py:411
  (57 other events, 648.6 us)
Sparse Core Ops, SparseCore 0:
  9.9 46.6 all-gather.7
  70.3 40.8 all-gather.11
  112.8 62.6 all-gather.9
  176.9 44.6 all-gather.13
  239.0 75.9 reduce-scatter.4
  317.3 77.2 reduce-scatter.6
  396.9 94.0 reduce-scatter.8
  494.3 117.7 all-gather.15
  615.1 75.7 reduce-scatter.10
  693.5 82.2 all-gather.17
  777.4 159.2 all-gather.19
